TPU v7x, 32 devices: a whole 2x2x4 slice. The times are simulated.
32 devices in a mesh: ens: 2 (over y), rows: 8 (over z, x), fa: 2 (over core).
Axes of the slice: x: 2, y: 2, z: 4, core: 2. Of those that a mesh axis runs over, the one named last changes fastest.
Arguments:
- init_fields: float32 [2, 16, 128, 1792], P('fa', 'ens', 'rows'), parts along dimension 1, may hold values from -6 to 6
- streamwise: float32 [128, 1792], P('rows'), may hold values from 0 to 0.25
- crossflow: float32 [128, 1792], P('rows'), may hold values from -0.15 to 0.15
- diffusivity: float32 [128, 1792], P('rows'), may hold values from 0.1 to 0.24
- obstacle: int32 [128, 1792], P('rows'), may hold values from 0 to 1, as said below
- cell_weight: float32 [128, 1792], P('rows'), may hold values from 1 to 30, as said below
Outputs:
- final_fields: float32 [2, 16, 128, 1792], P('fa', 'ens', 'rows'), parts along dimension 1
- hankel: float32 [64, 32], P('ens'), parts along dimension 0
There are 2 independent parts, one for each index of `ens`. A program takes and returns all parts, laid end to end along the dimension named above; an argument that names none is the same for every part. Nothing has to cross between parts.
Inputs may be any that keep to these rules, and one draw needn't show every extreme that they name: `obstacle`: 1 on the cells of one disk, 0 elsewhere. `cell_weight`: positive areas.
All inputs are finite; a program needn't handle non-finite values.
Results may differ from a plain program's by a relative error of at most 0.0018.
Values may be sent and summed in bfloat16 or wider, within the bound.
No kernel may reach another device: no remote copies, remote signals or barrier semaphores. Data moves between devices by JAX's collectives and lax.ppermute only.
A program may use at most 64 MiB of HBM per device.

v0:
```python
import math

import jax
import jax.numpy as jnp
from jax import lax
from jax.sharding import PartitionSpec as P

NSNAP = 4
STRIDE = 3


def padded_2(shard, sides, width):
    for axis, dim in sides:
        size, length = (lax.axis_size(axis), shard.shape[dim])
        up = [(i, (i + 1) % size) for i in range(size - 1)]
        down = [(j, i) for i, j in up]
        last = lax.slice_in_dim(shard, length - width, length, axis=dim)
        first = lax.slice_in_dim(shard, 0, width, axis=dim)
        before = lax.ppermute(last, axis, up)
        after = lax.ppermute(first, axis, down)
        shard = jnp.concatenate([before, shard, after], axis=dim)
    return shard


def swapped(shard, axis, stride):
    return lax.ppermute(shard, axis, [(i, i ^ 1 << stride) for i in range(lax.axis_size(axis))])


def local(init_fields, streamwise, crossflow, diffusivity, obstacle, cell_weight):
    is_adjoint = lax.axis_index("fa") == 1
    field_now = init_fields[0]
    inputs_count, rows_local, cols_local = field_now.shape
    margin = STRIDE + 1
    solid_cells = obstacle.astype(jnp.float32)
    stacked = jnp.stack(
        [streamwise, crossflow, diffusivity, solid_cells, jnp.ones_like(solid_cells)]
    )
    extended = padded_2(stacked, (("rows", 1),), margin)
    padded = jnp.pad(extended, ((0, 0), (0, 0), (1, 1)))
    row_span = rows_local + 2 * STRIDE

    def beside_all(row_shift, col_shift):
        return padded[
            :, 1 + row_shift : 1 + row_shift + row_span, 1 + col_shift : 1 + col_shift + cols_local
        ]

    middle = beside_all(0, 0)
    eastern = beside_all(0, 1)
    western = beside_all(0, -1)
    northern = beside_all(1, 0)
    southern = beside_all(-1, 0)
    speed_x = middle[0]
    speed_y = middle[1]
    viscous = middle[2]
    blocked = middle[3]
    inside = middle[4]
    forward = (
        -speed_x / 2 + viscous,
        speed_x / 2 + viscous,
        -speed_y / 2 + viscous,
        speed_y / 2 + viscous,
    )
    adjoint = (
        eastern[0] / 2 + eastern[2],
        -western[0] / 2 + western[2],
        northern[1] / 2 + northern[2],
        -southern[1] / 2 + southern[2],
    )
    east_weight, west_weight, north_weight, south_weight = tuple(
        (jnp.where(is_adjoint, adj_term, fwd_term) for fwd_term, adj_term in zip(forward, adjoint))
    )
    centre_weight = -4.0 * viscous
    open_cells = 1.0 - blocked
    before = jnp.where(is_adjoint, open_cells, 1.0)
    after_mask = jnp.where(is_adjoint, 1.0, open_cells) * inside
    scaling = jnp.where(is_adjoint, cell_weight, 1.0)

    def advance(region, first_row):
        length = region.shape[1]
        start_input = first_row + STRIDE
        masked = before[start_input : start_input + length] * region
        widened = jnp.pad(masked, ((0, 0), (0, 0), (1, 1)))
        out_rows = length - 2
        start_output = start_input + 1

        def rows_of(weight):
            return weight[start_output : start_output + out_rows]

        centre = masked[:, 1:-1]
        summed = (
            centre
            + rows_of(east_weight) * widened[:, 1:-1, 2:]
            + rows_of(west_weight) * widened[:, 1:-1, :-2]
        )
        summed = (
            summed
            + rows_of(north_weight) * widened[:, 2:, 1:-1]
            + rows_of(south_weight) * widened[:, :-2, 1:-1]
        )
        summed = summed + rows_of(centre_weight) * centre
        return rows_of(after_mask) * summed

    def block_single(counter, current):
        grown_field = padded_2(current, (("rows", 1),), 1)
        return advance(grown_field, -1)

    half_cols = cols_local // 2
    keep_start = lax.axis_index("fa") * half_cols
    send_start = (1 - lax.axis_index("fa")) * half_cols
    kept_parts = []
    received = []
    for snap_index in range(NSNAP):
        field_now = lax.fori_loop(0, STRIDE, block_single, field_now)
        snapshot = (scaling * field_now).astype(jnp.bfloat16)
        own_part = lax.dynamic_slice_in_dim(snapshot, keep_start, half_cols, 2)
        sent_part = lax.dynamic_slice_in_dim(snapshot, send_start, half_cols, 2)
        kept_parts.append(own_part)
        received.append(sent_part)
    snapshot_count = NSNAP * inputs_count
    own_all = jnp.stack(kept_parts).reshape(snapshot_count, -1)
    other_all = jnp.stack(received)
    other_all = swapped(other_all, "fa", 0)
    other_all = other_all.reshape(snapshot_count, -1)
    product = lax.dot_general(
        own_all, other_all, (((1,), (1,)), ((), ())), preferred_element_type=jnp.float32
    )
    local_part = jnp.where(is_adjoint, product, product.T)
    summed_all = lax.psum(local_part, ("rows", "fa"))
    hankel = summed_all * (1.0 / math.sqrt(rows_local * lax.axis_size("rows") * cols_local))
    return (field_now[None], hankel)


def solution(mesh):
    placed = (
        P("fa", "ens", "rows", None),
        P("rows", None),
        P("rows", None),
        P("rows", None),
        P("rows", None),
        P("rows", None),
    )
    return jax.shard_map(
        local,
        mesh=mesh,
        in_specs=placed,
        out_specs=(P("fa", "ens", "rows", None), P("ens", None)),
        check_vma=False,
    )
```

profile of v0, /device:TPU:0, one launch (start us, length us, event | category | flops | bytes accessed | tf_op | source)
XLA Modules:
  0.0 247.3 jit_solution(1238004839971723349)
XLA Ops:
  0.7 0.8 copy-done.21
  1.8 4.9 %collective-permute-start.8 = (f32[5,4,1792]{2,1,0:T(4,128)S(1)}, f32[5,4,1792]{2,1,0:T(4,128)S(1)}, u32[]{:S(2)}, u32[]{:S(2)}) collective-permute-start(f32[5,4,1792]{2,1,0:T(4,128)S(1)} %get-tuple-element.545), channel_id=1, source_target_pairs={{0,2},{2,4},{4,6},{6,8},{8,10},{10,12},{12,14},{1,3},{3,5},{5,7},{... | collective-permute-start | bytes 430088 | tf_op jit(solution)/shard_map/ppermute | solution.py:19
  6.7 1.3 collective-permute-start.9
  8.6 1.0 collective-permute-done.8
  9.7 4.1 %collective-permute-done.9 = f32[5,4,1792]{2,1,0:T(4,128)S(1)} collective-permute-done((f32[5,4,1792]{2,1,0:T(4,128)S(1)}, f32[5,4,1792]{2,1,0:T(4,128)S(1)}, u32[]{:S(2)}, u32[]{:S(2)}) %collective-permute-start.9) | collective-permute-done | bytes 143392 | tf_op jit(solution)/shard_map/ppermute | solution.py:20
  14.2 0.9 copy-done
  15.1 29.1 %while.48 = (s32[]{:T(128)}, f32[8,16,1792]{2,1,0:T(8,128)S(1)}, f32[22,1792]{1,0:T(8,128)S(1)}, f32[22,1792]{1,0:T(8,128)S(1)}, f32[22,1792]{1,0:T(8,128)S(1)},...) while((s32[]{:T(128)}, f32[8,16,1792]{2,1,0:T(8,128)S(1)}, ...), condition=%wide.region_1.2_spmd, body=%wide.region_0.1_spmd.sunk | while | flops 3297282 | bytes 10250421 | solution.py:113
  15.2 1.3 collective-permute-start
  16.5 5.0 %collective-permute-start.1 = (f32[8,1,1792]{2,1,0:T(1,128)S(1)}, f32[8,1,1792]{2,1,0:T(1,128)S(1)}, u32[]{:S(2)}, u32[]{:S(2)}) collective-permute-start(f32[8,1,1792]{2,1,0:T(1,128)S(1)} %get-tuple-element.765), channel_id=1, source_target_pairs={{0,2},{2,4},{4,6},{6,8},{8,10},{10,12},{12,14},{1,3},{3,5},{5,7},{... | collective-permute-start | bytes 172040 | tf_op jit(solution)/shard_map/while/body/eval_jaxpr/ppermute | solution.py:19
  21.7 1.6 collective-permute-done.1
  23.5 0.8 fusion.64
  24.5 1.3 collective-permute-start
  25.8 5.4 %collective-permute-start.1 = (f32[8,1,1792]{2,1,0:T(1,128)S(1)}, f32[8,1,1792]{2,1,0:T(1,128)S(1)}, u32[]{:S(2)}, u32[]{:S(2)}) collective-permute-start(f32[8,1,1792]{2,1,0:T(1,128)S(1)} %get-tuple-element.765), channel_id=1, source_target_pairs={{0,2},{2,4},{4,6},{6,8},{8,10},{10,12},{12,14},{1,3},{3,5},{5,7},{... | collective-permute-start | bytes 172040 | tf_op jit(solution)/shard_map/while/body/eval_jaxpr/ppermute | solution.py:19
  31.4 1.6 collective-permute-done.1
  33.3 0.8 fusion.64
  34.2 1.3 collective-permute-start
  35.5 5.8 %collective-permute-start.1 = (f32[8,1,1792]{2,1,0:T(1,128)S(1)}, f32[8,1,1792]{2,1,0:T(1,128)S(1)}, u32[]{:S(2)}, u32[]{:S(2)}) collective-permute-start(f32[8,1,1792]{2,1,0:T(1,128)S(1)} %get-tuple-element.765), channel_id=1, source_target_pairs={{0,2},{2,4},{4,6},{6,8},{8,10},{10,12},{12,14},{1,3},{3,5},{5,7},{... | collective-permute-start | bytes 172040 | tf_op jit(solution)/shard_map/while/body/eval_jaxpr/ppermute | solution.py:19
  41.5 1.6 collective-permute-done.1
  44.3 36.5 %while.49 = (s32[]{:T(128)}, f32[8,16,1792]{2,1,0:T(8,128)S(1)}, f32[22,1792]{1,0:T(8,128)S(1)}, f32[22,1792]{1,0:T(8,128)S(1)}, f32[22,1792]{1,0:T(8,128)S(1)},...) while((s32[]{:T(128)}, f32[8,16,1792]{2,1,0:T(8,128)S(1)}, ...), condition=%wide.region_3.4_spmd, body=%wide.region_2.3_spmd.sunk | while | flops 3297282 | bytes 11626761 | solution.py:113
  45.0 1.3 collective-permute-start.2
  46.3 6.4 %collective-permute-start.3 = (f32[8,1,1792]{2,1,0:T(1,128)}, f32[8,1,1792]{2,1,0:T(1,128)}, u32[]{:S(2)}, u32[]{:S(2)}) collective-permute-start(f32[8,1,1792]{2,1,0:T(1,128)} %get-tuple-element.776), channel_id=1, source_target_pairs={{0,2},{2,4},{4,6},{6,8},{8,10},{10,12},{12,14},{1,3},{3,5},{5,7},{... | collective-permute-start | bytes 172040 | tf_op jit(solution)/shard_map/while/body/eval_jaxpr/ppermute | solution.py:19
  54.8 1.1 maximum_multiply_fusion.9
  57.6 1.3 collective-permute-start.2
  58.9 5.9 %collective-permute-start.3 = (f32[8,1,1792]{2,1,0:T(1,128)}, f32[8,1,1792]{2,1,0:T(1,128)}, u32[]{:S(2)}, u32[]{:S(2)}) collective-permute-start(f32[8,1,1792]{2,1,0:T(1,128)} %get-tuple-element.776), channel_id=1, source_target_pairs={{0,2},{2,4},{4,6},{6,8},{8,10},{10,12},{12,14},{1,3},{3,5},{5,7},{... | collective-permute-start | bytes 172040 | tf_op jit(solution)/shard_map/while/body/eval_jaxpr/ppermute | solution.py:19
  66.8 1.1 maximum_multiply_fusion.9
  69.6 1.3 collective-permute-start.2
  70.9 5.8 %collective-permute-start.3 = (f32[8,1,1792]{2,1,0:T(1,128)}, f32[8,1,1792]{2,1,0:T(1,128)}, u32[]{:S(2)}, u32[]{:S(2)}) collective-permute-start(f32[8,1,1792]{2,1,0:T(1,128)} %get-tuple-element.776), channel_id=1, source_target_pairs={{0,2},{2,4},{4,6},{6,8},{8,10},{10,12},{12,14},{1,3},{3,5},{5,7},{... | collective-permute-start | bytes 172040 | tf_op jit(solution)/shard_map/while/body/eval_jaxpr/ppermute | solution.py:19
  78.7 1.1 maximum_multiply_fusion.9
  82.8 44.5 %while.50 = (s32[]{:T(128)}, f32[8,16,1792]{2,1,0:T(8,128)S(1)}, f32[22,1792]{1,0:T(8,128)}, f32[22,1792]{1,0:T(8,128)S(1)}, f32[22,1792]{1,0:T(8,128)}, /*index...) while((s32[]{:T(128)}, f32[8,16,1792]{2,1,0:T(8,128)S(1)}, ...), condition=%wide.region_5.6_spmd, body=%wide.region_4.5_spmd.sunk | while | flops 3297282 | bytes 13805945 | solution.py:113
  83.6 1.3 collective-permute-start.4
  84.9 5.8 %collective-permute-start.5 = (f32[8,1,1792]{2,1,0:T(1,128)}, f32[8,1,1792]{2,1,0:T(1,128)}, u32[]{:S(2)}, u32[]{:S(2)}) collective-permute-start(f32[8,1,1792]{2,1,0:T(1,128)} %get-tuple-element.787), channel_id=1, source_target_pairs={{0,2},{2,4},{4,6},{6,8},{8,10},{10,12},{12,14},{1,3},{3,5},{5,7},{... | collective-permute-start | bytes 172040 | tf_op jit(solution)/shard_map/while/body/eval_jaxpr/ppermute | solution.py:19
  92.7 1.6 slice.722
  95.6 1.3 maximum_multiply_fusion.10
  98.6 1.3 collective-permute-start.4
  99.9 5.7 %collective-permute-start.5 = (f32[8,1,1792]{2,1,0:T(1,128)}, f32[8,1,1792]{2,1,0:T(1,128)}, u32[]{:S(2)}, u32[]{:S(2)}) collective-permute-start(f32[8,1,1792]{2,1,0:T(1,128)} %get-tuple-element.787), channel_id=1, source_target_pairs={{0,2},{2,4},{4,6},{6,8},{8,10},{10,12},{12,14},{1,3},{3,5},{5,7},{... | collective-permute-start | bytes 172040 | tf_op jit(solution)/shard_map/while/body/eval_jaxpr/ppermute | solution.py:19
  107.6 1.6 slice.722
  110.5 1.3 maximum_multiply_fusion.10
  113.5 1.3 collective-permute-start.4
  114.8 5.5 %collective-permute-start.5 = (f32[8,1,1792]{2,1,0:T(1,128)}, f32[8,1,1792]{2,1,0:T(1,128)}, u32[]{:S(2)}, u32[]{:S(2)}) collective-permute-start(f32[8,1,1792]{2,1,0:T(1,128)} %get-tuple-element.787), channel_id=1, source_target_pairs={{0,2},{2,4},{4,6},{6,8},{8,10},{10,12},{12,14},{1,3},{3,5},{5,7},{... | collective-permute-start | bytes 172040 | tf_op jit(solution)/shard_map/while/body/eval_jaxpr/ppermute | solution.py:19
  122.2 1.6 slice.722
  125.2 1.3 maximum_multiply_fusion.10
  127.4 0.9 copy.34
  128.3 51.0 %while.51 = (s32[]{:T(128)}, f32[8,16,1792]{2,1,0:T(8,128)}, f32[22,1792]{1,0:T(8,128)}, f32[22,1792]{1,0:T(8,128)S(1)}, f32[22,1792]{1,0:T(8,128)}, /*index=5*/...) while((s32[]{:T(128)}, f32[8,16,1792]{2,1,0:T(8,128)}, ...), condition=%wide.region_7.8_spmd, body=%wide.region_6.7_spmd.sunk | while | flops 3297282 | bytes 13805945 | solution.py:113
  128.3 1.9 fusion.69
  130.2 1.3 collective-permute-start.6
  131.5 5.5 %collective-permute-start.7 = (f32[8,1,1792]{2,1,0:T(1,128)}, f32[8,1,1792]{2,1,0:T(1,128)}, u32[]{:S(2)}, u32[]{:S(2)}) collective-permute-start(f32[8,1,1792]{2,1,0:T(1,128)} %get-tuple-element.798), channel_id=1, source_target_pairs={{0,2},{2,4},{4,6},{6,8},{8,10},{10,12},{12,14},{1,3},{3,5},{5,7},{... | collective-permute-start | bytes 172040 | tf_op jit(solution)/shard_map/while/body/eval_jaxpr/ppermute | solution.py:19
  139.0 1.6 slice.736
  142.0 1.5 maximum_multiply_fusion.11
  143.6 1.8 fusion.70
  145.3 1.9 fusion.69
  147.2 1.3 collective-permute-start.6
  148.5 5.5 %collective-permute-start.7 = (f32[8,1,1792]{2,1,0:T(1,128)}, f32[8,1,1792]{2,1,0:T(1,128)}, u32[]{:S(2)}, u32[]{:S(2)}) collective-permute-start(f32[8,1,1792]{2,1,0:T(1,128)} %get-tuple-element.798), channel_id=1, source_target_pairs={{0,2},{2,4},{4,6},{6,8},{8,10},{10,12},{12,14},{1,3},{3,5},{5,7},{... | collective-permute-start | bytes 172040 | tf_op jit(solution)/shard_map/while/body/eval_jaxpr/ppermute | solution.py:19
  156.0 1.6 slice.736
  159.0 1.5 maximum_multiply_fusion.11
  160.6 1.8 fusion.70
  162.3 1.9 fusion.69
  164.2 1.3 collective-permute-start.6
  165.5 5.5 %collective-permute-start.7 = (f32[8,1,1792]{2,1,0:T(1,128)}, f32[8,1,1792]{2,1,0:T(1,128)}, u32[]{:S(2)}, u32[]{:S(2)}) collective-permute-start(f32[8,1,1792]{2,1,0:T(1,128)} %get-tuple-element.798), channel_id=1, source_target_pairs={{0,2},{2,4},{4,6},{6,8},{8,10},{10,12},{12,14},{1,3},{3,5},{5,7},{... | collective-permute-start | bytes 172040 | tf_op jit(solution)/shard_map/while/body/eval_jaxpr/ppermute | solution.py:19
  173.0 1.6 slice.736
  176.0 1.5 maximum_multiply_fusion.11
  177.6 1.8 fusion.70
  179.3 1.6 multiply_convert_fusion.3
  181.7 2.1 collective-permute-done.10
  184.4 62.2 %psum.7 = f32[32,32]{1,0:T(8,128)S(1)} all-reduce(f32[32,32]{1,0:T(8,128)S(1)} %bitcast_select_fusion), channel_id=1, replica_groups=mesh['ens'=2,'rows'=8,'fa'=2] {'rows','fa'}, use_global_device_ids=true, to_apply=%region_8.9 | all-reduce | flops 1024 | bytes 8192 | tf_op jit(solution)/shard_map/psum | solution.py:128
  (258 shorter events, 43.3 us)
Async XLA Ops:
  0.7 7.3 %copy-start.25 = (f32[16,1792]{1,0:T(8,128)S(1)}, f32[16,1792]{1,0:T(8,128)}, u32[]{:S(2)}) copy-start(f32[16,1792]{1,0:T(8,128)} %param.19) | copy-start | bytes 344068
  1.8 7.9 %collective-permute-start.8 = (f32[5,4,1792]{2,1,0:T(4,128)S(1)}, f32[5,4,1792]{2,1,0:T(4,128)S(1)}, u32[]{:S(2)}, u32[]{:S(2)}) collective-permute-start(f32[5,4,1792]{2,1,0:T(4,128)S(1)} %get-tuple-element.545), channel_id=1, source_target_pairs={{0,2},{2,4},{4,6},{6,8},{8,10},{10,12},{12,14},{1,3},{3,5},{5,7},{... | collective-permute-start | bytes 430088 | tf_op jit(solution)/shard_map/ppermute | solution.py:19
  6.7 7.1 %collective-permute-start.9 = (f32[5,4,1792]{2,1,0:T(4,128)S(1)}, f32[5,4,1792]{2,1,0:T(4,128)S(1)}, u32[]{:S(2)}, u32[]{:S(2)}) collective-permute-start(f32[5,4,1792]{2,1,0:T(4,128)S(1)} %get-tuple-element.546), channel_id=1, source_target_pairs={{2,0},{4,2},{6,4},{8,6},{10,8},{12,10},{14,12},{3,1},{5,3},{7,5},{... | collective-permute-start | bytes 430088 | tf_op jit(solution)/shard_map/ppermute | solution.py:20
  15.2 6.5 %collective-permute-start = (f32[8,1,1792]{2,1,0:T(1,128)S(1)}, f32[8,1,1792]{2,1,0:T(1,128)S(1)}, u32[]{:S(2)}, u32[]{:S(2)}) collective-permute-start(f32[8,1,1792]{2,1,0:T(1,128)S(1)} %get-tuple-element.764), channel_id=1, source_target_pairs={{2,0},{4,2},{6,4},{8,6},{10,8},{12,10},{14,12},{3,1},{5,3},{7,5},{... | collective-permute-start | bytes 172040 | tf_op jit(solution)/shard_map/while/body/eval_jaxpr/ppermute | solution.py:20
  16.5 6.8 %collective-permute-start.1 = (f32[8,1,1792]{2,1,0:T(1,128)S(1)}, f32[8,1,1792]{2,1,0:T(1,128)S(1)}, u32[]{:S(2)}, u32[]{:S(2)}) collective-permute-start(f32[8,1,1792]{2,1,0:T(1,128)S(1)} %get-tuple-element.765), channel_id=1, source_target_pairs={{0,2},{2,4},{4,6},{6,8},{8,10},{10,12},{12,14},{1,3},{3,5},{5,7},{... | collective-permute-start | bytes 172040 | tf_op jit(solution)/shard_map/while/body/eval_jaxpr/ppermute | solution.py:19
  24.5 7.0 %collective-permute-start = (f32[8,1,1792]{2,1,0:T(1,128)S(1)}, f32[8,1,1792]{2,1,0:T(1,128)S(1)}, u32[]{:S(2)}, u32[]{:S(2)}) collective-permute-start(f32[8,1,1792]{2,1,0:T(1,128)S(1)} %get-tuple-element.764), channel_id=1, source_target_pairs={{2,0},{4,2},{6,4},{8,6},{10,8},{12,10},{14,12},{3,1},{5,3},{7,5},{... | collective-permute-start | bytes 172040 | tf_op jit(solution)/shard_map/while/body/eval_jaxpr/ppermute | solution.py:20
  25.8 7.3 %collective-permute-start.1 = (f32[8,1,1792]{2,1,0:T(1,128)S(1)}, f32[8,1,1792]{2,1,0:T(1,128)S(1)}, u32[]{:S(2)}, u32[]{:S(2)}) collective-permute-start(f32[8,1,1792]{2,1,0:T(1,128)S(1)} %get-tuple-element.765), channel_id=1, source_target_pairs={{0,2},{2,4},{4,6},{6,8},{8,10},{10,12},{12,14},{1,3},{3,5},{5,7},{... | collective-permute-start | bytes 172040 | tf_op jit(solution)/shard_map/while/body/eval_jaxpr/ppermute | solution.py:19
  34.2 7.3 %collective-permute-start = (f32[8,1,1792]{2,1,0:T(1,128)S(1)}, f32[8,1,1792]{2,1,0:T(1,128)S(1)}, u32[]{:S(2)}, u32[]{:S(2)}) collective-permute-start(f32[8,1,1792]{2,1,0:T(1,128)S(1)} %get-tuple-element.764), channel_id=1, source_target_pairs={{2,0},{4,2},{6,4},{8,6},{10,8},{12,10},{14,12},{3,1},{5,3},{7,5},{... | collective-permute-start | bytes 172040 | tf_op jit(solution)/shard_map/while/body/eval_jaxpr/ppermute | solution.py:20
  35.5 7.6 %collective-permute-start.1 = (f32[8,1,1792]{2,1,0:T(1,128)S(1)}, f32[8,1,1792]{2,1,0:T(1,128)S(1)}, u32[]{:S(2)}, u32[]{:S(2)}) collective-permute-start(f32[8,1,1792]{2,1,0:T(1,128)S(1)} %get-tuple-element.765), channel_id=1, source_target_pairs={{0,2},{2,4},{4,6},{6,8},{8,10},{10,12},{12,14},{1,3},{3,5},{5,7},{... | collective-permute-start | bytes 172040 | tf_op jit(solution)/shard_map/while/body/eval_jaxpr/ppermute | solution.py:19
  45.0 9.8 %collective-permute-start.2 = (f32[8,1,1792]{2,1,0:T(1,128)}, f32[8,1,1792]{2,1,0:T(1,128)}, u32[]{:S(2)}, u32[]{:S(2)}) collective-permute-start(f32[8,1,1792]{2,1,0:T(1,128)} %get-tuple-element.775), channel_id=1, source_target_pairs={{2,0},{4,2},{6,4},{8,6},{10,8},{12,10},{14,12},{3,1},{5,3},{7,5},{... | collective-permute-start | bytes 172040 | tf_op jit(solution)/shard_map/while/body/eval_jaxpr/ppermute | solution.py:20
  46.3 8.5 %collective-permute-start.3 = (f32[8,1,1792]{2,1,0:T(1,128)}, f32[8,1,1792]{2,1,0:T(1,128)}, u32[]{:S(2)}, u32[]{:S(2)}) collective-permute-start(f32[8,1,1792]{2,1,0:T(1,128)} %get-tuple-element.776), channel_id=1, source_target_pairs={{0,2},{2,4},{4,6},{6,8},{8,10},{10,12},{12,14},{1,3},{3,5},{5,7},{... | collective-permute-start | bytes 172040 | tf_op jit(solution)/shard_map/while/body/eval_jaxpr/ppermute | solution.py:19
  57.6 9.2 %collective-permute-start.2 = (f32[8,1,1792]{2,1,0:T(1,128)}, f32[8,1,1792]{2,1,0:T(1,128)}, u32[]{:S(2)}, u32[]{:S(2)}) collective-permute-start(f32[8,1,1792]{2,1,0:T(1,128)} %get-tuple-element.775), channel_id=1, source_target_pairs={{2,0},{4,2},{6,4},{8,6},{10,8},{12,10},{14,12},{3,1},{5,3},{7,5},{... | collective-permute-start | bytes 172040 | tf_op jit(solution)/shard_map/while/body/eval_jaxpr/ppermute | solution.py:20
  58.9 7.9 %collective-permute-start.3 = (f32[8,1,1792]{2,1,0:T(1,128)}, f32[8,1,1792]{2,1,0:T(1,128)}, u32[]{:S(2)}, u32[]{:S(2)}) collective-permute-start(f32[8,1,1792]{2,1,0:T(1,128)} %get-tuple-element.776), channel_id=1, source_target_pairs={{0,2},{2,4},{4,6},{6,8},{8,10},{10,12},{12,14},{1,3},{3,5},{5,7},{... | collective-permute-start | bytes 172040 | tf_op jit(solution)/shard_map/while/body/eval_jaxpr/ppermute | solution.py:19
  69.6 9.1 %collective-permute-start.2 = (f32[8,1,1792]{2,1,0:T(1,128)}, f32[8,1,1792]{2,1,0:T(1,128)}, u32[]{:S(2)}, u32[]{:S(2)}) collective-permute-start(f32[8,1,1792]{2,1,0:T(1,128)} %get-tuple-element.775), channel_id=1, source_target_pairs={{2,0},{4,2},{6,4},{8,6},{10,8},{12,10},{14,12},{3,1},{5,3},{7,5},{... | collective-permute-start | bytes 172040 | tf_op jit(solution)/shard_map/while/body/eval_jaxpr/ppermute | solution.py:20
  70.9 7.9 %collective-permute-start.3 = (f32[8,1,1792]{2,1,0:T(1,128)}, f32[8,1,1792]{2,1,0:T(1,128)}, u32[]{:S(2)}, u32[]{:S(2)}) collective-permute-start(f32[8,1,1792]{2,1,0:T(1,128)} %get-tuple-element.776), channel_id=1, source_target_pairs={{0,2},{2,4},{4,6},{6,8},{8,10},{10,12},{12,14},{1,3},{3,5},{5,7},{... | collective-permute-start | bytes 172040 | tf_op jit(solution)/shard_map/while/body/eval_jaxpr/ppermute | solution.py:19
  82.9 11.4 %copy-start.3 = (f32[22,1792]{1,0:T(8,128)S(1)}, f32[22,1792]{1,0:T(8,128)}, u32[]{:S(2)}) copy-start(f32[22,1792]{1,0:T(8,128)} %get-tuple-element.883) | copy-start | bytes 473092 | tf_op jit(solution)/shard_map/while
  82.9 12.1 %copy-start.6 = (f32[22,1792]{1,0:T(8,128)S(1)}, f32[22,1792]{1,0:T(8,128)}, u32[]{:S(2)}) copy-start(f32[22,1792]{1,0:T(8,128)} %get-tuple-element.881) | copy-start | bytes 473092 | tf_op jit(solution)/shard_map/while
  83.6 12.0 %collective-permute-start.4 = (f32[8,1,1792]{2,1,0:T(1,128)}, f32[8,1,1792]{2,1,0:T(1,128)}, u32[]{:S(2)}, u32[]{:S(2)}) collective-permute-start(f32[8,1,1792]{2,1,0:T(1,128)} %get-tuple-element.786), channel_id=1, source_target_pairs={{2,0},{4,2},{6,4},{8,6},{10,8},{12,10},{14,12},{3,1},{5,3},{7,5},{... | collective-permute-start | bytes 172040 | tf_op jit(solution)/shard_map/while/body/eval_jaxpr/ppermute | solution.py:20
  84.9 10.7 %collective-permute-start.5 = (f32[8,1,1792]{2,1,0:T(1,128)}, f32[8,1,1792]{2,1,0:T(1,128)}, u32[]{:S(2)}, u32[]{:S(2)}) collective-permute-start(f32[8,1,1792]{2,1,0:T(1,128)} %get-tuple-element.787), channel_id=1, source_target_pairs={{0,2},{2,4},{4,6},{6,8},{8,10},{10,12},{12,14},{1,3},{3,5},{5,7},{... | collective-permute-start | bytes 172040 | tf_op jit(solution)/shard_map/while/body/eval_jaxpr/ppermute | solution.py:19
  95.6 1.4 copy-start.13
  95.6 1.4 copy-start.14
  95.6 1.4 copy-start.15
  97.8 11.4 %copy-start.3 = (f32[22,1792]{1,0:T(8,128)S(1)}, f32[22,1792]{1,0:T(8,128)}, u32[]{:S(2)}) copy-start(f32[22,1792]{1,0:T(8,128)} %get-tuple-element.883) | copy-start | bytes 473092 | tf_op jit(solution)/shard_map/while
  97.8 12.0 %copy-start.6 = (f32[22,1792]{1,0:T(8,128)S(1)}, f32[22,1792]{1,0:T(8,128)}, u32[]{:S(2)}) copy-start(f32[22,1792]{1,0:T(8,128)} %get-tuple-element.881) | copy-start | bytes 473092 | tf_op jit(solution)/shard_map/while
  98.6 11.9 %collective-permute-start.4 = (f32[8,1,1792]{2,1,0:T(1,128)}, f32[8,1,1792]{2,1,0:T(1,128)}, u32[]{:S(2)}, u32[]{:S(2)}) collective-permute-start(f32[8,1,1792]{2,1,0:T(1,128)} %get-tuple-element.786), channel_id=1, source_target_pairs={{2,0},{4,2},{6,4},{8,6},{10,8},{12,10},{14,12},{3,1},{5,3},{7,5},{... | collective-permute-start | bytes 172040 | tf_op jit(solution)/shard_map/while/body/eval_jaxpr/ppermute | solution.py:20
  99.9 10.7 %collective-permute-start.5 = (f32[8,1,1792]{2,1,0:T(1,128)}, f32[8,1,1792]{2,1,0:T(1,128)}, u32[]{:S(2)}, u32[]{:S(2)}) collective-permute-start(f32[8,1,1792]{2,1,0:T(1,128)} %get-tuple-element.787), channel_id=1, source_target_pairs={{0,2},{2,4},{4,6},{6,8},{8,10},{10,12},{12,14},{1,3},{3,5},{5,7},{... | collective-permute-start | bytes 172040 | tf_op jit(solution)/shard_map/while/body/eval_jaxpr/ppermute | solution.py:19
  110.5 1.4 copy-start.13
  110.5 1.4 copy-start.14
  110.5 1.4 copy-start.15
  112.7 11.1 %copy-start.3 = (f32[22,1792]{1,0:T(8,128)S(1)}, f32[22,1792]{1,0:T(8,128)}, u32[]{:S(2)}) copy-start(f32[22,1792]{1,0:T(8,128)} %get-tuple-element.883) | copy-start | bytes 473092 | tf_op jit(solution)/shard_map/while
  112.7 11.7 %copy-start.6 = (f32[22,1792]{1,0:T(8,128)S(1)}, f32[22,1792]{1,0:T(8,128)}, u32[]{:S(2)}) copy-start(f32[22,1792]{1,0:T(8,128)} %get-tuple-element.881) | copy-start | bytes 473092 | tf_op jit(solution)/shard_map/while
  113.5 11.7 %collective-permute-start.4 = (f32[8,1,1792]{2,1,0:T(1,128)}, f32[8,1,1792]{2,1,0:T(1,128)}, u32[]{:S(2)}, u32[]{:S(2)}) collective-permute-start(f32[8,1,1792]{2,1,0:T(1,128)} %get-tuple-element.786), channel_id=1, source_target_pairs={{2,0},{4,2},{6,4},{8,6},{10,8},{12,10},{14,12},{3,1},{5,3},{7,5},{... | collective-permute-start | bytes 172040 | tf_op jit(solution)/shard_map/while/body/eval_jaxpr/ppermute | solution.py:20
  114.8 10.4 %collective-permute-start.5 = (f32[8,1,1792]{2,1,0:T(1,128)}, f32[8,1,1792]{2,1,0:T(1,128)}, u32[]{:S(2)}, u32[]{:S(2)}) collective-permute-start(f32[8,1,1792]{2,1,0:T(1,128)} %get-tuple-element.787), channel_id=1, source_target_pairs={{0,2},{2,4},{4,6},{6,8},{8,10},{10,12},{12,14},{1,3},{3,5},{5,7},{... | collective-permute-start | bytes 172040 | tf_op jit(solution)/shard_map/while/body/eval_jaxpr/ppermute | solution.py:19
  125.2 1.4 copy-start.13
  125.2 1.4 copy-start.14
  125.2 1.4 copy-start.15
  128.3 12.3 %copy-start.4 = (f32[22,1792]{1,0:T(8,128)S(1)}, f32[22,1792]{1,0:T(8,128)}, u32[]{:S(2)}) copy-start(f32[22,1792]{1,0:T(8,128)} %get-tuple-element.913) | copy-start | bytes 473092 | tf_op jit(solution)/shard_map/while
  128.3 13.0 %copy-start.7 = (f32[22,1792]{1,0:T(8,128)S(1)}, f32[22,1792]{1,0:T(8,128)}, u32[]{:S(2)}) copy-start(f32[22,1792]{1,0:T(8,128)} %get-tuple-element.911) | copy-start | bytes 473092 | tf_op jit(solution)/shard_map/while
  130.2 11.7 %collective-permute-start.6 = (f32[8,1,1792]{2,1,0:T(1,128)}, f32[8,1,1792]{2,1,0:T(1,128)}, u32[]{:S(2)}, u32[]{:S(2)}) collective-permute-start(f32[8,1,1792]{2,1,0:T(1,128)} %get-tuple-element.797), channel_id=1, source_target_pairs={{2,0},{4,2},{6,4},{8,6},{10,8},{12,10},{14,12},{3,1},{5,3},{7,5},{... | collective-permute-start | bytes 172040 | tf_op jit(solution)/shard_map/while/body/eval_jaxpr/ppermute | solution.py:20
  131.5 10.4 %collective-permute-start.7 = (f32[8,1,1792]{2,1,0:T(1,128)}, f32[8,1,1792]{2,1,0:T(1,128)}, u32[]{:S(2)}, u32[]{:S(2)}) collective-permute-start(f32[8,1,1792]{2,1,0:T(1,128)} %get-tuple-element.798), channel_id=1, source_target_pairs={{0,2},{2,4},{4,6},{6,8},{8,10},{10,12},{12,14},{1,3},{3,5},{5,7},{... | collective-permute-start | bytes 172040 | tf_op jit(solution)/shard_map/while/body/eval_jaxpr/ppermute | solution.py:19
  141.9 1.6 copy-start.16
  141.9 1.6 copy-start.17
  141.9 1.6 copy-start.18
  141.9 1.6 copy-start.19
  141.9 1.6 copy-start.20
  145.3 12.3 %copy-start.4 = (f32[22,1792]{1,0:T(8,128)S(1)}, f32[22,1792]{1,0:T(8,128)}, u32[]{:S(2)}) copy-start(f32[22,1792]{1,0:T(8,128)} %get-tuple-element.913) | copy-start | bytes 473092 | tf_op jit(solution)/shard_map/while
  145.3 12.9 %copy-start.7 = (f32[22,1792]{1,0:T(8,128)S(1)}, f32[22,1792]{1,0:T(8,128)}, u32[]{:S(2)}) copy-start(f32[22,1792]{1,0:T(8,128)} %get-tuple-element.911) | copy-start | bytes 473092 | tf_op jit(solution)/shard_map/while
  147.2 11.7 %collective-permute-start.6 = (f32[8,1,1792]{2,1,0:T(1,128)}, f32[8,1,1792]{2,1,0:T(1,128)}, u32[]{:S(2)}, u32[]{:S(2)}) collective-permute-start(f32[8,1,1792]{2,1,0:T(1,128)} %get-tuple-element.797), channel_id=1, source_target_pairs={{2,0},{4,2},{6,4},{8,6},{10,8},{12,10},{14,12},{3,1},{5,3},{7,5},{... | collective-permute-start | bytes 172040 | tf_op jit(solution)/shard_map/while/body/eval_jaxpr/ppermute | solution.py:20
  148.5 10.4 %collective-permute-start.7 = (f32[8,1,1792]{2,1,0:T(1,128)}, f32[8,1,1792]{2,1,0:T(1,128)}, u32[]{:S(2)}, u32[]{:S(2)}) collective-permute-start(f32[8,1,1792]{2,1,0:T(1,128)} %get-tuple-element.798), channel_id=1, source_target_pairs={{0,2},{2,4},{4,6},{6,8},{8,10},{10,12},{12,14},{1,3},{3,5},{5,7},{... | collective-permute-start | bytes 172040 | tf_op jit(solution)/shard_map/while/body/eval_jaxpr/ppermute | solution.py:19
  158.9 1.6 copy-start.16
  158.9 1.6 copy-start.17
  158.9 1.6 copy-start.18
  158.9 1.6 copy-start.19
  158.9 1.6 copy-start.20
  162.3 12.3 %copy-start.4 = (f32[22,1792]{1,0:T(8,128)S(1)}, f32[22,1792]{1,0:T(8,128)}, u32[]{:S(2)}) copy-start(f32[22,1792]{1,0:T(8,128)} %get-tuple-element.913) | copy-start | bytes 473092 | tf_op jit(solution)/shard_map/while
  162.3 12.9 %copy-start.7 = (f32[22,1792]{1,0:T(8,128)S(1)}, f32[22,1792]{1,0:T(8,128)}, u32[]{:S(2)}) copy-start(f32[22,1792]{1,0:T(8,128)} %get-tuple-element.911) | copy-start | bytes 473092 | tf_op jit(solution)/shard_map/while
  164.2 11.7 %collective-permute-start.6 = (f32[8,1,1792]{2,1,0:T(1,128)}, f32[8,1,1792]{2,1,0:T(1,128)}, u32[]{:S(2)}, u32[]{:S(2)}) collective-permute-start(f32[8,1,1792]{2,1,0:T(1,128)} %get-tuple-element.797), channel_id=1, source_target_pairs={{2,0},{4,2},{6,4},{8,6},{10,8},{12,10},{14,12},{3,1},{5,3},{7,5},{... | collective-permute-start | bytes 172040 | tf_op jit(solution)/shard_map/while/body/eval_jaxpr/ppermute | solution.py:20
  165.5 10.4 %collective-permute-start.7 = (f32[8,1,1792]{2,1,0:T(1,128)}, f32[8,1,1792]{2,1,0:T(1,128)}, u32[]{:S(2)}, u32[]{:S(2)}) collective-permute-start(f32[8,1,1792]{2,1,0:T(1,128)} %get-tuple-element.798), channel_id=1, source_target_pairs={{0,2},{2,4},{4,6},{6,8},{8,10},{10,12},{12,14},{1,3},{3,5},{5,7},{... | collective-permute-start | bytes 172040 | tf_op jit(solution)/shard_map/while/body/eval_jaxpr/ppermute | solution.py:19
  175.9 1.6 copy-start.16
  175.9 1.6 copy-start.17
  175.9 1.6 copy-start.18
  175.9 1.6 copy-start.19
  175.9 1.6 copy-start.20
  181.3 2.5 %collective-permute-start.10 = (bf16[4,8,16,896]{3,2,1,0:T(8,128)(2,1)S(1)}, bf16[4,8,16,896]{3,2,1,0:T(8,128)(2,1)S(1)}, u32[]{:S(2)}, u32[]{:S(2)}) collective-permute-start(bf16[4,8,16,896]{3,2,1,0:T(8,128)(2,1)S(1)} %pad_maximum_fusion), channel_id=1, source_target_pairs={{0,1},{1,0},{2,3},{3,2},{4,5},{5,4},{6,7},{7,6},{8,9},{9,8},{10,11... | collective-permute-start | bytes 2752520 | tf_op jit(solution)/shard_map/ppermute | solution.py:26
  (23 other events, 25.7 us)
where the time goes:
time: 249 us; the launch traced here: 247 us
  starting transfers between devices  89.3 us (36%)
  blocking collectives  62.2 us (25%)
  local copies, waits for them, and re-layouts  52.1 us (21%)
  other arithmetic  28.9 us (12%)
  waiting for transfers between devices  12.3 us (5%)
    ppermute x13, starting transfers between devices, padded_2(): before = lax.ppermute(last, axis, up)  72.5 us
    psum x1, blocking collectives, local(): summed_all = lax.psum(local_part, ('rows', 'fa'))  62.2 us
    slice x72, local copies, waits for them, and re-layouts, rows_of(): return weight[start_output:start_output + out_rows]  31.6 us
    ppermute x13, starting transfers between devices, padded_2(): after = lax.ppermute(first, axis, down)  16.7 us
    mul x12, other arithmetic, advance(): return rows_of(after_mask) * summed  12.8 us
    mul x12, other arithmetic, advance(): masked = before[start_input:start_input + length] * region  12.6 us
    slice x13, local copies, waits for them, and re-layouts, padded_2(): last = lax.slice_in_dim(shard, length - width, length, axis=dim)  10.5 us
    ppermute x13, waiting for transfers between devices, padded_2(): before = lax.ppermute(last, axis, up)  5.84 us
  transfers between devices with their start and end apart: 27, of which 9 were waited for; matrix products, arithmetic and copies ran while one was open for 15% of the time, Pallas kernels for 0%

commit v1 on v0

v1 whole, which is shorter than its diff:
```python
import functools
import math

import jax
import jax.numpy as jnp
from jax import lax
from jax.experimental import pallas as pl
from jax.experimental.pallas import tpu as pltpu
from jax.sharding import PartitionSpec as P

NSNAP = 4
STRIDE = 3
HALO = NSNAP * STRIDE
LANES = 128
SUB = 8


def up8(count):
    return -(-count // SUB) * SUB


def tiled(array):
    inputs, rows, cols = array.shape
    split = array.reshape(inputs, rows // SUB, SUB, cols // LANES, LANES)
    return split.transpose(0, 1, 3, 2, 4).reshape(-1, LANES)


def untiled(array, shape):
    inputs, rows, cols = shape
    split = array.reshape(inputs, rows // SUB, cols // LANES, SUB, LANES)
    return split.transpose(0, 1, 3, 2, 4).reshape(shape)


def tile_of(rows, cols, row, tile, inputs):
    start = (row // SUB * (cols // LANES) + tile) * SUB + row % SUB
    return pl.ds(start, inputs, stride=rows * cols // LANES)


def pack_kernel(rows, inputs, field, along, across, viscous, solid, up, down, coefs):
    cols = along.shape[1]
    signed = jnp.where(solid[...] != 0, -viscous[...], viscous[...])
    for out, first in ((up, rows - HALO), (down, 0)):
        for step in range(HALO):
            for tile in range(cols // LANES):
                part = field[tile_of(rows, cols, first + step, tile, inputs), :]
                at = (slice(step * inputs, (step + 1) * inputs), slice(tile * LANES, (tile + 1) * LANES))
                out[at] = part.astype(out.dtype)
        coefs[0:HALO, :] = along[first : first + HALO, :]
        coefs[HALO : 2 * HALO, :] = across[first : first + HALO, :]
        coefs[2 * HALO : 3 * HALO, :] = signed[first : first + HALO]
        out[HALO * inputs :, :] = coefs[...].astype(out.dtype)


def march_kernel(
    rows, inputs, adjoint_ref, field, along, across, viscous, solid, area, low, high,
    final, kept, sent,
    state, coefs, raw_x, raw_y, raw_d, east_w, west_w, north_w, south_w, centre_w, scale_w,
):
    adjoint = adjoint_ref[0]
    is_adjoint = adjoint == 1
    cols = along.shape[1]
    half = cols // 2
    span = rows + 2 * HALO
    tiles = cols // LANES

    raw_x[HALO : HALO + rows, :] = along[...]
    raw_y[HALO : HALO + rows, :] = across[...]
    raw_d[HALO : HALO + rows, :] = jnp.where(solid[...] != 0, -viscous[...], viscous[...])
    for source, first in ((low, 0), (high, HALO + rows)):
        coefs[...] = source[HALO * inputs :, :].astype(jnp.float32)
        raw_x[first : first + HALO, :] = coefs[0:HALO, :]
        raw_y[first : first + HALO, :] = coefs[HALO : 2 * HALO, :]
        raw_d[first : first + HALO, :] = coefs[2 * HALO : 3 * HALO, :]
    column = lax.broadcasted_iota(jnp.int32, (SUB, cols), 1)
    for first in range(0, span, SUB):
        at = slice(first, first + SUB)
        signed = raw_d[at, :]
        opened = jnp.where(signed < 0, 0.0, 1.0)
        spread = jnp.abs(signed)
        half_x = raw_x[at, :] * 0.5
        half_y = raw_y[at, :] * 0.5
        east = opened * (spread - half_x)
        west = opened * (spread + half_x)
        north = opened * (spread - half_y)
        south = opened * (spread + half_y)
        east_a = pltpu.roll(west, cols - 1, 1)
        west_a = pltpu.roll(east, 1, 1)
        for ref, values in (
            (east_w, jnp.where(column == cols - 1, 0.0, jnp.where(is_adjoint, east_a, east))),
            (west_w, jnp.where(column == 0, 0.0, jnp.where(is_adjoint, west_a, west))),
            (north_w, jnp.where(is_adjoint, south, north)),
            (south_w, jnp.where(is_adjoint, north, south)),
            (centre_w, opened * (1.0 - 4.0 * spread)),
        ):
            for tile in range(tiles):
                ref[tile * span + first : tile * span + first + SUB, :] = values[
                    :, tile * LANES : (tile + 1) * LANES
                ]
    scale = jnp.where(is_adjoint, area[...], 1.0)
    for tile in range(tiles):
        scale_w[tile * rows : (tile + 1) * rows, :] = scale[:, tile * LANES : (tile + 1) * LANES]

    state[0, 0 : HALO * inputs, :] = low[0 : HALO * inputs, :].astype(jnp.float32)
    state[0, (HALO + rows) * inputs :, :] = high[0 : HALO * inputs, :].astype(jnp.float32)
    for row in range(rows):
        for tile in range(tiles):
            at = (slice((HALO + row) * inputs, (HALO + row + 1) * inputs), slice(tile * LANES, (tile + 1) * LANES))
            state[(0, *at)] = field[tile_of(rows, cols, row, tile, inputs), :]

    lane = lax.broadcasted_iota(jnp.int32, (inputs, LANES), 1)
    group = 2

    for step in range(1, HALO + 1):
        src, dst = (step - 1) % 2, step % 2

        def advance(index, carry, step=step, src=src, dst=dst):
            row0 = step + index * group

            def cell(row, tile):
                at = pl.ds(pl.multiple_of(row * inputs, inputs), inputs)
                return state[src, at, tile * LANES : (tile + 1) * LANES]

            def weight(ref, row, tile):
                return ref[pl.ds(tile * span + row, inputs, stride=0), :]

            for tile in range(tiles):
                column = [cell(row0 + n - 1, tile) for n in range(group + 2)]
                for n in range(group):
                    row = row0 + n
                    here = column[n + 1]
                    after = cell(row, (tile + 1) % tiles)
                    before = cell(row, (tile - 1) % tiles)
                    eastern = pltpu.roll(jnp.where(lane == 0, after, here), LANES - 1, 1)
                    western = pltpu.roll(jnp.where(lane == LANES - 1, before, here), 1, 1)
                    total = weight(centre_w, row, tile) * here
                    total += weight(east_w, row, tile) * eastern
                    total += weight(west_w, row, tile) * western
                    total += weight(north_w, row + adjoint, tile) * column[n + 2]
                    total += weight(south_w, row - adjoint, tile) * column[n]
                    at = pl.ds(pl.multiple_of(row * inputs, inputs), inputs)
                    state[dst, at, tile * LANES : (tile + 1) * LANES] = total
            return carry

        lax.fori_loop(0, (span - 2 * step) // group, advance, 0)
        if step % STRIDE == 0:
            snap = slice((step // STRIDE - 1) * inputs, (step // STRIDE) * inputs)

            def record(row, carry, dst=dst, snap=snap):
                at = pl.ds(pl.multiple_of((HALO + row) * inputs, inputs), inputs)
                for out, first in ((kept, adjoint * (tiles // 2)), (sent, (1 - adjoint) * (tiles // 2))):
                    for tile in range(tiles // 2):
                        where = pl.ds(pl.multiple_of((first + tile) * LANES, LANES), LANES)
                        factor = scale_w[pl.ds((first + tile) * rows + row, inputs, stride=0), :]
                        value = state[dst, at, where] * factor
                        out_at = pl.ds(pl.multiple_of(row * half + tile * LANES, LANES), LANES)
                        out[snap, out_at] = value.astype(out.dtype)
                return carry

            lax.fori_loop(0, rows, record, 0)
    for row in range(rows):
        for tile in range(tiles):
            at = (slice((HALO + row) * inputs, (HALO + row + 1) * inputs), slice(tile * LANES, (tile + 1) * LANES))
            final[tile_of(rows, cols, row, tile, inputs), :] = state[(HALO % 2, *at)]


def local(init_fields, streamwise, crossflow, diffusivity, obstacle, cell_weight):
    adjoint = lax.axis_index("fa").astype(jnp.int32)
    _, inputs, rows, cols = init_fields.shape
    field = tiled(init_fields[0])
    coef_rows = up8(3 * HALO)
    packed_rows = HALO * inputs + coef_rows
    span = rows + 2 * HALO
    half = cols // 2
    vmem = pl.BlockSpec(memory_space=pltpu.VMEM)
    bf16, f32 = jnp.bfloat16, jnp.float32

    packed = jax.ShapeDtypeStruct((packed_rows, cols), bf16)
    up, down = pl.pallas_call(
        functools.partial(pack_kernel, rows, inputs),
        out_shape=(packed, packed),
        in_specs=[vmem] * 5,
        out_specs=(vmem, vmem),
        scratch_shapes=[pltpu.VMEM((coef_rows, cols), f32)],
        name="pack",
    )(field, streamwise, crossflow, diffusivity, obstacle)
    size = lax.axis_size("rows")
    low = lax.ppermute(up, "rows", [(i, i + 1) for i in range(size - 1)])
    high = lax.ppermute(down, "rows", [(i + 1, i) for i in range(size - 1)])

    snaps = jax.ShapeDtypeStruct((NSNAP * inputs, rows * half), bf16)
    grid_rows = pltpu.VMEM((span, cols), f32)
    weights = pltpu.VMEM((cols // LANES * span, LANES), f32)
    final, kept, sent = pl.pallas_call(
        functools.partial(march_kernel, rows, inputs),
        out_shape=(jax.ShapeDtypeStruct(field.shape, f32), snaps, snaps),
        in_specs=[pl.BlockSpec(memory_space=pltpu.SMEM)] + [vmem] * 8,
        out_specs=(vmem,) * 3,
        scratch_shapes=[
            pltpu.VMEM((2, span * inputs, cols), f32),
            pltpu.VMEM((coef_rows, cols), f32),
            *[grid_rows] * 3,
            *[weights] * 5,
            pltpu.VMEM((cols // LANES * rows, LANES), f32),
        ],
        name="march",
    )(adjoint[None], field, streamwise, crossflow, diffusivity, obstacle, cell_weight, low, high)

    other = lax.ppermute(sent, "fa", [(0, 1), (1, 0)])
    product = lax.dot_general(kept, other, (((1,), (1,)), ((), ())), preferred_element_type=f32)
    total = jnp.where(adjoint == 1, product, product.T)
    total = total + lax.ppermute(total, "fa", [(0, 1), (1, 0)])
    if size & (size - 1) == 0:
        stride = 1
        while stride < size:
            total = total + lax.ppermute(total, "rows", [(i, i ^ stride) for i in range(size)])
            stride *= 2
    else:
        total = lax.psum(total, "rows")
    hankel = total * (1.0 / math.sqrt(rows * size * cols))
    return (untiled(final, init_fields.shape[1:])[None], hankel)


def solution(mesh):
    placed = (
        P("fa", "ens", "rows", None),
        P("rows", None),
        P("rows", None),
        P("rows", None),
        P("rows", None),
        P("rows", None),
    )
    return jax.shard_map(
        local,
        mesh=mesh,
        in_specs=placed,
        out_specs=(P("fa", "ens", "rows", None), P("ens", None)),
        check_vma=False,
    )
```

time: 249 us -> 394 us (1.58)
  Pallas kernels: 0 us -> 347 us
  starting transfers between devices: 89.3 us -> 14.6 us
  blocking collectives: 62.2 us -> 0 us
  local copies, waits for them, and re-layouts: 52.1 us -> 1.03 us
  other arithmetic: 28.9 us -> 0.63 us
  waiting for transfers between devices: 12.3 us -> 28.7 us
    pallas_call x0 -> x2, Pallas kernels: none -> 347 us  [the longest x1 343 us: local(): pl.pallas_call(functools.partial(march_kernel, rows, inputs), out_shape=(...]
    ppermute x27 -> x7, starting transfers between devices: 89.3 us -> 14.6 us  [the longest x3 8.24 us: local(): lax.ppermute(total, 'rows', [(i, i ^ stride) for i in range(size)])]
    psum x1 -> x0, blocking collectives: 62.2 us -> none  [local(): summed_all = lax.psum(local_part, ('rows', 'fa'))]
    slice x97 -> x0, local copies, waits for them, and re-layouts: 46.3 us -> none  [the longest x72 31.6 us: rows_of(): return weight[start_output:start_output + out_rows]]
    mul x26 -> x1, other arithmetic: 26.3 us -> 0.61 us  [local(): hankel = total * (1.0 / math.sqrt(rows * size * cols))]
    ppermute x27 -> x7, waiting for transfers between devices: 12.3 us -> 28.7 us  [the longest x1 19.8 us: local(): low = lax.ppermute(up, 'rows', [(i, i + 1) for i in range(size - 1)])]
    unnamed x26 -> x4, local copies, waits for them, and re-layouts: 5.31 us -> 0.95 us
  transfers between devices with their start and end apart: 27 -> 7, of which waited for: 9 -> 6; matrix products, arithmetic and copies ran while one was open for 15% -> 0% of each run, Pallas kernels for 0% -> 0%
where the time goes in v1:
time: 394 us
  Pallas kernels  347 us (88%)
  waiting for transfers between devices  28.7 us (7%)
  starting transfers between devices  14.6 us (4%)
    pallas_call x1, Pallas kernels, local(): pl.pallas_call(functools.partial(march_kernel, rows, inputs), out_shape=(...  343 us
    ppermute x1, waiting for transfers between devices, local(): low = lax.ppermute(up, 'rows', [(i, i + 1) for i in range(size - 1)])  19.8 us
    ppermute x3, starting transfers between devices, local(): lax.ppermute(total, 'rows', [(i, i ^ stride) for i in range(size)])  8.24 us
  transfers between devices with their start and end apart: 7, of which 6 were waited for; matrix products, arithmetic and copies ran while one was open for 0% of the time, Pallas kernels for 0%

profile of v1, /device:TPU:0, one launch (start us, length us, event | category | flops | bytes accessed | tf_op | source)
XLA Modules:
  0.0 393.7 jit_solution(2070536771259804834)
XLA Ops:
  0.6 3.0 pack.1
  3.7 4.9 %collective-permute-start = (bf16[136,1792]{1,0:T(8,128)(2,1)}, bf16[136,1792]{1,0:T(8,128)(2,1)S(1)}, u32[]{:S(2)}, u32[]{:S(2)}) collective-permute-start(bf16[136,1792]{1,0:T(8,128)(2,1)} %get-tuple-element.7), channel_id=1, source_target_pairs={{0,2},{2,4},{4,6},{6,8},{8,10},{10,12},{12,14},{1,3},{3,5},{5,7},{... | collective-permute-start | bytes 1462280 | tf_op jit(solution)/shard_map/ppermute | solution.py:187
  8.6 1.3 collective-permute-start.1
  9.9 19.8 %collective-permute-done.low = bf16[136,1792]{1,0:T(8,128)(2,1)S(1)} collective-permute-done((bf16[136,1792]{1,0:T(8,128)(2,1)}, bf16[136,1792]{1,0:T(8,128)(2,1)S(1)}, u32[]{:S(2)}, u32[]{:S(2)}) %collective-permute-start) | collective-permute-done | bytes 487456 | tf_op jit(solution)/shard_map/ppermute | solution.py:187
  29.7 0.0 copy-start
  29.7 0.0 collective-permute-done.1.high
  29.7 0.0 copy-start.1
  29.7 0.8 copy-done
  30.5 0.2 copy-done.1
  30.6 343.5 %march.1 = (f32[1792,128]{1,0:T(8,128)}, bf16[32,14336]{1,0:T(8,128)(2,1)}, bf16[32,14336]{1,0:T(8,128)(2,1)}) custom-call(s32[1]{0:T(128)} %bitcast.adjoint_ref, f32[1792,128]{1,0:T(8,128)} %bitcast.16, f32[16,1792]{1,0:T(8,128)} %along.3, f32[16,1792]{1,0:T(8,128)} %across.3, f32[16,1792]{1,0:T(8,128)} %viscous.3, s32[16,1792]{1,0:T(8,128)} %solid.3, ...), custom_call_target="tpu_custom_call" | custom-call | tf_op jit(solution)/shard_map/march/pallas_call | solution.py:193
  374.1 0.0 collective-permute-start.2
  374.1 2.7 collective-permute-done.2
  376.8 1.5 fusion
  378.3 0.1 copy.8
  378.4 0.2 collective-permute-start.3
  378.6 1.0 collective-permute-done.3
  379.7 2.4 collective-permute-start.4
  382.0 1.7 collective-permute-done.4
  383.8 2.8 collective-permute-start.5
  386.6 1.7 collective-permute-done.5
  388.3 3.0 collective-permute-start.6
  391.3 1.7 collective-permute-done.6
  393.1 0.6 add_multiply_fusion
  (4 shorter events, 0.0 us)
Async XLA Ops:
  3.7 26.0 %collective-permute-start = (bf16[136,1792]{1,0:T(8,128)(2,1)}, bf16[136,1792]{1,0:T(8,128)(2,1)S(1)}, u32[]{:S(2)}, u32[]{:S(2)}) collective-permute-start(bf16[136,1792]{1,0:T(8,128)(2,1)} %get-tuple-element.7), channel_id=1, source_target_pairs={{0,2},{2,4},{4,6},{6,8},{8,10},{10,12},{12,14},{1,3},{3,5},{5,7},{... | collective-permute-start | bytes 1462280 | tf_op jit(solution)/shard_map/ppermute | solution.py:187
  8.6 21.1 %collective-permute-start.1 = (bf16[136,1792]{1,0:T(8,128)(2,1)}, bf16[136,1792]{1,0:T(8,128)(2,1)S(1)}, u32[]{:S(2)}, u32[]{:S(2)}) collective-permute-start(bf16[136,1792]{1,0:T(8,128)(2,1)} %get-tuple-element.8), channel_id=1, source_target_pairs={{2,0},{4,2},{6,4},{8,6},{10,8},{12,10},{14,12},{3,1},{5,3},{7,5},{... | collective-permute-start | bytes 1462280 | tf_op jit(solution)/shard_map/ppermute | solution.py:188
  29.7 0.8 copy-start
  29.7 0.9 copy-start.1
  374.1 2.7 collective-permute-start.2
  378.4 1.2 collective-permute-start.3
  379.7 4.1 %collective-permute-start.4 = (f32[32,32]{1,0:T(8,128)S(1)}, f32[32,32]{1,0:T(8,128)S(1)}, u32[]{:S(2)}, u32[]{:S(2)}) collective-permute-start(f32[32,32]{1,0:T(8,128)S(1)} %add.12), channel_id=1, source_target_pairs={{0,2},{2,0},{4,6},{6,4},{8,10},{10,8},{12,14},{14,12},{1,3},{3,1},... | collective-permute-start | bytes 12296 | tf_op jit(solution)/shard_map/ppermute | solution.py:215
  383.8 4.5 %collective-permute-start.5 = (f32[32,32]{1,0:T(8,128)S(1)}, f32[32,32]{1,0:T(8,128)S(1)}, u32[]{:S(2)}, u32[]{:S(2)}) collective-permute-start(f32[32,32]{1,0:T(8,128)S(1)} %add.13), channel_id=1, source_target_pairs={{0,4},{2,6},{4,0},{6,2},{8,12},{10,14},{12,8},{14,10},{1,5},{3,7},... | collective-permute-start | bytes 12296 | tf_op jit(solution)/shard_map/ppermute | solution.py:215
  388.3 4.8 %collective-permute-start.6 = (f32[32,32]{1,0:T(8,128)S(1)}, f32[32,32]{1,0:T(8,128)S(1)}, u32[]{:S(2)}, u32[]{:S(2)}) collective-permute-start(f32[32,32]{1,0:T(8,128)S(1)} %add.14), channel_id=1, source_target_pairs={{0,8},{2,10},{4,12},{6,14},{8,0},{10,2},{12,4},{14,6},{1,9},{3,11}... | collective-permute-start | bytes 12296 | tf_op jit(solution)/shard_map/ppermute | solution.py:215

commit v2 on v1

--- a/solution.py
+++ b/solution.py
@@ -54,7 +54,7 @@
 def march_kernel(
     rows, inputs, adjoint_ref, field, along, across, viscous, solid, area, low, high,
     final, kept, sent,
-    state, coefs, raw_x, raw_y, raw_d, east_w, west_w, north_w, south_w, centre_w, scale_w,
+    state_a, state_b, coefs, raw_x, raw_y, raw_d, east_w, west_w, north_w, south_w, centre_w, scale_w,
 ):
     adjoint = adjoint_ref[0]
     is_adjoint = adjoint == 1
@@ -100,25 +100,26 @@
     for tile in range(tiles):
         scale_w[tile * rows : (tile + 1) * rows, :] = scale[:, tile * LANES : (tile + 1) * LANES]
 
-    state[0, 0 : HALO * inputs, :] = low[0 : HALO * inputs, :].astype(jnp.float32)
-    state[0, (HALO + rows) * inputs :, :] = high[0 : HALO * inputs, :].astype(jnp.float32)
+    state_a[0 : HALO * inputs, :] = low[0 : HALO * inputs, :].astype(jnp.float32)
+    state_a[(HALO + rows) * inputs :, :] = high[0 : HALO * inputs, :].astype(jnp.float32)
     for row in range(rows):
         for tile in range(tiles):
             at = (slice((HALO + row) * inputs, (HALO + row + 1) * inputs), slice(tile * LANES, (tile + 1) * LANES))
-            state[(0, *at)] = field[tile_of(rows, cols, row, tile, inputs), :]
-
+            state_a[at] = field[tile_of(rows, cols, row, tile, inputs), :]
+
+    states = (state_a, state_b)
     lane = lax.broadcasted_iota(jnp.int32, (inputs, LANES), 1)
     group = 2
 
     for step in range(1, HALO + 1):
-        src, dst = (step - 1) % 2, step % 2
+        src, dst = states[(step - 1) % 2], states[step % 2]
 
         def advance(index, carry, step=step, src=src, dst=dst):
             row0 = step + index * group
 
             def cell(row, tile):
                 at = pl.ds(pl.multiple_of(row * inputs, inputs), inputs)
-                return state[src, at, tile * LANES : (tile + 1) * LANES]
+                return src[at, tile * LANES : (tile + 1) * LANES]
 
             def weight(ref, row, tile):
                 return ref[pl.ds(tile * span + row, inputs, stride=0), :]
@@ -138,7 +139,7 @@
                     total += weight(north_w, row + adjoint, tile) * column[n + 2]
                     total += weight(south_w, row - adjoint, tile) * column[n]
                     at = pl.ds(pl.multiple_of(row * inputs, inputs), inputs)
-                    state[dst, at, tile * LANES : (tile + 1) * LANES] = total
+                    dst[at, tile * LANES : (tile + 1) * LANES] = total
             return carry
 
         lax.fori_loop(0, (span - 2 * step) // group, advance, 0)
@@ -151,7 +152,7 @@
                     for tile in range(tiles // 2):
                         where = pl.ds(pl.multiple_of((first + tile) * LANES, LANES), LANES)
                         factor = scale_w[pl.ds((first + tile) * rows + row, inputs, stride=0), :]
-                        value = state[dst, at, where] * factor
+                        value = dst[at, where] * factor
                         out_at = pl.ds(pl.multiple_of(row * half + tile * LANES, LANES), LANES)
                         out[snap, out_at] = value.astype(out.dtype)
                 return carry
@@ -160,7 +161,7 @@
     for row in range(rows):
         for tile in range(tiles):
             at = (slice((HALO + row) * inputs, (HALO + row + 1) * inputs), slice(tile * LANES, (tile + 1) * LANES))
-            final[tile_of(rows, cols, row, tile, inputs), :] = state[(HALO % 2, *at)]
+            final[tile_of(rows, cols, row, tile, inputs), :] = states[HALO % 2][at]
 
 
 def local(init_fields, streamwise, crossflow, diffusivity, obstacle, cell_weight):
@@ -196,7 +197,7 @@
         in_specs=[pl.BlockSpec(memory_space=pltpu.SMEM)] + [vmem] * 8,
         out_specs=(vmem,) * 3,
         scratch_shapes=[
-            pltpu.VMEM((2, span * inputs, cols), f32),
+            *[pltpu.VMEM((span * inputs, cols), f32)] * 2,
             pltpu.VMEM((coef_rows, cols), f32),
             *[grid_rows] * 3,
             *[weights] * 5,

time: 394 us -> 78.9 us (0.20)
  Pallas kernels: 347 us -> 31.4 us
    pallas_call x1, Pallas kernels: 343 us -> 28.4 us  [local(): pl.pallas_call(functools.partial(march_kernel, rows, inputs), out_shape=(...]
where the time goes in v2:
time: 78.9 us; the launch traced here: 78.6 us
  Pallas kernels  31.4 us (40%)
  waiting for transfers between devices  28.7 us (36%)
  starting transfers between devices  14.6 us (19%)
  matrix products  1.54 us (2%)
  local copies, waits for them, and re-layouts  1.03 us (1%)
    pallas_call x1, Pallas kernels, local(): pl.pallas_call(functools.partial(march_kernel, rows, inputs), out_shape=(...  28.4 us
    ppermute x1, waiting for transfers between devices, local(): low = lax.ppermute(up, 'rows', [(i, i + 1) for i in range(size - 1)])  19.8 us
    ppermute x3, starting transfers between devices, local(): lax.ppermute(total, 'rows', [(i, i ^ stride) for i in range(size)])  8.24 us
    ppermute x3, waiting for transfers between devices, local(): lax.ppermute(total, 'rows', [(i, i ^ stride) for i in range(size)])  5.15 us
    ppermute x1, starting transfers between devices, local(): low = lax.ppermute(up, 'rows', [(i, i + 1) for i in range(size - 1)])  4.89 us
    pallas_call x1, Pallas kernels, local(): pl.pallas_call(functools.partial(pack_kernel, rows, inputs), out_shape=(p...  3.05 us
    ppermute x1, waiting for transfers between devices, local(): other = lax.ppermute(sent, 'fa', [(0, 1), (1, 0)])  2.68 us
  transfers between devices with their start and end apart: 7, of which 6 were waited for; matrix products, arithmetic and copies ran while one was open for 0% of the time, Pallas kernels for 0%

profile of v2, /device:TPU:0, one launch (start us, length us, event | category | flops | bytes accessed | tf_op | source)
XLA Modules:
  0.0 78.6 jit_solution(5021787606449211470)
XLA Ops:
  0.6 3.0 %pack.1 = (bf16[136,1792]{1,0:T(8,128)(2,1)}, bf16[136,1792]{1,0:T(8,128)(2,1)}) custom-call(f32[1792,128]{1,0:T(8,128)} %bitcast.15, f32[16,1792]{1,0:T(8,128)} %along.3, f32[16,1792]{1,0:T(8,128)} %across.3, f32[16,1792]{1,0:T(8,128)} %viscous.3, s32[16,1792]{1,0:T(8,128)} %solid.3), custom_call_target="tpu_custom_call" | custom-call | tf_op jit(solution)/shard_map/pack/pallas_call | solution.py:179
  3.7 4.9 %collective-permute-start = (bf16[136,1792]{1,0:T(8,128)(2,1)}, bf16[136,1792]{1,0:T(8,128)(2,1)S(1)}, u32[]{:S(2)}, u32[]{:S(2)}) collective-permute-start(bf16[136,1792]{1,0:T(8,128)(2,1)} %get-tuple-element.7), channel_id=1, source_target_pairs={{0,2},{2,4},{4,6},{6,8},{8,10},{10,12},{12,14},{1,3},{3,5},{5,7},{... | collective-permute-start | bytes 1462280 | tf_op jit(solution)/shard_map/ppermute | solution.py:188
  8.6 1.3 %collective-permute-start.1 = (bf16[136,1792]{1,0:T(8,128)(2,1)}, bf16[136,1792]{1,0:T(8,128)(2,1)S(1)}, u32[]{:S(2)}, u32[]{:S(2)}) collective-permute-start(bf16[136,1792]{1,0:T(8,128)(2,1)} %get-tuple-element.8), channel_id=1, source_target_pairs={{2,0},{4,2},{6,4},{8,6},{10,8},{12,10},{14,12},{3,1},{5,3},{7,5},{... | collective-permute-start | bytes 1462280 | tf_op jit(solution)/shard_map/ppermute | solution.py:189
  9.9 19.8 %collective-permute-done.low = bf16[136,1792]{1,0:T(8,128)(2,1)S(1)} collective-permute-done((bf16[136,1792]{1,0:T(8,128)(2,1)}, bf16[136,1792]{1,0:T(8,128)(2,1)S(1)}, u32[]{:S(2)}, u32[]{:S(2)}) %collective-permute-start) | collective-permute-done | bytes 487456 | tf_op jit(solution)/shard_map/ppermute | solution.py:188
  29.7 0.0 copy-start
  29.7 0.0 collective-permute-done.1.high
  29.7 0.0 copy-start.1
  29.7 0.8 %copy-done = bf16[136,1792]{1,0:T(8,128)(2,1)} copy-done((bf16[136,1792]{1,0:T(8,128)(2,1)}, bf16[136,1792]{1,0:T(8,128)(2,1)S(1)}, u32[]{:S(2)}) %copy-start) | copy-done | bytes 487448
  30.5 0.2 copy-done.1
  30.6 28.4 %march.1 = (f32[1792,128]{1,0:T(8,128)}, bf16[32,14336]{1,0:T(8,128)(2,1)}, bf16[32,14336]{1,0:T(8,128)(2,1)}) custom-call(s32[1]{0:T(128)} %bitcast.adjoint_ref, f32[1792,128]{1,0:T(8,128)} %bitcast.16, f32[16,1792]{1,0:T(8,128)} %along.3, f32[16,1792]{1,0:T(8,128)} %across.3, f32[16,1792]{1,0:T(8,128)} %viscous.3, s32[16,1792]{1,0:T(8,128)} %solid.3, ...), custom_call_target="tpu_custom_call" | custom-call | tf_op jit(solution)/shard_map/march/pallas_call | solution.py:194
  59.0 0.0 collective-permute-start.2
  59.0 2.7 %collective-permute-done.2 = bf16[32,14336]{1,0:T(8,128)(2,1)S(1)} collective-permute-done((bf16[32,14336]{1,0:T(8,128)(2,1)}, bf16[32,14336]{1,0:T(8,128)(2,1)S(1)}, u32[]{:S(2)}, u32[]{:S(2)}) %collective-permute-start.2) | collective-permute-done | bytes 917536 | tf_op jit(solution)/shard_map/ppermute | solution.py:209
  61.7 1.5 %fusion = f32[32,32]{1,0:T(8,128)S(1)} fusion(bf16[32,14336]{1,0:T(8,128)(2,1)} %get-tuple-element.10, bf16[32,14336]{1,0:T(8,128)(2,1)S(1)} %collective-permute-done.2), kind=kOutput, calls=%fused_computation.2 | convolution fusion | flops 29360128 | bytes 1839104 | tf_op jit(solution)/shard_map/dot_general | solution.py:210
  63.3 0.1 copy.8
  63.3 0.2 collective-permute-start.3
  63.5 1.0 %collective-permute-done.3 = f32[32,32]{1,0:T(8,128)S(1)} collective-permute-done((f32[32,32]{1,0:T(8,128)S(1)}, f32[32,32]{1,0:T(8,128)S(1)}, u32[]{:S(2)}, u32[]{:S(2)}) %collective-permute-start.3) | collective-permute-done | bytes 4128 | tf_op jit(solution)/shard_map/ppermute | solution.py:212
  64.6 2.4 %collective-permute-start.4 = (f32[32,32]{1,0:T(8,128)S(1)}, f32[32,32]{1,0:T(8,128)S(1)}, u32[]{:S(2)}, u32[]{:S(2)}) collective-permute-start(f32[32,32]{1,0:T(8,128)S(1)} %add.12), channel_id=1, source_target_pairs={{0,2},{2,0},{4,6},{6,4},{8,10},{10,8},{12,14},{14,12},{1,3},{3,1},... | collective-permute-start | bytes 12296 | tf_op jit(solution)/shard_map/ppermute | solution.py:216
  67.0 1.7 %collective-permute-done.4 = f32[32,32]{1,0:T(8,128)S(1)} collective-permute-done((f32[32,32]{1,0:T(8,128)S(1)}, f32[32,32]{1,0:T(8,128)S(1)}, u32[]{:S(2)}, u32[]{:S(2)}) %collective-permute-start.4) | collective-permute-done | bytes 4128 | tf_op jit(solution)/shard_map/ppermute | solution.py:216
  68.7 2.8 %collective-permute-start.5 = (f32[32,32]{1,0:T(8,128)S(1)}, f32[32,32]{1,0:T(8,128)S(1)}, u32[]{:S(2)}, u32[]{:S(2)}) collective-permute-start(f32[32,32]{1,0:T(8,128)S(1)} %add.13), channel_id=1, source_target_pairs={{0,4},{2,6},{4,0},{6,2},{8,12},{10,14},{12,8},{14,10},{1,5},{3,7},... | collective-permute-start | bytes 12296 | tf_op jit(solution)/shard_map/ppermute | solution.py:216
  71.5 1.7 %collective-permute-done.5 = f32[32,32]{1,0:T(8,128)S(1)} collective-permute-done((f32[32,32]{1,0:T(8,128)S(1)}, f32[32,32]{1,0:T(8,128)S(1)}, u32[]{:S(2)}, u32[]{:S(2)}) %collective-permute-start.5) | collective-permute-done | bytes 4128 | tf_op jit(solution)/shard_map/ppermute | solution.py:216
  73.2 3.0 %collective-permute-start.6 = (f32[32,32]{1,0:T(8,128)S(1)}, f32[32,32]{1,0:T(8,128)S(1)}, u32[]{:S(2)}, u32[]{:S(2)}) collective-permute-start(f32[32,32]{1,0:T(8,128)S(1)} %add.14), channel_id=1, source_target_pairs={{0,8},{2,10},{4,12},{6,14},{8,0},{10,2},{12,4},{14,6},{1,9},{3,11}... | collective-permute-start | bytes 12296 | tf_op jit(solution)/shard_map/ppermute | solution.py:216
  76.3 1.7 %collective-permute-done.6 = f32[32,32]{1,0:T(8,128)S(1)} collective-permute-done((f32[32,32]{1,0:T(8,128)S(1)}, f32[32,32]{1,0:T(8,128)S(1)}, u32[]{:S(2)}, u32[]{:S(2)}) %collective-permute-start.6) | collective-permute-done | bytes 4128 | tf_op jit(solution)/shard_map/ppermute | solution.py:216
  78.0 0.6 add_multiply_fusion
  (4 shorter events, 0.0 us)
Async XLA Ops:
  3.7 26.0 %collective-permute-start = (bf16[136,1792]{1,0:T(8,128)(2,1)}, bf16[136,1792]{1,0:T(8,128)(2,1)S(1)}, u32[]{:S(2)}, u32[]{:S(2)}) collective-permute-start(bf16[136,1792]{1,0:T(8,128)(2,1)} %get-tuple-element.7), channel_id=1, source_target_pairs={{0,2},{2,4},{4,6},{6,8},{8,10},{10,12},{12,14},{1,3},{3,5},{5,7},{... | collective-permute-start | bytes 1462280 | tf_op jit(solution)/shard_map/ppermute | solution.py:188
  8.6 21.1 %collective-permute-start.1 = (bf16[136,1792]{1,0:T(8,128)(2,1)}, bf16[136,1792]{1,0:T(8,128)(2,1)S(1)}, u32[]{:S(2)}, u32[]{:S(2)}) collective-permute-start(bf16[136,1792]{1,0:T(8,128)(2,1)} %get-tuple-element.8), channel_id=1, source_target_pairs={{2,0},{4,2},{6,4},{8,6},{10,8},{12,10},{14,12},{3,1},{5,3},{7,5},{... | collective-permute-start | bytes 1462280 | tf_op jit(solution)/shard_map/ppermute | solution.py:189
  29.7 0.8 %copy-start = (bf16[136,1792]{1,0:T(8,128)(2,1)}, bf16[136,1792]{1,0:T(8,128)(2,1)S(1)}, u32[]{:S(2)}) copy-start(bf16[136,1792]{1,0:T(8,128)(2,1)S(1)} %collective-permute-done.low) | copy-start | bytes 1462276
  29.7 0.9 %copy-start.1 = (bf16[136,1792]{1,0:T(8,128)(2,1)}, bf16[136,1792]{1,0:T(8,128)(2,1)S(1)}, u32[]{:S(2)}) copy-start(bf16[136,1792]{1,0:T(8,128)(2,1)S(1)} %collective-permute-done.1.high) | copy-start | bytes 1462276
  59.0 2.7 %collective-permute-start.2 = (bf16[32,14336]{1,0:T(8,128)(2,1)}, bf16[32,14336]{1,0:T(8,128)(2,1)S(1)}, u32[]{:S(2)}, u32[]{:S(2)}) collective-permute-start(bf16[32,14336]{1,0:T(8,128)(2,1)} %get-tuple-element.11), channel_id=1, source_target_pairs={{0,1},{1,0},{2,3},{3,2},{4,5},{5,4},{6,7},{7,6},{8,9},{9,8},{10,11... | collective-permute-start | bytes 2752520 | tf_op jit(solution)/shard_map/ppermute | solution.py:209
  63.3 1.2 %collective-permute-start.3 = (f32[32,32]{1,0:T(8,128)S(1)}, f32[32,32]{1,0:T(8,128)S(1)}, u32[]{:S(2)}, u32[]{:S(2)}) collective-permute-start(f32[32,32]{1,0:T(8,128)S(1)} %bitcast_select_fusion), channel_id=1, source_target_pairs={{0,1},{1,0},{2,3},{3,2},{4,5},{5,4},{6,7},{7,6},{8,9},{9,8},{10,11... | collective-permute-start | bytes 12296 | tf_op jit(solution)/shard_map/ppermute | solution.py:212
  64.6 4.1 %collective-permute-start.4 = (f32[32,32]{1,0:T(8,128)S(1)}, f32[32,32]{1,0:T(8,128)S(1)}, u32[]{:S(2)}, u32[]{:S(2)}) collective-permute-start(f32[32,32]{1,0:T(8,128)S(1)} %add.12), channel_id=1, source_target_pairs={{0,2},{2,0},{4,6},{6,4},{8,10},{10,8},{12,14},{14,12},{1,3},{3,1},... | collective-permute-start | bytes 12296 | tf_op jit(solution)/shard_map/ppermute | solution.py:216
  68.7 4.5 %collective-permute-start.5 = (f32[32,32]{1,0:T(8,128)S(1)}, f32[32,32]{1,0:T(8,128)S(1)}, u32[]{:S(2)}, u32[]{:S(2)}) collective-permute-start(f32[32,32]{1,0:T(8,128)S(1)} %add.13), channel_id=1, source_target_pairs={{0,4},{2,6},{4,0},{6,2},{8,12},{10,14},{12,8},{14,10},{1,5},{3,7},... | collective-permute-start | bytes 12296 | tf_op jit(solution)/shard_map/ppermute | solution.py:216
  73.2 4.8 %collective-permute-start.6 = (f32[32,32]{1,0:T(8,128)S(1)}, f32[32,32]{1,0:T(8,128)S(1)}, u32[]{:S(2)}, u32[]{:S(2)}) collective-permute-start(f32[32,32]{1,0:T(8,128)S(1)} %add.14), channel_id=1, source_target_pairs={{0,8},{2,10},{4,12},{6,14},{8,0},{10,2},{12,4},{14,6},{1,9},{3,11}... | collective-permute-start | bytes 12296 | tf_op jit(solution)/shard_map/ppermute | solution.py:216

commit v3 on v2

v3 whole, which is shorter than its diff:
```python
import functools
import math

import jax
import jax.numpy as jnp
from jax import lax
from jax.experimental import pallas as pl
from jax.experimental.pallas import tpu as pltpu
from jax.sharding import PartitionSpec as P

NSNAP = 4
STRIDE = 3
HALO = NSNAP * STRIDE
LANES = 128
SUB = 8
PAIR = 2 * LANES
F32 = jnp.float32
BF16 = jnp.bfloat16


def up8(count):
    return -(-count // SUB) * SUB


def lanes_of(tile):
    return slice(tile * LANES, (tile + 1) * LANES)


def tiled(array):
    inputs, rows, cols = array.shape
    split = array.reshape(inputs, rows // SUB, SUB, cols // LANES, LANES)
    return split.transpose(0, 1, 3, 2, 4).reshape(-1, LANES)


def untiled(array, shape):
    inputs, rows, cols = shape
    split = array.reshape(inputs, rows // SUB, cols // LANES, SUB, LANES)
    return split.transpose(0, 1, 3, 2, 4).reshape(shape)


def tile_of(rows, cols, row, tile, inputs):
    start = (row // SUB * (cols // LANES) + tile) * SUB + row % SUB
    return pl.ds(start, inputs, stride=rows * cols // LANES)


def sorting_matrix(back=False):
    source = lax.broadcasted_iota(jnp.int32, (PAIR, PAIR), 1 if back else 0)
    target = lax.broadcasted_iota(jnp.int32, (PAIR, PAIR), 0 if back else 1)
    wanted = jnp.where(target < LANES, 2 * target, 2 * (target - LANES) + 1)
    return jnp.where(source == wanted, 1.0, 0.0).astype(BF16)


def moved(part, matrix):
    return jnp.dot(part, matrix, preferred_element_type=F32)


def moved_whole(values, matrix):
    top = values.astype(BF16)
    rest = values - top.astype(F32)
    middle = rest.astype(BF16)
    bottom = (rest - middle.astype(F32)).astype(BF16)
    return (moved(top, matrix) + moved(middle, matrix)) + moved(bottom, matrix)


def eastern(tiles, tile, lane, count):
    if tile % 2 == 0:
        return tiles[tile + 1]
    after = tiles[(tile + 1) % count]
    return pltpu.roll(jnp.where(lane == 0, after, tiles[tile - 1]), LANES - 1, 1)


def western(tiles, tile, lane, count):
    if tile % 2 == 1:
        return tiles[tile - 1]
    before = tiles[(tile - 1) % count]
    return pltpu.roll(jnp.where(lane == LANES - 1, before, tiles[tile + 1]), 1, 1)


def weights_of(along, across, signed, is_adjoint):
    lane = lax.broadcasted_iota(jnp.int32, along[0].shape, 1)
    count = len(along)
    east, west, north, south, centre = [], [], [], [], []
    for tile in range(count):
        opened = jnp.where(signed[tile] < 0, 0.0, 1.0)
        spread = jnp.abs(signed[tile])
        half_x, half_y = along[tile] * 0.5, across[tile] * 0.5
        east.append(opened * (spread - half_x))
        west.append(opened * (spread + half_x))
        low, high = opened * (spread - half_y), opened * (spread + half_y)
        north.append(jnp.where(is_adjoint, high, low))
        south.append(jnp.where(is_adjoint, low, high))
        centre.append(opened * (1.0 - 4.0 * spread))
    east_w = [jnp.where(is_adjoint, eastern(west, t, lane, count), east[t]) for t in range(count)]
    west_w = [jnp.where(is_adjoint, western(east, t, lane, count), west[t]) for t in range(count)]
    east_w[-1] = jnp.where(lane == LANES - 1, 0.0, east_w[-1])
    west_w[0] = jnp.where(lane == 0, 0.0, west_w[0])
    return east_w, west_w, north, south, centre


def pack_kernel(rows, inputs, field, along, across, viscous, solid, up, down, coefs):
    cols = along.shape[1]
    signed = jnp.where(solid[...] != 0, -viscous[...], viscous[...])
    for out, first in ((up, rows - HALO), (down, 0)):
        for step in range(HALO):
            for tile in range(cols // LANES):
                part = field[tile_of(rows, cols, first + step, tile, inputs), :]
                out[step * inputs : (step + 1) * inputs, lanes_of(tile)] = part.astype(out.dtype)
        coefs[0:HALO, :] = along[first : first + HALO, :]
        coefs[HALO : 2 * HALO, :] = across[first : first + HALO, :]
        coefs[2 * HALO : 3 * HALO, :] = signed[first : first + HALO]
        out[HALO * inputs :, :] = coefs[...].astype(out.dtype)


def prepare_kernel(
    rows, inputs, adjoint_ref, field, along, across, viscous, solid, area, own, weights, scale, lined
):
    is_adjoint = adjoint_ref[0] == 1
    cols = along.shape[1]
    matrix = sorting_matrix()
    for row in range(rows):
        for tile in range(cols // LANES):
            lined[row * inputs : (row + 1) * inputs, lanes_of(tile)] = field[
                tile_of(rows, cols, row, tile, inputs), :
            ]
    signed = jnp.where(solid[...] != 0, -viscous[...], viscous[...])
    factor = jnp.where(is_adjoint, area[...], 1.0)
    sorted_coefs = [[], [], []]
    for pair in range(cols // PAIR):
        at = slice(pair * PAIR, (pair + 1) * PAIR)
        own[:, at] = moved_whole(lined[:, at], matrix)
        for kept, values in zip(sorted_coefs, (along[:, at], across[:, at], signed[:, at])):
            values = moved_whole(values, matrix)
            kept += [values[:, :LANES], values[:, LANES:]]
        values = moved_whole(factor[:, at], matrix)
        for side in range(2):
            tile = 2 * pair + side
            scale[tile * rows : (tile + 1) * rows, :] = values[:, lanes_of(side)]
    for index, tiles in enumerate(weights_of(*sorted_coefs, is_adjoint)):
        for tile, values in enumerate(tiles):
            weights[index, tile * rows : (tile + 1) * rows, :] = values


def march_kernel(
    rows, inputs, adjoint_ref, own, own_weights, scale, low, high,
    final, kept, sent,
    state_a, state_b, coefs, east_w, west_w, north_w, south_w, centre_w,
):
    adjoint = adjoint_ref[0]
    is_adjoint = adjoint == 1
    cols = own.shape[1]
    half = cols // 2
    span = rows + 2 * HALO
    wide = span + 2 * SUB
    tiles = cols // LANES
    matrix = sorting_matrix()
    all_weights = (east_w, west_w, north_w, south_w, centre_w)

    for source, first in ((low, 0), (high, HALO + rows)):
        sorted_coefs = [[], [], []]
        for pair in range(cols // PAIR):
            at = slice(pair * PAIR, (pair + 1) * PAIR)
            values = moved(source[:, at], matrix)
            state_a[(1 + first) * inputs : (1 + first + HALO) * inputs, at] = values[: HALO * inputs]
            coefs[:, at] = values[HALO * inputs :]
            for index, taken in enumerate(sorted_coefs):
                part = coefs[index * HALO : (index + 1) * HALO, at]
                taken += [part[:, :LANES], part[:, LANES:]]
        for ref, values in zip(all_weights, weights_of(*sorted_coefs, is_adjoint)):
            for tile in range(tiles):
                start = tile * wide + SUB + first
                ref[start : start + HALO, :] = values[tile]
    state_a[(1 + HALO) * inputs : (1 + HALO + rows) * inputs, :] = own[...]
    for index, ref in enumerate(all_weights):
        for tile in range(tiles):
            start = tile * wide + SUB + HALO
            ref[start : start + rows, :] = own_weights[index, tile * rows : (tile + 1) * rows, :]

    states = (state_a, state_b)
    lane = lax.broadcasted_iota(jnp.int32, (inputs, LANES), 1)
    for step in range(1, HALO + 1):
        src, dst = states[(step - 1) % 2], states[step % 2]
        count = span - 2 * step
        group = min((8, 7, 9, 10, 6, 11), key=lambda size: -(-count // size) * size)
        trips = -(-count // group)
        first_row = step - (trips * group - count) // 2

        def advance(index, carry, src=src, dst=dst, first_row=first_row, group=group):
            row0 = first_row + index * group

            def at_row(row):
                return pl.ds(pl.multiple_of((1 + row) * inputs, inputs), inputs)

            def weight(ref, row, tile):
                return ref[pl.ds(tile * wide + SUB + row, inputs, stride=0), :]

            lines = [{} for _ in range(group + 2)]
            for pair in range(tiles // 2):
                for n, line in enumerate(lines):
                    for tile in (2 * pair - 1, 2 * pair, 2 * pair + 1, 2 * pair + 2):
                        tile %= tiles
                        if tile not in line and (tile // 2 == pair or 0 < n <= group):
                            line[tile] = src[at_row(row0 + n - 1), lanes_of(tile)]
                for n in range(group):
                    row = row0 + n
                    here = lines[n + 1]
                    for tile in (2 * pair, 2 * pair + 1):
                        total = weight(centre_w, row, tile) * here[tile]
                        total += weight(north_w, row + adjoint, tile) * lines[n + 2][tile]
                        total += weight(south_w, row - adjoint, tile) * lines[n][tile]
                        total += weight(east_w, row, tile) * eastern(here, tile, lane, tiles)
                        total += weight(west_w, row, tile) * western(here, tile, lane, tiles)
                        dst[at_row(row), lanes_of(tile)] = total
            return carry

        lax.fori_loop(0, trips, advance, 0)
        if step % STRIDE == 0:
            snap = slice((step // STRIDE - 1) * inputs, (step // STRIDE) * inputs)

            def record(first, second, scaled, dst=dst, snap=snap):
                for row in range(rows):
                    at = slice((1 + HALO + row) * inputs, (2 + HALO + row) * inputs)
                    for tile in range(tiles):
                        value = dst[at, lanes_of(tile)]
                        if scaled:
                            value = value * scale[pl.ds(tile * rows + row, inputs, stride=0), :]
                        out = first if tile < tiles // 2 else second
                        start = row * half + tile % (tiles // 2) * LANES
                        out[snap, start : start + LANES] = value.astype(out.dtype)

            @pl.when(is_adjoint)
            def _():
                record(sent, kept, True)

            @pl.when(jnp.logical_not(is_adjoint))
            def _():
                record(kept, sent, False)

    final[...] = states[HALO % 2][(1 + HALO) * inputs : (1 + HALO + rows) * inputs, :]


def finish_kernel(rows, inputs, last, final):
    cols = last.shape[1]
    matrix = sorting_matrix(back=True)
    for pair in range(cols // PAIR):
        values = moved_whole(last[:, pair * PAIR : (pair + 1) * PAIR], matrix)
        for row in range(rows):
            for side in range(2):
                final[tile_of(rows, cols, row, 2 * pair + side, inputs), :] = values[
                    row * inputs : (row + 1) * inputs, lanes_of(side)
                ]


def local(init_fields, streamwise, crossflow, diffusivity, obstacle, cell_weight):
    adjoint = lax.axis_index("fa").astype(jnp.int32)
    flag = adjoint[None]
    _, inputs, rows, cols = init_fields.shape
    field = tiled(init_fields[0])
    coef_rows = up8(3 * HALO)
    packed_rows = HALO * inputs + coef_rows
    span = rows + 2 * HALO
    half = cols // 2
    tiles = cols // LANES
    vmem = pl.BlockSpec(memory_space=pltpu.VMEM)
    smem = pl.BlockSpec(memory_space=pltpu.SMEM)

    def shape(*dims, dtype=F32):
        return jax.ShapeDtypeStruct(dims, dtype)

    def cost(amount):
        return pl.CostEstimate(flops=amount, bytes_accessed=4 * field.size * 4, transcendentals=0)

    params = pltpu.CompilerParams(vmem_limit_bytes=24 << 20)
    packed = shape(packed_rows, cols, dtype=BF16)
    up, down = pl.pallas_call(
        functools.partial(pack_kernel, rows, inputs),
        out_shape=(packed, packed),
        in_specs=[vmem] * 5,
        out_specs=(vmem, vmem),
        scratch_shapes=[pltpu.VMEM((coef_rows, cols), F32)],
        compiler_params=params,
        name="pack",
    )(field, streamwise, crossflow, diffusivity, obstacle)
    size = lax.axis_size("rows")
    low = lax.ppermute(up, "rows", [(i, i + 1) for i in range(size - 1)])
    high = lax.ppermute(down, "rows", [(i + 1, i) for i in range(size - 1)])

    own, own_weights, scale = pl.pallas_call(
        functools.partial(prepare_kernel, rows, inputs),
        out_shape=(
            shape(rows * inputs, cols),
            shape(5, tiles * rows, LANES),
            shape(tiles * rows, LANES),
        ),
        in_specs=[smem] + [vmem] * 6,
        out_specs=(vmem,) * 3,
        scratch_shapes=[pltpu.VMEM((rows * inputs, cols), F32)],
        compiler_params=params,
        cost_estimate=cost(10**9),
        name="prepare",
    )(flag, field, streamwise, crossflow, diffusivity, obstacle, cell_weight)

    snaps = shape(NSNAP * inputs, rows * half, dtype=BF16)
    last, kept, sent = pl.pallas_call(
        functools.partial(march_kernel, rows, inputs),
        out_shape=(shape(rows * inputs, cols), snaps, snaps),
        in_specs=[smem] + [vmem] * 5,
        out_specs=(vmem,) * 3,
        scratch_shapes=[
            *[pltpu.VMEM(((span + 2) * inputs, cols), F32)] * 2,
            pltpu.VMEM((coef_rows, cols), F32),
            *[pltpu.VMEM((tiles * (span + 2 * SUB), LANES), F32)] * 5,
        ],
        compiler_params=params,
        name="march",
    )(flag, own, own_weights, scale, low, high)

    other = lax.ppermute(sent, "fa", [(0, 1), (1, 0)])
    product = lax.dot_general(kept, other, (((1,), (1,)), ((), ())), preferred_element_type=F32)
    total = jnp.where(adjoint == 1, product, product.T)
    total = total + lax.ppermute(total, "fa", [(0, 1), (1, 0)])
    if size & (size - 1) == 0:
        stride = 1
        while stride < size:
            total = total + lax.ppermute(total, "rows", [(i, i ^ stride) for i in range(size)])
            stride *= 2
    else:
        total = lax.psum(total, "rows")
    hankel = total * (1.0 / math.sqrt(rows * size * cols))
    final = pl.pallas_call(
        functools.partial(finish_kernel, rows, inputs),
        out_shape=shape(*field.shape),
        in_specs=[vmem],
        out_specs=vmem,
        compiler_params=params,
        cost_estimate=cost(10**7),
        name="finish",
    )(last)
    return (untiled(final, init_fields.shape[1:])[None], hankel)


def solution(mesh):
    placed = (
        P("fa", "ens", "rows", None),
        P("rows", None),
        P("rows", None),
        P("rows", None),
        P("rows", None),
        P("rows", None),
    )
    return jax.shard_map(
        local,
        mesh=mesh,
        in_specs=placed,
        out_specs=(P("fa", "ens", "rows", None), P("ens", None)),
        check_vma=False,
    )
```

time: 78.9 us -> 64.5 us (0.82)
  Pallas kernels: 31.4 us -> 18 us
  waiting for transfers between devices: 28.7 us -> 23.9 us
  local copies, waits for them, and re-layouts: 1.03 us -> 5.76 us
  matrix products: 1.54 us -> 0.37 us
    pallas_call x1, Pallas kernels: 28.4 us -> 12.5 us  [local(): pl.pallas_call(functools.partial(march_kernel, rows, inputs), out_shape=(...]
    unnamed x4 -> x22, local copies, waits for them, and re-layouts: 0.95 us -> 5.68 us
    pallas_call x0 -> x2, Pallas kernels: none -> 3.94 us  [the longest x1 2.13 us: local(): pl.pallas_call(functools.partial(prepare_kernel, rows, inputs), out_shape...]
    ppermute x1, waiting for transfers between devices: 19.8 us -> 16.7 us  [local(): low = lax.ppermute(up, 'rows', [(i, i + 1) for i in range(size - 1)])]
    ppermute x3, waiting for transfers between devices: 5.15 us -> 3.43 us  [local(): lax.ppermute(total, 'rows', [(i, i ^ stride) for i in range(size)])]
    pallas_call x1, Pallas kernels: 3.05 us -> 1.64 us  [local(): pl.pallas_call(functools.partial(pack_kernel, rows, inputs), out_shape=(p...]
    dot_general x1, matrix products: 1.54 us -> 0.37 us  [local(): lax.dot_general(kept, other, (((1,), (1,)), ((), ())), preferred_element_...]
  transfers between devices with their start and end apart: 7 -> 7, of which waited for: 6 -> 5; matrix products, arithmetic and copies ran while one was open for 0% -> 0% of each run, Pallas kernels for 0% -> 6%
where the time goes in v3:
time: 64.5 us; the launch traced here: 64.2 us
  waiting for transfers between devices  23.9 us (37%)
  Pallas kernels  18 us (28%)
  starting transfers between devices  14.8 us (23%)
  local copies, waits for them, and re-layouts  5.76 us (9%)
  between operations  0.74 us (1%)
    ppermute x1, waiting for transfers between devices, local(): low = lax.ppermute(up, 'rows', [(i, i + 1) for i in range(size - 1)])  16.7 us
    pallas_call x1, Pallas kernels, local(): pl.pallas_call(functools.partial(march_kernel, rows, inputs), out_shape=(...  12.5 us
    ppermute x3, starting transfers between devices, local(): lax.ppermute(total, 'rows', [(i, i ^ stride) for i in range(size)])  8.42 us
    unnamed x22, local copies, waits for them, and re-layouts  5.68 us
    ppermute x1, starting transfers between devices, local(): low = lax.ppermute(up, 'rows', [(i, i + 1) for i in range(size - 1)])  4.89 us
    ppermute x3, waiting for transfers between devices, local(): lax.ppermute(total, 'rows', [(i, i ^ stride) for i in range(size)])  3.43 us
    ppermute x1, waiting for transfers between devices, local(): other = lax.ppermute(sent, 'fa', [(0, 1), (1, 0)])  2.68 us
    pallas_call x1, Pallas kernels, local(): pl.pallas_call(functools.partial(prepare_kernel, rows, inputs), out_shape...  2.13 us
  transfers between devices with their start and end apart: 7, of which 5 were waited for; matrix products, arithmetic and copies ran while one was open for 0% of the time, Pallas kernels for 6%

profile of v3, /device:TPU:0, one launch (start us, length us, event | category | flops | bytes accessed | tf_op | source)
XLA Modules:
  0.0 64.2 jit_solution(7137948084866315651)
XLA Ops:
  0.6 0.0 copy-start
  0.6 1.2 %copy-done = f32[1,8,16,1792]{3,2,1,0:T(8,128)S(1)} copy-done((f32[1,8,16,1792]{3,2,1,0:T(8,128)S(1)}, f32[1,8,16,1792]{3,2,1,0:T(8,128)}, u32[]{:S(2)}) %copy-start) | copy-done | bytes 917528
  1.8 0.0 copy-start.2
  1.8 0.9 %copy-done.2 = f32[16,1792]{1,0:T(8,128)S(1)} copy-done((f32[16,1792]{1,0:T(8,128)S(1)}, f32[16,1792]{1,0:T(8,128)}, u32[]{:S(2)}) %copy-start.2) | copy-done | bytes 114712
  2.7 0.0 copy-start.4
  2.7 0.9 %copy-done.4 = f32[16,1792]{1,0:T(8,128)S(1)} copy-done((f32[16,1792]{1,0:T(8,128)S(1)}, f32[16,1792]{1,0:T(8,128)}, u32[]{:S(2)}) %copy-start.4) | copy-done | bytes 114712
  3.6 0.0 copy-start.6
  3.6 0.9 %copy-done.6 = f32[16,1792]{1,0:T(8,128)S(1)} copy-done((f32[16,1792]{1,0:T(8,128)S(1)}, f32[16,1792]{1,0:T(8,128)}, u32[]{:S(2)}) %copy-start.6) | copy-done | bytes 114712
  4.5 0.0 copy-start.8
  4.5 0.9 %copy-done.8 = s32[16,1792]{1,0:T(8,128)S(1)} copy-done((s32[16,1792]{1,0:T(8,128)S(1)}, s32[16,1792]{1,0:T(8,128)}, u32[]{:S(2)}) %copy-start.8) | copy-done | bytes 114712
  5.4 0.0 copy-start.1
  5.4 0.0 copy-start.3
  5.4 0.0 copy-start.5
  5.4 0.0 copy-start.7
  5.4 0.0 copy-start.9
  5.4 1.6 %pack.1 = (bf16[136,1792]{1,0:T(8,128)(2,1)}, bf16[136,1792]{1,0:T(8,128)(2,1)S(1)}) custom-call(f32[1792,128]{1,0:T(8,128)S(1)} %bitcast.15, f32[16,1792]{1,0:T(8,128)S(1)} %copy-done.2, f32[16,1792]{1,0:T(8,128)S(1)} %copy-done.4, f32[16,1792]{1,0:T(8,128)S(1)} %copy-done.6, s32[16,1792]{1,0:T(8,128)S(1)} %copy-done.8), custom_call_target="tpu_custom_call" | custom-call | tf_op jit(solution)/shard_map/pack/pallas_call | solution.py:274
  7.1 4.9 %collective-permute-start = (bf16[136,1792]{1,0:T(8,128)(2,1)}, bf16[136,1792]{1,0:T(8,128)(2,1)S(1)}, u32[]{:S(2)}, u32[]{:S(2)}) collective-permute-start(bf16[136,1792]{1,0:T(8,128)(2,1)} %get-tuple-element.13), channel_id=1, source_target_pairs={{0,2},{2,4},{4,6},{6,8},{8,10},{10,12},{12,14},{1,3},{3,5},{5,7},{... | collective-permute-start | bytes 1462280 | tf_op jit(solution)/shard_map/ppermute | solution.py:284
  12.0 1.3 %collective-permute-start.1 = (bf16[136,1792]{1,0:T(8,128)(2,1)S(1)}, bf16[136,1792]{1,0:T(8,128)(2,1)S(1)}, u32[]{:S(2)}, u32[]{:S(2)}) collective-permute-start(bf16[136,1792]{1,0:T(8,128)(2,1)S(1)} %get-tuple-element.14), channel_id=1, source_target_pairs={{2,0},{4,2},{6,4},{8,6},{10,8},{12,10},{14,12},{3,1},{5,3},{7,5},{... | collective-permute-start | bytes 1462280 | tf_op jit(solution)/shard_map/ppermute | solution.py:285
  13.3 0.0 copy-done.1
  13.3 0.0 copy-done.3
  13.3 0.0 copy-done.5
  13.3 0.0 copy-done.7
  13.3 0.0 copy-done.9
  13.3 0.0 copy-start.10
  13.3 0.9 %copy-done.10 = f32[16,1792]{1,0:T(8,128)S(1)} copy-done((f32[16,1792]{1,0:T(8,128)S(1)}, f32[16,1792]{1,0:T(8,128)}, u32[]{:S(2)}) %copy-start.10) | copy-done | bytes 114712
  14.2 2.1 %prepare.1 = (f32[128,1792]{1,0:T(8,128)S(1)}, f32[5,224,128]{2,1,0:T(8,128)S(1)}, f32[224,128]{1,0:T(8,128)S(1)}) custom-call(s32[1]{0:T(128)} %bitcast.adjoint_ref, f32[1792,128]{1,0:T(8,128)S(1)} %bitcast.16, f32[16,1792]{1,0:T(8,128)S(1)} %copy-done.3, f32[16,1792]{1,0:T(8,128)S(1)} %copy-done.5, f32[16,1792]{1,0:T(8,128)S(1)} %copy-done.7, ...), custom_call_target="tpu_custom_call" | custom-call | flops 1000000000 | bytes 3670016 | tf_op jit(solution)/shard_map/prepare/pallas_call | solution.py:287
  16.4 16.7 %collective-permute-done.low = bf16[136,1792]{1,0:T(8,128)(2,1)S(1)} collective-permute-done((bf16[136,1792]{1,0:T(8,128)(2,1)}, bf16[136,1792]{1,0:T(8,128)(2,1)S(1)}, u32[]{:S(2)}, u32[]{:S(2)}) %collective-permute-start) | collective-permute-done | bytes 487456 | tf_op jit(solution)/shard_map/ppermute | solution.py:284
  33.1 0.0 collective-permute-done.1.high
  33.1 12.5 %march.1 = (f32[128,1792]{1,0:T(8,128)S(1)}, bf16[32,14336]{1,0:T(8,128)(2,1)S(1)}, bf16[32,14336]{1,0:T(8,128)(2,1)}) custom-call(s32[1]{0:T(128)} %bitcast.adjoint_ref, f32[128,1792]{1,0:T(8,128)S(1)} %get-tuple-element.10.own, f32[5,224,128]{2,1,0:T(8,128)S(1)} %get-tuple-element.11.own_weights, f32[224,128]{1,0:T(8,128)S(1)} %get-tuple-element.12.scale, ...), custom_call_target="tpu_custom_call" | custom-call | tf_op jit(solution)/shard_map/march/pallas_call | solution.py:303
  45.5 0.0 collective-permute-start.2
  45.5 2.7 %collective-permute-done.2 = bf16[32,14336]{1,0:T(8,128)(2,1)S(1)} collective-permute-done((bf16[32,14336]{1,0:T(8,128)(2,1)}, bf16[32,14336]{1,0:T(8,128)(2,1)S(1)}, u32[]{:S(2)}, u32[]{:S(2)}) %collective-permute-start.2) | collective-permute-done | bytes 917536 | tf_op jit(solution)/shard_map/ppermute | solution.py:317
  48.2 0.4 fusion
  48.6 0.1 copy.8
  48.7 0.2 collective-permute-start.3
  48.9 1.1 %collective-permute-done.3 = f32[32,32]{1,0:T(8,128)S(1)} collective-permute-done((f32[32,32]{1,0:T(8,128)S(1)}, f32[32,32]{1,0:T(8,128)S(1)}, u32[]{:S(2)}, u32[]{:S(2)}) %collective-permute-start.3) | collective-permute-done | bytes 4128 | tf_op jit(solution)/shard_map/ppermute | solution.py:320
  49.9 2.4 %collective-permute-start.4 = (f32[32,32]{1,0:T(8,128)S(1)}, f32[32,32]{1,0:T(8,128)S(1)}, u32[]{:S(2)}, u32[]{:S(2)}) collective-permute-start(f32[32,32]{1,0:T(8,128)S(1)} %add.12), channel_id=1, source_target_pairs={{0,2},{2,0},{4,6},{6,4},{8,10},{10,8},{12,14},{14,12},{1,3},{3,1},... | collective-permute-start | bytes 12296 | tf_op jit(solution)/shard_map/ppermute | solution.py:324
  52.3 1.7 %collective-permute-done.4 = f32[32,32]{1,0:T(8,128)S(1)} collective-permute-done((f32[32,32]{1,0:T(8,128)S(1)}, f32[32,32]{1,0:T(8,128)S(1)}, u32[]{:S(2)}, u32[]{:S(2)}) %collective-permute-start.4) | collective-permute-done | bytes 4128 | tf_op jit(solution)/shard_map/ppermute | solution.py:324
  54.0 3.0 %collective-permute-start.5 = (f32[32,32]{1,0:T(8,128)S(1)}, f32[32,32]{1,0:T(8,128)S(1)}, u32[]{:S(2)}, u32[]{:S(2)}) collective-permute-start(f32[32,32]{1,0:T(8,128)S(1)} %add.13), channel_id=1, source_target_pairs={{0,4},{2,6},{4,0},{6,2},{8,12},{10,14},{12,8},{14,10},{1,5},{3,7},... | collective-permute-start | bytes 12296 | tf_op jit(solution)/shard_map/ppermute | solution.py:324
  57.0 1.7 %collective-permute-done.5 = f32[32,32]{1,0:T(8,128)S(1)} collective-permute-done((f32[32,32]{1,0:T(8,128)S(1)}, f32[32,32]{1,0:T(8,128)S(1)}, u32[]{:S(2)}, u32[]{:S(2)}) %collective-permute-start.5) | collective-permute-done | bytes 4128 | tf_op jit(solution)/shard_map/ppermute | solution.py:324
  58.7 3.0 %collective-permute-start.6 = (f32[32,32]{1,0:T(8,128)S(1)}, f32[32,32]{1,0:T(8,128)S(1)}, u32[]{:S(2)}, u32[]{:S(2)}) collective-permute-start(f32[32,32]{1,0:T(8,128)S(1)} %add.14), channel_id=1, source_target_pairs={{0,8},{2,10},{4,12},{6,14},{8,0},{10,2},{12,4},{14,6},{1,9},{3,11}... | collective-permute-start | bytes 12296 | tf_op jit(solution)/shard_map/ppermute | solution.py:324
  61.8 1.8 %finish.1 = f32[1792,128]{1,0:T(8,128)} custom-call(f32[128,1792]{1,0:T(8,128)S(1)} %get-tuple-element.15.last), custom_call_target="tpu_custom_call" | custom-call | flops 10000000 | bytes 3670016 | tf_op jit(solution)/shard_map/finish/pallas_call | solution.py:329
  63.6 0.0 collective-permute-done.6
  63.6 0.6 add_multiply_fusion
  (4 shorter events, 0.0 us)
Async XLA Ops:
  0.6 1.2 %copy-start = (f32[1,8,16,1792]{3,2,1,0:T(8,128)S(1)}, f32[1,8,16,1792]{3,2,1,0:T(8,128)}, u32[]{:S(2)}) copy-start(f32[1,8,16,1792]{3,2,1,0:T(8,128)} %param.6) | copy-start | bytes 2752516
  1.8 0.9 %copy-start.2 = (f32[16,1792]{1,0:T(8,128)S(1)}, f32[16,1792]{1,0:T(8,128)}, u32[]{:S(2)}) copy-start(f32[16,1792]{1,0:T(8,128)} %along.3) | copy-start | bytes 344068
  2.7 0.9 %copy-start.4 = (f32[16,1792]{1,0:T(8,128)S(1)}, f32[16,1792]{1,0:T(8,128)}, u32[]{:S(2)}) copy-start(f32[16,1792]{1,0:T(8,128)} %across.3) | copy-start | bytes 344068
  3.6 0.9 %copy-start.6 = (f32[16,1792]{1,0:T(8,128)S(1)}, f32[16,1792]{1,0:T(8,128)}, u32[]{:S(2)}) copy-start(f32[16,1792]{1,0:T(8,128)} %viscous.3) | copy-start | bytes 344068
  4.5 0.9 %copy-start.8 = (s32[16,1792]{1,0:T(8,128)S(1)}, s32[16,1792]{1,0:T(8,128)}, u32[]{:S(2)}) copy-start(s32[16,1792]{1,0:T(8,128)} %solid.3) | copy-start | bytes 344068
  5.4 7.9 %copy-start.1 = (f32[1,8,16,1792]{3,2,1,0:T(8,128)S(1)}, f32[1,8,16,1792]{3,2,1,0:T(8,128)}, u32[]{:S(2)}) copy-start(f32[1,8,16,1792]{3,2,1,0:T(8,128)} %param.6) | copy-start | bytes 2752516
  5.4 7.9 %copy-start.3 = (f32[16,1792]{1,0:T(8,128)S(1)}, f32[16,1792]{1,0:T(8,128)}, u32[]{:S(2)}) copy-start(f32[16,1792]{1,0:T(8,128)} %along.3) | copy-start | bytes 344068
  5.4 7.9 %copy-start.5 = (f32[16,1792]{1,0:T(8,128)S(1)}, f32[16,1792]{1,0:T(8,128)}, u32[]{:S(2)}) copy-start(f32[16,1792]{1,0:T(8,128)} %across.3) | copy-start | bytes 344068
  5.4 7.9 %copy-start.7 = (f32[16,1792]{1,0:T(8,128)S(1)}, f32[16,1792]{1,0:T(8,128)}, u32[]{:S(2)}) copy-start(f32[16,1792]{1,0:T(8,128)} %viscous.3) | copy-start | bytes 344068
  5.4 7.9 %copy-start.9 = (s32[16,1792]{1,0:T(8,128)S(1)}, s32[16,1792]{1,0:T(8,128)}, u32[]{:S(2)}) copy-start(s32[16,1792]{1,0:T(8,128)} %solid.3) | copy-start | bytes 344068
  7.1 26.0 %collective-permute-start = (bf16[136,1792]{1,0:T(8,128)(2,1)}, bf16[136,1792]{1,0:T(8,128)(2,1)S(1)}, u32[]{:S(2)}, u32[]{:S(2)}) collective-permute-start(bf16[136,1792]{1,0:T(8,128)(2,1)} %get-tuple-element.13), channel_id=1, source_target_pairs={{0,2},{2,4},{4,6},{6,8},{8,10},{10,12},{12,14},{1,3},{3,5},{5,7},{... | collective-permute-start | bytes 1462280 | tf_op jit(solution)/shard_map/ppermute | solution.py:284
  12.0 21.1 %collective-permute-start.1 = (bf16[136,1792]{1,0:T(8,128)(2,1)S(1)}, bf16[136,1792]{1,0:T(8,128)(2,1)S(1)}, u32[]{:S(2)}, u32[]{:S(2)}) collective-permute-start(bf16[136,1792]{1,0:T(8,128)(2,1)S(1)} %get-tuple-element.14), channel_id=1, source_target_pairs={{2,0},{4,2},{6,4},{8,6},{10,8},{12,10},{14,12},{3,1},{5,3},{7,5},{... | collective-permute-start | bytes 1462280 | tf_op jit(solution)/shard_map/ppermute | solution.py:285
  13.3 0.9 %copy-start.10 = (f32[16,1792]{1,0:T(8,128)S(1)}, f32[16,1792]{1,0:T(8,128)}, u32[]{:S(2)}) copy-start(f32[16,1792]{1,0:T(8,128)} %area.1) | copy-start | bytes 344068
  45.5 2.7 %collective-permute-start.2 = (bf16[32,14336]{1,0:T(8,128)(2,1)}, bf16[32,14336]{1,0:T(8,128)(2,1)S(1)}, u32[]{:S(2)}, u32[]{:S(2)}) collective-permute-start(bf16[32,14336]{1,0:T(8,128)(2,1)} %get-tuple-element.17), channel_id=1, source_target_pairs={{0,1},{1,0},{2,3},{3,2},{4,5},{5,4},{6,7},{7,6},{8,9},{9,8},{10,11... | collective-permute-start | bytes 2752520 | tf_op jit(solution)/shard_map/ppermute | solution.py:317
  48.7 1.2 %collective-permute-start.3 = (f32[32,32]{1,0:T(8,128)S(1)}, f32[32,32]{1,0:T(8,128)S(1)}, u32[]{:S(2)}, u32[]{:S(2)}) collective-permute-start(f32[32,32]{1,0:T(8,128)S(1)} %bitcast_select_fusion), channel_id=1, source_target_pairs={{0,1},{1,0},{2,3},{3,2},{4,5},{5,4},{6,7},{7,6},{8,9},{9,8},{10,11... | collective-permute-start | bytes 12296 | tf_op jit(solution)/shard_map/ppermute | solution.py:320
  49.9 4.1 %collective-permute-start.4 = (f32[32,32]{1,0:T(8,128)S(1)}, f32[32,32]{1,0:T(8,128)S(1)}, u32[]{:S(2)}, u32[]{:S(2)}) collective-permute-start(f32[32,32]{1,0:T(8,128)S(1)} %add.12), channel_id=1, source_target_pairs={{0,2},{2,0},{4,6},{6,4},{8,10},{10,8},{12,14},{14,12},{1,3},{3,1},... | collective-permute-start | bytes 12296 | tf_op jit(solution)/shard_map/ppermute | solution.py:324
  54.0 4.7 %collective-permute-start.5 = (f32[32,32]{1,0:T(8,128)S(1)}, f32[32,32]{1,0:T(8,128)S(1)}, u32[]{:S(2)}, u32[]{:S(2)}) collective-permute-start(f32[32,32]{1,0:T(8,128)S(1)} %add.13), channel_id=1, source_target_pairs={{0,4},{2,6},{4,0},{6,2},{8,12},{10,14},{12,8},{14,10},{1,5},{3,7},... | collective-permute-start | bytes 12296 | tf_op jit(solution)/shard_map/ppermute | solution.py:324
  58.7 4.9 %collective-permute-start.6 = (f32[32,32]{1,0:T(8,128)S(1)}, f32[32,32]{1,0:T(8,128)S(1)}, u32[]{:S(2)}, u32[]{:S(2)}) collective-permute-start(f32[32,32]{1,0:T(8,128)S(1)} %add.14), channel_id=1, source_target_pairs={{0,8},{2,10},{4,12},{6,14},{8,0},{10,2},{12,4},{14,6},{1,9},{3,11}... | collective-permute-start | bytes 12296 | tf_op jit(solution)/shard_map/ppermute | solution.py:324

commit v4 on v3

--- a/solution.py
+++ b/solution.py
@@ -7,6 +7,7 @@
 from jax.experimental import pallas as pl
 from jax.experimental.pallas import tpu as pltpu
 from jax.sharding import PartitionSpec as P
+
 
 NSNAP = 4
 STRIDE = 3
@@ -76,7 +77,7 @@
     return pltpu.roll(jnp.where(lane == LANES - 1, before, tiles[tile + 1]), 1, 1)
 
 
-def weights_of(along, across, signed, is_adjoint):
+def weights_of(along, across, signed, is_adjoint, first_col=True, last_col=True):
     lane = lax.broadcasted_iota(jnp.int32, along[0].shape, 1)
     count = len(along)
     east, west, north, south, centre = [], [], [], [], []
@@ -92,23 +93,47 @@
         centre.append(opened * (1.0 - 4.0 * spread))
     east_w = [jnp.where(is_adjoint, eastern(west, t, lane, count), east[t]) for t in range(count)]
     west_w = [jnp.where(is_adjoint, western(east, t, lane, count), west[t]) for t in range(count)]
-    east_w[-1] = jnp.where(lane == LANES - 1, 0.0, east_w[-1])
-    west_w[0] = jnp.where(lane == 0, 0.0, west_w[0])
+    if last_col:
+        east_w[-1] = jnp.where(lane == LANES - 1, 0.0, east_w[-1])
+    if first_col:
+        west_w[0] = jnp.where(lane == 0, 0.0, west_w[0])
     return east_w, west_w, north, south, centre
 
 
-def pack_kernel(rows, inputs, field, along, across, viscous, solid, up, down, coefs):
+def pack_kernel(
+    rows, inputs, cuts, field_in, along_in, across_in, viscous_in, solid_in, *refs
+):
+    outs, (coefs, field, along, across, viscous, solid, sems) = refs[:-7], refs[-7:]
     cols = along.shape[1]
+    copies = [
+        pltpu.make_async_copy(source, target, sems.at[index])
+        for index, (source, target) in enumerate(
+            (
+                (field_in, field),
+                (along_in, along),
+                (across_in, across),
+                (viscous_in, viscous),
+                (solid_in, solid),
+            )
+        )
+    ]
+    for copy in copies:
+        copy.start()
+    for copy in copies:
+        copy.wait()
     signed = jnp.where(solid[...] != 0, -viscous[...], viscous[...])
-    for out, first in ((up, rows - HALO), (down, 0)):
-        for step in range(HALO):
-            for tile in range(cols // LANES):
-                part = field[tile_of(rows, cols, first + step, tile, inputs), :]
-                out[step * inputs : (step + 1) * inputs, lanes_of(tile)] = part.astype(out.dtype)
+    for side, first in enumerate((rows - HALO, 0)):
         coefs[0:HALO, :] = along[first : first + HALO, :]
         coefs[HALO : 2 * HALO, :] = across[first : first + HALO, :]
         coefs[2 * HALO : 3 * HALO, :] = signed[first : first + HALO]
-        out[HALO * inputs :, :] = coefs[...].astype(out.dtype)
+        for chunk, (left, right) in enumerate(cuts):
+            out = outs[2 * chunk + side]
+            for step in range(HALO):
+                for tile in range(left // LANES, right // LANES):
+                    part = field[tile_of(rows, cols, first + step, tile, inputs), :]
+                    to = lanes_of(tile - left // LANES)
+                    out[step * inputs : (step + 1) * inputs, to] = part.astype(out.dtype)
+            out[HALO * inputs :, :] = coefs[:, left:right].astype(out.dtype)
 
 
 def prepare_kernel(
@@ -140,40 +165,47 @@
             weights[index, tile * rows : (tile + 1) * rows, :] = values
 
 
-def march_kernel(
-    rows, inputs, adjoint_ref, own, own_weights, scale, low, high,
-    final, kept, sent,
-    state_a, state_b, coefs, east_w, west_w, north_w, south_w, centre_w,
-):
+def march_kernel(rows, inputs, first_pair, last_pair, sources, owned, all_pairs, adjoint_ref, own, own_weights, scale, *refs):
+    count = 2 * (1 + max(operand for operand, _ in sources))
+    halos, refs = refs[:count], refs[count:]
+    if last_pair < all_pairs:
+        for side in range(2):
+            refs[3][side] = halos[side][:, (last_pair - 1 - first_pair) * PAIR :]
+        refs = (*refs[:3], *refs[4:])
+    last, kept, sent, state_a, state_b, coefs, east_w, west_w, north_w, south_w, centre_w = refs
     adjoint = adjoint_ref[0]
     is_adjoint = adjoint == 1
-    cols = own.shape[1]
-    half = cols // 2
+    tiles = 2 * (last_pair - first_pair)
+    tile0 = 2 * first_pair
     span = rows + 2 * HALO
     wide = span + 2 * SUB
-    tiles = cols // LANES
     matrix = sorting_matrix()
     all_weights = (east_w, west_w, north_w, south_w, centre_w)
-
-    for source, first in ((low, 0), (high, HALO + rows)):
+    edges = (first_pair == 0, last_pair == all_pairs)
+
+    for side, first in ((0, 0), (1, HALO + rows)):
         sorted_coefs = [[], [], []]
-        for pair in range(cols // PAIR):
+        for pair, (operand, place) in enumerate(sources):
             at = slice(pair * PAIR, (pair + 1) * PAIR)
-            values = moved(source[:, at], matrix)
+            source = halos[2 * operand + side]
+            values = moved(source[:, place * PAIR : (place + 1) * PAIR], matrix)
             state_a[(1 + first) * inputs : (1 + first + HALO) * inputs, at] = values[: HALO * inputs]
             coefs[:, at] = values[HALO * inputs :]
             for index, taken in enumerate(sorted_coefs):
                 part = coefs[index * HALO : (index + 1) * HALO, at]
                 taken += [part[:, :LANES], part[:, LANES:]]
-        for ref, values in zip(all_weights, weights_of(*sorted_coefs, is_adjoint)):
+        for ref, values in zip(all_weights, weights_of(*sorted_coefs, is_adjoint, *edges)):
             for tile in range(tiles):
                 start = tile * wide + SUB + first
                 ref[start : start + HALO, :] = values[tile]
-    state_a[(1 + HALO) * inputs : (1 + HALO + rows) * inputs, :] = own[...]
+    state_a[(1 + HALO) * inputs : (1 + HALO + rows) * inputs, :] = own[
+        :, tile0 * LANES : (tile0 + tiles) * LANES
+    ]
     for index, ref in enumerate(all_weights):
         for tile in range(tiles):
             start = tile * wide + SUB + HALO
-            ref[start : start + rows, :] = own_weights[index, tile * rows : (tile + 1) * rows, :]
+            at = slice((tile0 + tile) * rows, (tile0 + tile + 1) * rows)
+            ref[start : start + rows, :] = own_weights[index, at, :]
 
     states = (state_a, state_b)
     lane = lax.broadcasted_iota(jnp.int32, (inputs, LANES), 1)
@@ -222,9 +254,19 @@
                     for tile in range(tiles):
                         value = dst[at, lanes_of(tile)]
                         if scaled:
-                            value = value * scale[pl.ds(tile * rows + row, inputs, stride=0), :]
+                            factor = pl.ds((tile0 + tile) * rows + row, inputs, stride=0)
+                            value = value * scale[factor, :]
+                        low_lane, high_lane = 0, LANES
+                        if tile < 2:
+                            low_lane = owned[0]
+                        if tile >= tiles - 2:
+                            high_lane = owned[1]
+                        if low_lane > 0:
+                            value = jnp.where(lane >= low_lane, value, 0.0)
+                        if high_lane < LANES:
+                            value = jnp.where(lane < high_lane, value, 0.0)
                         out = first if tile < tiles // 2 else second
-                        start = row * half + tile % (tiles // 2) * LANES
+                        start = (row * (tiles // 2) + tile % (tiles // 2)) * LANES
                         out[snap, start : start + LANES] = value.astype(out.dtype)
 
             @pl.when(is_adjoint)
@@ -235,17 +277,38 @@
             def _():
                 record(kept, sent, False)
 
-    final[...] = states[HALO % 2][(1 + HALO) * inputs : (1 + HALO + rows) * inputs, :]
-
-
-def finish_kernel(rows, inputs, last, final):
-    cols = last.shape[1]
+    last[...] = states[HALO % 2][(1 + HALO) * inputs : (1 + HALO + rows) * inputs, :]
+
+
+def meet_kernel(adjoint_ref, mine_a, other_a, mine_b, other_b, product):
+    def met(rows, columns):
+        return lax.dot_general(
+            rows[...], columns[...], (((1,), (1,)), ((), ())), preferred_element_type=F32
+        )
+
+    @pl.when(adjoint_ref[0] == 0)
+    def _():
+        product[...] = met(other_a, mine_a) + met(other_b, mine_b)
+
+    @pl.when(adjoint_ref[0] != 0)
+    def _():
+        product[...] = met(mine_a, other_a) + met(mine_b, other_b)
+
+
+def finish_kernel(rows, inputs, shared, left, right, final):
     matrix = sorting_matrix(back=True)
-    for pair in range(cols // PAIR):
-        values = moved_whole(last[:, pair * PAIR : (pair + 1) * PAIR], matrix)
+    lane = lax.broadcasted_iota(jnp.int32, (rows * inputs, PAIR), 1)
+    pairs = shared + right.shape[1] // PAIR
+    for pair in range(pairs):
+        if pair <= shared:
+            values = left[:, pair * PAIR : (pair + 1) * PAIR]
+        if pair >= shared:
+            others = right[:, (pair - shared) * PAIR : (pair - shared + 1) * PAIR]
+            values = jnp.where(lane % LANES < LANES // 2, values, others) if pair == shared else others
+        values = moved_whole(values, matrix)
         for row in range(rows):
             for side in range(2):
-                final[tile_of(rows, cols, row, 2 * pair + side, inputs), :] = values[
+                final[tile_of(rows, pairs * PAIR, row, 2 * pair + side, inputs), :] = values[
                     row * inputs : (row + 1) * inputs, lanes_of(side)
                 ]
 
@@ -258,7 +321,6 @@
     coef_rows = up8(3 * HALO)
     packed_rows = HALO * inputs + coef_rows
     span = rows + 2 * HALO
-    half = cols // 2
     tiles = cols // LANES
     vmem = pl.BlockSpec(memory_space=pltpu.VMEM)
     smem = pl.BlockSpec(memory_space=pltpu.SMEM)
@@ -269,22 +331,40 @@
     def cost(amount):
         return pl.CostEstimate(flops=amount, bytes_accessed=4 * field.size * 4, transcendentals=0)
 
-    params = pltpu.CompilerParams(vmem_limit_bytes=24 << 20)
-    packed = shape(packed_rows, cols, dtype=BF16)
-    up, down = pl.pallas_call(
-        functools.partial(pack_kernel, rows, inputs),
-        out_shape=(packed, packed),
-        in_specs=[vmem] * 5,
-        out_specs=(vmem, vmem),
-        scratch_shapes=[pltpu.VMEM((coef_rows, cols), F32)],
+    params = pltpu.CompilerParams(vmem_limit_bytes=14 << 20)
+    hbm = pl.BlockSpec(memory_space=pltpu.HBM)
+    pairs = cols // PAIR
+    shared = pairs // 2
+    cut = (shared + 1) * PAIR
+    cuts = ((0, cut), (cut, cols))
+    packed = [
+        shape(packed_rows, right - left, dtype=BF16) for left, right in cuts for _ in range(2)
+    ]
+    plane = pltpu.VMEM((rows, cols), F32)
+    up_a, down_a, up_b, down_b = pl.pallas_call(
+        functools.partial(pack_kernel, rows, inputs, cuts),
+        out_shape=packed,
+        in_specs=[hbm] * 5,
+        out_specs=[vmem] * 4,
+        scratch_shapes=[
+            pltpu.VMEM((coef_rows, cols), F32),
+            pltpu.VMEM(field.shape, F32),
+            plane,
+            plane,
+            plane,
+            pltpu.VMEM((rows, cols), jnp.int32),
+            pltpu.SemaphoreType.DMA((5,)),
+        ],
         compiler_params=params,
         name="pack",
-    )(field, streamwise, crossflow, diffusivity, obstacle)
+    )(*[pltpu.with_memory_space_constraint(x, pltpu.HBM) for x in (field, streamwise, crossflow, diffusivity, obstacle)])
     size = lax.axis_size("rows")
-    low = lax.ppermute(up, "rows", [(i, i + 1) for i in range(size - 1)])
-    high = lax.ppermute(down, "rows", [(i + 1, i) for i in range(size - 1)])
-
-    own, own_weights, scale = pl.pallas_call(
+    rise = [(i, i + 1) for i in range(size - 1)]
+    fall = [(j, i) for i, j in rise]
+    low_a, high_a = lax.ppermute(up_a, "rows", rise), lax.ppermute(down_a, "rows", fall)
+    low_b, high_b = lax.ppermute(up_b, "rows", rise), lax.ppermute(down_b, "rows", fall)
+
+    prepare = pl.pallas_call(
         functools.partial(prepare_kernel, rows, inputs),
         out_shape=(
             shape(rows * inputs, cols),
@@ -297,27 +377,57 @@
         compiler_params=params,
         cost_estimate=cost(10**9),
         name="prepare",
-    )(flag, field, streamwise, crossflow, diffusivity, obstacle, cell_weight)
-
-    snaps = shape(NSNAP * inputs, rows * half, dtype=BF16)
-    last, kept, sent = pl.pallas_call(
-        functools.partial(march_kernel, rows, inputs),
-        out_shape=(shape(rows * inputs, cols), snaps, snaps),
-        in_specs=[smem] + [vmem] * 5,
-        out_specs=(vmem,) * 3,
-        scratch_shapes=[
-            *[pltpu.VMEM(((span + 2) * inputs, cols), F32)] * 2,
-            pltpu.VMEM((coef_rows, cols), F32),
-            *[pltpu.VMEM((tiles * (span + 2 * SUB), LANES), F32)] * 5,
-        ],
+    )
+    own, own_weights, scale = prepare(
+        flag, field, streamwise, crossflow, diffusivity, obstacle, cell_weight
+    )
+
+    def march(first_pair, last_pair, sources, owned, halos):
+        more = [shape(2, packed_rows, PAIR, dtype=BF16)] * (last_pair < pairs)
+        chunk = (last_pair - first_pair) * PAIR
+        return pl.pallas_call(
+            functools.partial(
+                march_kernel, rows, inputs, first_pair, last_pair, sources, owned, pairs
+            ),
+            out_shape=(
+                shape(rows * inputs, chunk),
+                *[shape(NSNAP * inputs, rows * chunk // 2, dtype=BF16)] * 2,
+                *more,
+            ),
+            in_specs=[smem] + [vmem] * (3 + len(halos)),
+            out_specs=(vmem,) * (3 + len(more)),
+            scratch_shapes=[
+                *[pltpu.VMEM(((span + 2) * inputs, chunk), F32)] * 2,
+                pltpu.VMEM((coef_rows, chunk), F32),
+                *[pltpu.VMEM((chunk // LANES * (span + 2 * SUB), LANES), F32)] * 5,
+            ],
+            compiler_params=params,
+            cost_estimate=cost(10**9),
+        )(flag, own, own_weights, scale, *halos)
+
+    middle = LANES // 2
+    last_a, kept_a, sent_a, both = march(
+        0, shared + 1, [(0, p) for p in range(shared + 1)], (0, middle), (low_a, high_a)
+    )
+    last_b, kept_b, sent_b = march(
+        shared,
+        pairs,
+        [(0, 0)] + [(1, p) for p in range(pairs - shared - 1)],
+        (middle, LANES),
+        (both[0], both[1], low_b, high_b),
+    )
+    swap = [(0, 1), (1, 0)]
+    other_a = lax.ppermute(sent_a, "fa", swap)
+    other_b = lax.ppermute(sent_b, "fa", swap)
+    total = pl.pallas_call(
+        meet_kernel,
+        out_shape=shape(NSNAP * inputs, NSNAP * inputs),
+        in_specs=[smem] + [vmem] * 4,
+        out_specs=vmem,
         compiler_params=params,
-        name="march",
-    )(flag, own, own_weights, scale, low, high)
-
-    other = lax.ppermute(sent, "fa", [(0, 1), (1, 0)])
-    product = lax.dot_general(kept, other, (((1,), (1,)), ((), ())), preferred_element_type=F32)
-    total = jnp.where(adjoint == 1, product, product.T)
-    total = total + lax.ppermute(total, "fa", [(0, 1), (1, 0)])
+        name="meet",
+    )(flag, kept_a, other_a, kept_b, other_b)
+    total = total + lax.ppermute(total, "fa", swap)
     if size & (size - 1) == 0:
         stride = 1
         while stride < size:
@@ -327,14 +437,14 @@
         total = lax.psum(total, "rows")
     hankel = total * (1.0 / math.sqrt(rows * size * cols))
     final = pl.pallas_call(
-        functools.partial(finish_kernel, rows, inputs),
+        functools.partial(finish_kernel, rows, inputs, shared),
         out_shape=shape(*field.shape),
-        in_specs=[vmem],
+        in_specs=[vmem] * 2,
         out_specs=vmem,
         compiler_params=params,
         cost_estimate=cost(10**7),
         name="finish",
-    )(last)
+    )(last_a, last_b)
     return (untiled(final, init_fields.shape[1:])[None], hankel)
 
 
@@ -347,6 +457,7 @@
         P("rows", None),
         P("rows", None),
     )
+
     return jax.shard_map(
         local,
         mesh=mesh,

time: 64.5 us -> 57.2 us (0.89)
  waiting for transfers between devices: 23.9 us -> 13.9 us
  starting transfers between devices: 14.8 us -> 20.2 us
  local copies, waits for them, and re-layouts: 5.76 us -> 0.93 us
  Pallas kernels: 18 us -> 20.5 us
    ppermute x4 -> x7, waiting for transfers between devices: 20.4 us -> 10.4 us  [the longest x1 7.2 us: local(): lax.ppermute(up_a, 'rows', rise)]
    ppermute x4 -> x7, starting transfers between devices: 6.37 us -> 12.8 us  [the longest x1 4.89 us: local(): lax.ppermute(up_a, 'rows', rise)]
    unnamed x22 -> x12, local copies, waits for them, and re-layouts: 5.68 us -> 0.91 us
    pallas_call x4 -> x6, Pallas kernels: 18 us -> 20.5 us  [the longest x2 13.9 us: march(): pl.pallas_call(functools.partial(march_kernel, rows, inputs, first_pair,...]
    ppermute x3, starting transfers between devices: 8.42 us -> 7.44 us  [local(): lax.ppermute(total, 'rows', [(i, i ^ stride) for i in range(size)])]
  transfers between devices with their start and end apart: 7 -> 10, of which waited for: 5 -> 6; matrix products, arithmetic and copies ran while one was open for 0% -> 0% of each run, Pallas kernels for 6% -> 19%
where the time goes in v4:
time: 57.2 us; the launch traced here: 57 us
  Pallas kernels  20.5 us (36%)
  starting transfers between devices  20.2 us (35%)
  waiting for transfers between devices  13.9 us (24%)
  local copies, waits for them, and re-layouts  0.93 us (2%)
  between operations  0.83 us (1%)
  other arithmetic  0.62 us (1%)
    pallas_call x2, Pallas kernels, march(): pl.pallas_call(functools.partial(march_kernel, rows, inputs, first_pair,...  13.9 us
    ppermute x3, starting transfers between devices, local(): lax.ppermute(total, 'rows', [(i, i ^ stride) for i in range(size)])  7.44 us
    ppermute x1, waiting for transfers between devices, local(): lax.ppermute(up_a, 'rows', rise)  7.2 us
    ppermute x1, starting transfers between devices, local(): lax.ppermute(up_a, 'rows', rise)  4.89 us
    ppermute x1, starting transfers between devices, local(): lax.ppermute(up_b, 'rows', rise)  4.56 us
    ppermute x3, waiting for transfers between devices, local(): lax.ppermute(total, 'rows', [(i, i ^ stride) for i in range(size)])  3.49 us
    pallas_call x1, Pallas kernels, local(): pl.pallas_call(functools.partial(pack_kernel, rows, inputs, cuts), out_sh...  2.3 us
    pallas_call x1, Pallas kernels, local(): prepare(flag, field, streamwise, crossflow, diffusivity, obstacle, cell_w...  2.13 us
  transfers between devices with their start and end apart: 10, of which 6 were waited for; matrix products, arithmetic and copies ran while one was open for 0% of the time, Pallas kernels for 19%

profile of v4, /device:TPU:0, one launch (start us, length us, event | category | flops | bytes accessed | tf_op | source)
XLA Modules:
  0.0 57.0 jit_solution(9685756000835730496)
XLA Ops:
  0.6 0.0 copy-start
  0.6 0.0 copy-start.1
  0.7 0.0 copy-start.2
  0.7 0.0 copy-start.3
  0.7 0.0 copy-start.4
  0.7 2.3 %pack.1 = (bf16[136,1024]{1,0:T(8,128)(2,1)S(1)}, bf16[136,1024]{1,0:T(8,128)(2,1)S(1)}, bf16[136,768]{1,0:T(8,128)(2,1)S(1)}, bf16[136,768]{1,0:T(8,128)(2,1)S(1)}) custom-call(f32[1792,128]{1,0:T(8,128)} %bitcast.15, f32[16,1792]{1,0:T(8,128)} %along_in.1, f32[16,1792]{1,0:T(8,128)} %across_in.1, f32[16,1792]{1,0:T(8,128)} %viscous_in.1, s32[16,1792]{1,0:T(8,128)} %solid_in.1), custom_call_target="tpu_custom_call" | custom-call | tf_op jit(solution)/shard_map/pack/pallas_call | solution.py:344
  3.0 4.9 %collective-permute-start = (bf16[136,1024]{1,0:T(8,128)(2,1)S(1)}, bf16[136,1024]{1,0:T(8,128)(2,1)S(1)}, u32[]{:S(2)}, u32[]{:S(2)}) collective-permute-start(bf16[136,1024]{1,0:T(8,128)(2,1)S(1)} %get-tuple-element.19), channel_id=1, source_target_pairs={{0,2},{2,4},{4,6},{6,8},{8,10},{10,12},{12,14},{1,3},{3,5},{5,7},{... | collective-permute-start | bytes 835592 | tf_op jit(solution)/shard_map/ppermute | solution.py:364
  7.9 1.3 %collective-permute-start.1 = (bf16[136,1024]{1,0:T(8,128)(2,1)S(1)}, bf16[136,1024]{1,0:T(8,128)(2,1)S(1)}, u32[]{:S(2)}, u32[]{:S(2)}) collective-permute-start(bf16[136,1024]{1,0:T(8,128)(2,1)S(1)} %get-tuple-element.20), channel_id=1, source_target_pairs={{2,0},{4,2},{6,4},{8,6},{10,8},{12,10},{14,12},{3,1},{5,3},{7,5},{... | collective-permute-start | bytes 835592 | tf_op jit(solution)/shard_map/ppermute | solution.py:364
  9.2 4.6 %collective-permute-start.2 = (bf16[136,768]{1,0:T(8,128)(2,1)S(1)}, bf16[136,768]{1,0:T(8,128)(2,1)S(1)}, u32[]{:S(2)}, u32[]{:S(2)}) collective-permute-start(bf16[136,768]{1,0:T(8,128)(2,1)S(1)} %get-tuple-element.23), channel_id=1, source_target_pairs={{0,2},{2,4},{4,6},{6,8},{8,10},{10,12},{12,14},{1,3},{3,5},{5,7},{... | collective-permute-start | bytes 626696 | tf_op jit(solution)/shard_map/ppermute | solution.py:365
  13.8 1.3 %collective-permute-start.3 = (bf16[136,768]{1,0:T(8,128)(2,1)S(1)}, bf16[136,768]{1,0:T(8,128)(2,1)S(1)}, u32[]{:S(2)}, u32[]{:S(2)}) collective-permute-start(bf16[136,768]{1,0:T(8,128)(2,1)S(1)} %get-tuple-element.24), channel_id=1, source_target_pairs={{2,0},{4,2},{6,4},{8,6},{10,8},{12,10},{14,12},{3,1},{5,3},{7,5},{... | collective-permute-start | bytes 626696 | tf_op jit(solution)/shard_map/ppermute | solution.py:365
  15.1 0.0 copy-done
  15.1 0.0 copy-done.1
  15.1 0.0 copy-done.2
  15.1 0.0 copy-done.3
  15.1 0.0 copy-done.4
  15.1 0.0 copy-start.5
  15.1 0.9 %copy-done.5 = f32[16,1792]{1,0:T(8,128)S(1)} copy-done((f32[16,1792]{1,0:T(8,128)S(1)}, f32[16,1792]{1,0:T(8,128)}, u32[]{:S(2)}) %copy-start.5) | copy-done | bytes 114712
  16.0 2.1 %prepare.1 = (f32[128,1792]{1,0:T(8,128)S(1)}, f32[5,224,128]{2,1,0:T(8,128)S(1)}, f32[224,128]{1,0:T(8,128)S(1)}) custom-call(s32[1]{0:T(128)} %bitcast.adjoint_ref, f32[1792,128]{1,0:T(8,128)S(1)} %bitcast.16, f32[16,1792]{1,0:T(8,128)S(1)} %copy-done.1, f32[16,1792]{1,0:T(8,128)S(1)} %copy-done.2, f32[16,1792]{1,0:T(8,128)S(1)} %copy-done.3, ...), custom_call_target="tpu_custom_call" | custom-call | flops 1000000000 | bytes 3670016 | tf_op jit(solution)/shard_map/prepare/pallas_call | solution.py:381
  18.1 7.2 %collective-permute-done.refs_0_ = bf16[136,1024]{1,0:T(8,128)(2,1)S(1)} collective-permute-done((bf16[136,1024]{1,0:T(8,128)(2,1)S(1)}, bf16[136,1024]{1,0:T(8,128)(2,1)S(1)}, u32[]{:S(2)}, u32[]{:S(2)}) %collective-permute-start) | collective-permute-done | bytes 278560 | tf_op jit(solution)/shard_map/ppermute | solution.py:364
  25.3 0.0 collective-permute-done.1.refs_1_
  25.3 6.9 %shard_map.77 = (f32[128,1024]{1,0:T(8,128)S(1)}, bf16[32,8192]{1,0:T(8,128)(2,1)S(1)}, bf16[32,8192]{1,0:T(8,128)(2,1)S(1)}, bf16[2,136,256]{2,1,0:T(8,128)(2,1)S(1)}) custom-call(s32[1]{0:T(128)} %bitcast.adjoint_ref, f32[128,1792]{1,0:T(8,128)S(1)} %get-tuple-element.16.own, f32[5,224,128]{2,1,0:T(8,128)S(1)} %get-tuple-element.17.own_weights, ...), custom_call_target="tpu_custom_call" | custom-call | flops 1000000000 | bytes 3670016 | tf_op jit(solution)/shard_map/pallas_call | solution.py:388
  32.3 0.0 collective-permute-done.2.refs_2_
  32.3 0.0 collective-permute-done.3.refs_3_
  32.3 6.9 %shard_map.78 = (f32[128,1024]{1,0:T(8,128)S(1)}, bf16[32,8192]{1,0:T(8,128)(2,1)S(1)}, bf16[32,8192]{1,0:T(8,128)(2,1)S(1)}) custom-call(s32[1]{0:T(128)} %bitcast.adjoint_ref, f32[128,1792]{1,0:T(8,128)S(1)} %get-tuple-element.16.own, f32[5,224,128]{2,1,0:T(8,128)S(1)} %get-tuple-element.17.own_weights, f32[224,128]{1,0:T(8,128)S(1)} %get-tuple-element.18.scale, ...), custom_call_target="tpu_custom_call" | custom-call | flops 1000000000 | bytes 3670016 | tf_op jit(solution)/shard_map/pallas_call | solution.py:388
  39.3 0.1 collective-permute-start.5
  39.4 0.5 collective-permute-start.4
  39.9 1.4 %collective-permute-done.5.other_b = bf16[32,8192]{1,0:T(8,128)(2,1)S(1)} collective-permute-done((bf16[32,8192]{1,0:T(8,128)(2,1)S(1)}, bf16[32,8192]{1,0:T(8,128)(2,1)S(1)}, u32[]{:S(2)}, u32[]{:S(2)}) %collective-permute-start.5) | collective-permute-done | bytes 524320 | tf_op jit(solution)/shard_map/ppermute | solution.py:421
  41.3 0.7 %collective-permute-done.4.other_a = bf16[32,8192]{1,0:T(8,128)(2,1)S(1)} collective-permute-done((bf16[32,8192]{1,0:T(8,128)(2,1)S(1)}, bf16[32,8192]{1,0:T(8,128)(2,1)S(1)}, u32[]{:S(2)}, u32[]{:S(2)}) %collective-permute-start.4) | collective-permute-done | bytes 524320 | tf_op jit(solution)/shard_map/ppermute | solution.py:420
  42.0 0.4 meet.1
  42.4 0.2 collective-permute-start.6
  42.6 1.0 %collective-permute-done.6 = f32[32,32]{1,0:T(8,128)S(1)} collective-permute-done((f32[32,32]{1,0:T(8,128)S(1)}, f32[32,32]{1,0:T(8,128)S(1)}, u32[]{:S(2)}, u32[]{:S(2)}) %collective-permute-start.6) | collective-permute-done | bytes 4128 | tf_op jit(solution)/shard_map/ppermute | solution.py:430
  43.6 2.5 %collective-permute-start.7 = (f32[32,32]{1,0:T(8,128)S(1)}, f32[32,32]{1,0:T(8,128)S(1)}, u32[]{:S(2)}, u32[]{:S(2)}) collective-permute-start(f32[32,32]{1,0:T(8,128)S(1)} %add.12), channel_id=1, source_target_pairs={{0,2},{2,0},{4,6},{6,4},{8,10},{10,8},{12,14},{14,12},{1,3},{3,1},... | collective-permute-start | bytes 12296 | tf_op jit(solution)/shard_map/ppermute | solution.py:434
  46.1 1.7 %collective-permute-done.7 = f32[32,32]{1,0:T(8,128)S(1)} collective-permute-done((f32[32,32]{1,0:T(8,128)S(1)}, f32[32,32]{1,0:T(8,128)S(1)}, u32[]{:S(2)}, u32[]{:S(2)}) %collective-permute-start.7) | collective-permute-done | bytes 4128 | tf_op jit(solution)/shard_map/ppermute | solution.py:434
  47.8 2.0 %collective-permute-start.8 = (f32[32,32]{1,0:T(8,128)S(1)}, f32[32,32]{1,0:T(8,128)S(1)}, u32[]{:S(2)}, u32[]{:S(2)}) collective-permute-start(f32[32,32]{1,0:T(8,128)S(1)} %add.13), channel_id=1, source_target_pairs={{0,4},{2,6},{4,0},{6,2},{8,12},{10,14},{12,8},{14,10},{1,5},{3,7},... | collective-permute-start | bytes 12296 | tf_op jit(solution)/shard_map/ppermute | solution.py:434
  49.8 1.8 %collective-permute-done.8 = f32[32,32]{1,0:T(8,128)S(1)} collective-permute-done((f32[32,32]{1,0:T(8,128)S(1)}, f32[32,32]{1,0:T(8,128)S(1)}, u32[]{:S(2)}, u32[]{:S(2)}) %collective-permute-start.8) | collective-permute-done | bytes 4128 | tf_op jit(solution)/shard_map/ppermute | solution.py:434
  51.6 3.0 %collective-permute-start.9 = (f32[32,32]{1,0:T(8,128)S(1)}, f32[32,32]{1,0:T(8,128)S(1)}, u32[]{:S(2)}, u32[]{:S(2)}) collective-permute-start(f32[32,32]{1,0:T(8,128)S(1)} %add.14), channel_id=1, source_target_pairs={{0,8},{2,10},{4,12},{6,14},{8,0},{10,2},{12,4},{14,6},{1,9},{3,11}... | collective-permute-start | bytes 12296 | tf_op jit(solution)/shard_map/ppermute | solution.py:434
  54.6 1.8 %finish.1 = f32[1792,128]{1,0:T(8,128)} custom-call(f32[128,1024]{1,0:T(8,128)S(1)} %get-tuple-element.21.left, f32[128,1024]{1,0:T(8,128)S(1)} %get-tuple-element.25.right), custom_call_target="tpu_custom_call" | custom-call | flops 10000000 | bytes 3670016 | tf_op jit(solution)/shard_map/finish/pallas_call | solution.py:439
  56.4 0.0 collective-permute-done.9
  56.4 0.6 %add_multiply_fusion = f32[32,32]{1,0:T(8,128)} fusion(f32[32,32]{1,0:T(8,128)S(1)} %add.14, f32[32,32]{1,0:T(8,128)S(1)} %collective-permute-done.9), kind=kLoop, calls=%fused_computation.2 | loop fusion | flops 2048 | bytes 12288 | tf_op jit(solution)/shard_map/mul | solution.py:438
  (4 shorter events, 0.0 us)
Async XLA Ops:
  0.6 14.4 %copy-start = (f32[1,8,16,1792]{3,2,1,0:T(8,128)S(1)}, f32[1,8,16,1792]{3,2,1,0:T(8,128)}, u32[]{:S(2)}) copy-start(f32[1,8,16,1792]{3,2,1,0:T(8,128)} %param.6) | copy-start | bytes 2752516
  0.6 14.4 %copy-start.1 = (f32[16,1792]{1,0:T(8,128)S(1)}, f32[16,1792]{1,0:T(8,128)}, u32[]{:S(2)}) copy-start(f32[16,1792]{1,0:T(8,128)} %along_in.1) | copy-start | bytes 344068
  0.7 14.4 %copy-start.2 = (f32[16,1792]{1,0:T(8,128)S(1)}, f32[16,1792]{1,0:T(8,128)}, u32[]{:S(2)}) copy-start(f32[16,1792]{1,0:T(8,128)} %across_in.1) | copy-start | bytes 344068
  0.7 14.4 %copy-start.3 = (f32[16,1792]{1,0:T(8,128)S(1)}, f32[16,1792]{1,0:T(8,128)}, u32[]{:S(2)}) copy-start(f32[16,1792]{1,0:T(8,128)} %viscous_in.1) | copy-start | bytes 344068
  0.7 14.4 %copy-start.4 = (s32[16,1792]{1,0:T(8,128)S(1)}, s32[16,1792]{1,0:T(8,128)}, u32[]{:S(2)}) copy-start(s32[16,1792]{1,0:T(8,128)} %solid_in.1) | copy-start | bytes 344068
  3.0 22.4 %collective-permute-start = (bf16[136,1024]{1,0:T(8,128)(2,1)S(1)}, bf16[136,1024]{1,0:T(8,128)(2,1)S(1)}, u32[]{:S(2)}, u32[]{:S(2)}) collective-permute-start(bf16[136,1024]{1,0:T(8,128)(2,1)S(1)} %get-tuple-element.19), channel_id=1, source_target_pairs={{0,2},{2,4},{4,6},{6,8},{8,10},{10,12},{12,14},{1,3},{3,5},{5,7},{... | collective-permute-start | bytes 835592 | tf_op jit(solution)/shard_map/ppermute | solution.py:364
  7.9 17.5 %collective-permute-start.1 = (bf16[136,1024]{1,0:T(8,128)(2,1)S(1)}, bf16[136,1024]{1,0:T(8,128)(2,1)S(1)}, u32[]{:S(2)}, u32[]{:S(2)}) collective-permute-start(bf16[136,1024]{1,0:T(8,128)(2,1)S(1)} %get-tuple-element.20), channel_id=1, source_target_pairs={{2,0},{4,2},{6,4},{8,6},{10,8},{12,10},{14,12},{3,1},{5,3},{7,5},{... | collective-permute-start | bytes 835592 | tf_op jit(solution)/shard_map/ppermute | solution.py:364
  9.2 23.1 %collective-permute-start.2 = (bf16[136,768]{1,0:T(8,128)(2,1)S(1)}, bf16[136,768]{1,0:T(8,128)(2,1)S(1)}, u32[]{:S(2)}, u32[]{:S(2)}) collective-permute-start(bf16[136,768]{1,0:T(8,128)(2,1)S(1)} %get-tuple-element.23), channel_id=1, source_target_pairs={{0,2},{2,4},{4,6},{6,8},{8,10},{10,12},{12,14},{1,3},{3,5},{5,7},{... | collective-permute-start | bytes 626696 | tf_op jit(solution)/shard_map/ppermute | solution.py:365
  13.8 18.6 %collective-permute-start.3 = (bf16[136,768]{1,0:T(8,128)(2,1)S(1)}, bf16[136,768]{1,0:T(8,128)(2,1)S(1)}, u32[]{:S(2)}, u32[]{:S(2)}) collective-permute-start(bf16[136,768]{1,0:T(8,128)(2,1)S(1)} %get-tuple-element.24), channel_id=1, source_target_pairs={{2,0},{4,2},{6,4},{8,6},{10,8},{12,10},{14,12},{3,1},{5,3},{7,5},{... | collective-permute-start | bytes 626696 | tf_op jit(solution)/shard_map/ppermute | solution.py:365
  15.1 0.9 %copy-start.5 = (f32[16,1792]{1,0:T(8,128)S(1)}, f32[16,1792]{1,0:T(8,128)}, u32[]{:S(2)}) copy-start(f32[16,1792]{1,0:T(8,128)} %area.1) | copy-start | bytes 344068
  39.3 2.0 %collective-permute-start.5 = (bf16[32,8192]{1,0:T(8,128)(2,1)S(1)}, bf16[32,8192]{1,0:T(8,128)(2,1)S(1)}, u32[]{:S(2)}, u32[]{:S(2)}) collective-permute-start(bf16[32,8192]{1,0:T(8,128)(2,1)S(1)} %get-tuple-element.29), channel_id=1, source_target_pairs={{0,1},{1,0},{2,3},{3,2},{4,5},{5,4},{6,7},{7,6},{8,9},{9,8},{10,11... | collective-permute-start | bytes 1572872 | tf_op jit(solution)/shard_map/ppermute | solution.py:421
  39.4 2.6 %collective-permute-start.4 = (bf16[32,8192]{1,0:T(8,128)(2,1)S(1)}, bf16[32,8192]{1,0:T(8,128)(2,1)S(1)}, u32[]{:S(2)}, u32[]{:S(2)}) collective-permute-start(bf16[32,8192]{1,0:T(8,128)(2,1)S(1)} %get-tuple-element.27), channel_id=1, source_target_pairs={{0,1},{1,0},{2,3},{3,2},{4,5},{5,4},{6,7},{7,6},{8,9},{9,8},{10,11... | collective-permute-start | bytes 1572872 | tf_op jit(solution)/shard_map/ppermute | solution.py:420
  42.4 1.2 %collective-permute-start.6 = (f32[32,32]{1,0:T(8,128)S(1)}, f32[32,32]{1,0:T(8,128)S(1)}, u32[]{:S(2)}, u32[]{:S(2)}) collective-permute-start(f32[32,32]{1,0:T(8,128)S(1)} %meet.1), channel_id=1, source_target_pairs={{0,1},{1,0},{2,3},{3,2},{4,5},{5,4},{6,7},{7,6},{8,9},{9,8},{10,11... | collective-permute-start | bytes 12296 | tf_op jit(solution)/shard_map/ppermute | solution.py:430
  43.6 4.2 %collective-permute-start.7 = (f32[32,32]{1,0:T(8,128)S(1)}, f32[32,32]{1,0:T(8,128)S(1)}, u32[]{:S(2)}, u32[]{:S(2)}) collective-permute-start(f32[32,32]{1,0:T(8,128)S(1)} %add.12), channel_id=1, source_target_pairs={{0,2},{2,0},{4,6},{6,4},{8,10},{10,8},{12,14},{14,12},{1,3},{3,1},... | collective-permute-start | bytes 12296 | tf_op jit(solution)/shard_map/ppermute | solution.py:434
  47.8 3.7 %collective-permute-start.8 = (f32[32,32]{1,0:T(8,128)S(1)}, f32[32,32]{1,0:T(8,128)S(1)}, u32[]{:S(2)}, u32[]{:S(2)}) collective-permute-start(f32[32,32]{1,0:T(8,128)S(1)} %add.13), channel_id=1, source_target_pairs={{0,4},{2,6},{4,0},{6,2},{8,12},{10,14},{12,8},{14,10},{1,5},{3,7},... | collective-permute-start | bytes 12296 | tf_op jit(solution)/shard_map/ppermute | solution.py:434
  51.6 4.8 %collective-permute-start.9 = (f32[32,32]{1,0:T(8,128)S(1)}, f32[32,32]{1,0:T(8,128)S(1)}, u32[]{:S(2)}, u32[]{:S(2)}) collective-permute-start(f32[32,32]{1,0:T(8,128)S(1)} %add.14), channel_id=1, source_target_pairs={{0,8},{2,10},{4,12},{6,14},{8,0},{10,2},{12,4},{14,6},{1,9},{3,11}... | collective-permute-start | bytes 12296 | tf_op jit(solution)/shard_map/ppermute | solution.py:434

commit v5 on v4

--- a/solution.py
+++ b/solution.py
@@ -101,10 +101,11 @@
 
 
 def pack_kernel(
-    rows, inputs, cuts, field_in, along_in, across_in, viscous_in, solid_in, *refs
+    rows, inputs, left, odd_ref, field_in, along_in, across_in, viscous_in, solid_in,
+    inner, outer, coefs, field, along, across, viscous, solid, sems,
 ):
-    outs, (coefs, field, along, across, viscous, solid, sems) = refs[:-7], refs[-7:]
     cols = along.shape[1]
+    right = left + inner.shape[1]
     copies = [
         pltpu.make_async_copy(source, target, sems.at[index])
         for index, (source, target) in enumerate(
@@ -121,19 +122,29 @@
         copy.start()
     for copy in copies:
         copy.wait()
-    signed = jnp.where(solid[...] != 0, -viscous[...], viscous[...])
-    for side, first in enumerate((rows - HALO, 0)):
-        coefs[0:HALO, :] = along[first : first + HALO, :]
-        coefs[HALO : 2 * HALO, :] = across[first : first + HALO, :]
-        coefs[2 * HALO : 3 * HALO, :] = signed[first : first + HALO]
-        for chunk, (left, right) in enumerate(cuts):
-            out = outs[2 * chunk + side]
-            for step in range(HALO):
-                for tile in range(left // LANES, right // LANES):
-                    part = field[tile_of(rows, cols, first + step, tile, inputs), :]
-                    to = lanes_of(tile - left // LANES)
-                    out[step * inputs : (step + 1) * inputs, to] = part.astype(out.dtype)
-            out[HALO * inputs :, :] = coefs[:, left:right].astype(out.dtype)
+    is_odd = odd_ref[0] == 1
+    signed = jnp.where(solid[:, left:right] != 0, -viscous[:, left:right], viscous[:, left:right])
+    planes = (along[:, left:right], across[:, left:right], signed)
+
+    def fill(out, first):
+        for index, plane in enumerate(planes):
+            coefs[index * HALO : (index + 1) * HALO, :] = plane[first : first + HALO]
+        out[HALO * inputs :, :] = coefs[...].astype(out.dtype)
+        for step in range(HALO):
+            for tile in range(left // LANES, right // LANES):
+                part = field[tile_of(rows, cols, first + step, tile, inputs), :]
+                to = lanes_of(tile - left // LANES)
+                out[step * inputs : (step + 1) * inputs, to] = part.astype(out.dtype)
+
+    @pl.when(is_odd)
+    def _():
+        fill(inner, 0)
+        fill(outer, rows - HALO)
+
+    @pl.when(jnp.logical_not(is_odd))
+    def _():
+        fill(inner, rows - HALO)
+        fill(outer, 0)
 
 
 def prepare_kernel(
@@ -165,16 +176,17 @@
             weights[index, tile * rows : (tile + 1) * rows, :] = values
 
 
-def march_kernel(rows, inputs, first_pair, last_pair, sources, owned, all_pairs, adjoint_ref, own, own_weights, scale, *refs):
+def march_kernel(rows, inputs, first_pair, last_pair, sources, owned, all_pairs, flags, own, own_weights, scale, *refs):
     count = 2 * (1 + max(operand for operand, _ in sources))
     halos, refs = refs[:count], refs[count:]
+    both = None
     if last_pair < all_pairs:
-        for side in range(2):
-            refs[3][side] = halos[side][:, (last_pair - 1 - first_pair) * PAIR :]
+        both = refs[3]
         refs = (*refs[:3], *refs[4:])
     last, kept, sent, state_a, state_b, coefs, east_w, west_w, north_w, south_w, centre_w = refs
-    adjoint = adjoint_ref[0]
+    adjoint = flags[0]
     is_adjoint = adjoint == 1
+    is_odd = flags[1] == 1
     tiles = 2 * (last_pair - first_pair)
     tile0 = 2 * first_pair
     span = rows + 2 * HALO
@@ -183,21 +195,38 @@
     all_weights = (east_w, west_w, north_w, south_w, centre_w)
     edges = (first_pair == 0, last_pair == all_pairs)
 
-    for side, first in ((0, 0), (1, HALO + rows)):
-        sorted_coefs = [[], [], []]
-        for pair, (operand, place) in enumerate(sources):
-            at = slice(pair * PAIR, (pair + 1) * PAIR)
-            source = halos[2 * operand + side]
-            values = moved(source[:, place * PAIR : (place + 1) * PAIR], matrix)
-            state_a[(1 + first) * inputs : (1 + first + HALO) * inputs, at] = values[: HALO * inputs]
-            coefs[:, at] = values[HALO * inputs :]
-            for index, taken in enumerate(sorted_coefs):
-                part = coefs[index * HALO : (index + 1) * HALO, at]
-                taken += [part[:, :LANES], part[:, LANES:]]
-        for ref, values in zip(all_weights, weights_of(*sorted_coefs, is_adjoint, *edges)):
-            for tile in range(tiles):
-                start = tile * wide + SUB + first
-                ref[start : start + HALO, :] = values[tile]
+    def fill(low_at, high_at):
+        for side, first, at_side in ((0, 0, low_at), (1, HALO + rows, high_at)):
+            sorted_coefs = [[], [], []]
+            for pair, (operand, place) in enumerate(sources):
+                at = slice(pair * PAIR, (pair + 1) * PAIR)
+                source = halos[2 * operand + at_side[operand]]
+                source = source[:, place * PAIR : (place + 1) * PAIR]
+                if both is not None and pair == len(sources) - 1:
+                    both[side] = source
+                values = moved(source, matrix)
+                state_a[(1 + first) * inputs : (1 + first + HALO) * inputs, at] = values[
+                    : HALO * inputs
+                ]
+                coefs[:, at] = values[HALO * inputs :]
+                for index, taken in enumerate(sorted_coefs):
+                    part = coefs[index * HALO : (index + 1) * HALO, at]
+                    taken += [part[:, :LANES], part[:, LANES:]]
+            for ref, values in zip(all_weights, weights_of(*sorted_coefs, is_adjoint, *edges)):
+                for tile in range(tiles):
+                    start = tile * wide + SUB + first
+                    ref[start : start + HALO, :] = values[tile]
+
+    fixed = (0,) * (len(halos) // 2 - 1), (1,) * (len(halos) // 2 - 1)
+
+    @pl.when(is_odd)
+    def _():
+        fill((*fixed[0], 0), (*fixed[1], 1))
+
+    @pl.when(jnp.logical_not(is_odd))
+    def _():
+        fill((*fixed[0], 1), (*fixed[1], 0))
+
     state_a[(1 + HALO) * inputs : (1 + HALO + rows) * inputs, :] = own[
         :, tile0 * LANES : (tile0 + tiles) * LANES
     ]
@@ -211,40 +240,25 @@
     lane = lax.broadcasted_iota(jnp.int32, (inputs, LANES), 1)
     for step in range(1, HALO + 1):
         src, dst = states[(step - 1) % 2], states[step % 2]
-        count = span - 2 * step
-        group = min((8, 7, 9, 10, 6, 11), key=lambda size: -(-count // size) * size)
-        trips = -(-count // group)
-        first_row = step - (trips * group - count) // 2
-
-        def advance(index, carry, src=src, dst=dst, first_row=first_row, group=group):
-            row0 = first_row + index * group
-
-            def at_row(row):
-                return pl.ds(pl.multiple_of((1 + row) * inputs, inputs), inputs)
-
-            def weight(ref, row, tile):
-                return ref[pl.ds(tile * wide + SUB + row, inputs, stride=0), :]
-
-            lines = [{} for _ in range(group + 2)]
-            for pair in range(tiles // 2):
-                for n, line in enumerate(lines):
-                    for tile in (2 * pair - 1, 2 * pair, 2 * pair + 1, 2 * pair + 2):
-                        tile %= tiles
-                        if tile not in line and (tile // 2 == pair or 0 < n <= group):
-                            line[tile] = src[at_row(row0 + n - 1), lanes_of(tile)]
-                for n in range(group):
-                    row = row0 + n
-                    here = lines[n + 1]
-                    for tile in (2 * pair, 2 * pair + 1):
-                        total = weight(centre_w, row, tile) * here[tile]
-                        total += weight(north_w, row + adjoint, tile) * lines[n + 2][tile]
-                        total += weight(south_w, row - adjoint, tile) * lines[n][tile]
-                        total += weight(east_w, row, tile) * eastern(here, tile, lane, tiles)
-                        total += weight(west_w, row, tile) * western(here, tile, lane, tiles)
-                        dst[at_row(row), lanes_of(tile)] = total
-            return carry
-
-        lax.fori_loop(0, trips, advance, 0)
+
+        def line(row, src=src):
+            at = slice((1 + row) * inputs, (2 + row) * inputs)
+            return [src[at, lanes_of(tile)] for tile in range(tiles)]
+
+        def weight(ref, row, tile):
+            return ref[pl.ds(tile * wide + SUB + row, inputs, stride=0), :]
+
+        behind, here = line(step - 1), line(step)
+        for row in range(step, span - step):
+            ahead = line(row + 1)
+            for tile in range(tiles):
+                total = weight(centre_w, row, tile) * here[tile]
+                total += weight(north_w, row + adjoint, tile) * ahead[tile]
+                total += weight(south_w, row - adjoint, tile) * behind[tile]
+                total += weight(east_w, row, tile) * eastern(here, tile, lane, tiles)
+                total += weight(west_w, row, tile) * western(here, tile, lane, tiles)
+                dst[(1 + row) * inputs : (2 + row) * inputs, lanes_of(tile)] = total
+            behind, here = here, ahead
         if step % STRIDE == 0:
             snap = slice((step // STRIDE - 1) * inputs, (step // STRIDE) * inputs)
 
@@ -315,7 +329,8 @@
 
 def local(init_fields, streamwise, crossflow, diffusivity, obstacle, cell_weight):
     adjoint = lax.axis_index("fa").astype(jnp.int32)
-    flag = adjoint[None]
+    flag = jnp.stack([adjoint, lax.axis_index("rows").astype(jnp.int32) % 2])
+    odd = flag[1:]
     _, inputs, rows, cols = init_fields.shape
     field = tiled(init_fields[0])
     coef_rows = up8(3 * HALO)
@@ -336,33 +351,41 @@
     pairs = cols // PAIR
     shared = pairs // 2
     cut = (shared + 1) * PAIR
-    cuts = ((0, cut), (cut, cols))
-    packed = [
-        shape(packed_rows, right - left, dtype=BF16) for left, right in cuts for _ in range(2)
+    plane = pltpu.VMEM((rows, cols), F32)
+    grids = [
+        pltpu.with_memory_space_constraint(x, pltpu.HBM)
+        for x in (field, streamwise, crossflow, diffusivity, obstacle)
     ]
-    plane = pltpu.VMEM((rows, cols), F32)
-    up_a, down_a, up_b, down_b = pl.pallas_call(
-        functools.partial(pack_kernel, rows, inputs, cuts),
-        out_shape=packed,
-        in_specs=[hbm] * 5,
-        out_specs=[vmem] * 4,
-        scratch_shapes=[
-            pltpu.VMEM((coef_rows, cols), F32),
-            pltpu.VMEM(field.shape, F32),
-            plane,
-            plane,
-            plane,
-            pltpu.VMEM((rows, cols), jnp.int32),
-            pltpu.SemaphoreType.DMA((5,)),
-        ],
-        compiler_params=params,
-        name="pack",
-    )(*[pltpu.with_memory_space_constraint(x, pltpu.HBM) for x in (field, streamwise, crossflow, diffusivity, obstacle)])
+
+    def pack(left, right):
+        return pl.pallas_call(
+            functools.partial(pack_kernel, rows, inputs, left),
+            out_shape=[shape(packed_rows, right - left, dtype=BF16)] * 2,
+            in_specs=[smem] + [hbm] * 5,
+            out_specs=[vmem] * 2,
+            scratch_shapes=[
+                pltpu.VMEM((coef_rows, right - left), F32),
+                pltpu.VMEM(field.shape, F32),
+                plane,
+                plane,
+                plane,
+                pltpu.VMEM((rows, cols), jnp.int32),
+                pltpu.SemaphoreType.DMA((5,)),
+            ],
+            compiler_params=params,
+            cost_estimate=cost(10**8),
+        )(odd, *grids)
+
     size = lax.axis_size("rows")
-    rise = [(i, i + 1) for i in range(size - 1)]
-    fall = [(j, i) for i, j in rise]
-    low_a, high_a = lax.ppermute(up_a, "rows", rise), lax.ppermute(down_a, "rows", fall)
-    low_b, high_b = lax.ppermute(up_b, "rows", rise), lax.ppermute(down_b, "rows", fall)
+    inner = [(i, i ^ 1) for i in range(size) if i ^ 1 < size]
+    outer = [(i, (i - 1 ^ 1) + 1) for i in range(1, size) if (i - 1 ^ 1) + 1 < size]
+
+    def exchange(parts):
+        return lax.ppermute(parts[0], "rows", inner), lax.ppermute(parts[1], "rows", outer)
+
+    halo_a = exchange(pack(0, cut))
+    packed_b = pack(cut, cols)
+    halo_b = exchange(packed_b)
 
     prepare = pl.pallas_call(
         functools.partial(prepare_kernel, rows, inputs),
@@ -407,14 +430,14 @@
 
     middle = LANES // 2
     last_a, kept_a, sent_a, both = march(
-        0, shared + 1, [(0, p) for p in range(shared + 1)], (0, middle), (low_a, high_a)
+        0, shared + 1, [(0, p) for p in range(shared + 1)], (0, middle), halo_a
     )
     last_b, kept_b, sent_b = march(
         shared,
         pairs,
         [(0, 0)] + [(1, p) for p in range(pairs - shared - 1)],
         (middle, LANES),
-        (both[0], both[1], low_b, high_b),
+        (both[0], both[1], *halo_b),
     )
     swap = [(0, 1), (1, 0)]
     other_a = lax.ppermute(sent_a, "fa", swap)

time: 57.2 us -> 54.2 us (0.948)
  starting transfers between devices: 20.2 us -> 17.2 us
  Pallas kernels: 20.5 us -> 21.5 us
  local copies, waits for them, and re-layouts: 0.93 us -> 0.04 us
    ppermute x4, starting transfers between devices: 12 us -> 8.84 us  [the longest x2 7.36 us: exchange(): lax.ppermute(parts[0], 'rows', inner)]
    pallas_call x2, Pallas kernels: 13.9 us -> 12.5 us  [march(): pl.pallas_call(functools.partial(march_kernel, rows, inputs, first_pair,...]
    pallas_call x1 -> x2, Pallas kernels: 2.3 us -> 3.57 us  [pack(): pl.pallas_call(functools.partial(pack_kernel, rows, inputs, left), out_sh...]
    unnamed x12, local copies, waits for them, and re-layouts: 0.91 us -> 0.03 us
  transfers between devices with their start and end apart: 10 -> 10, of which waited for: 6 -> 6; matrix products, arithmetic and copies ran while one was open for 0% -> 0% of each run, Pallas kernels for 19% -> 23%
where the time goes in v5:
time: 54.2 us; the launch traced here: 54 us
  Pallas kernels  21.5 us (40%)
  starting transfers between devices  17.2 us (32%)
  waiting for transfers between devices  13.8 us (25%)
  between operations  0.78 us (1%)
  other arithmetic  0.7 us (1%)
    pallas_call x2, Pallas kernels, march(): pl.pallas_call(functools.partial(march_kernel, rows, inputs, first_pair,...  12.5 us
    ppermute x3, starting transfers between devices, local(): lax.ppermute(total, 'rows', [(i, i ^ stride) for i in range(size)])  7.62 us
    ppermute x2, starting transfers between devices, exchange(): lax.ppermute(parts[0], 'rows', inner)  7.36 us
    ppermute x2, waiting for transfers between devices, exchange(): lax.ppermute(parts[0], 'rows', inner)  7.16 us
    pallas_call x2, Pallas kernels, pack(): pl.pallas_call(functools.partial(pack_kernel, rows, inputs, left), out_sh...  3.57 us
    ppermute x3, waiting for transfers between devices, local(): lax.ppermute(total, 'rows', [(i, i ^ stride) for i in range(size)])  3.43 us
    pallas_call x1, Pallas kernels, local(): prepare(flag, field, streamwise, crossflow, diffusivity, obstacle, cell_w...  2.67 us
    pallas_call x1, Pallas kernels, local(): pl.pallas_call(functools.partial(finish_kernel, rows, inputs, shared), ou...  1.83 us
  transfers between devices with their start and end apart: 10, of which 6 were waited for; matrix products, arithmetic and copies ran while one was open for 0% of the time, Pallas kernels for 23%

profile of v5, /device:TPU:0, one launch (start us, length us, event | category | flops | bytes accessed | tf_op | source)
XLA Modules:
  0.0 54.0 jit_solution(15643767666614762184)
XLA Ops:
  0.6 0.0 copy-start.5
  0.7 1.9 %shard_map.77 = (bf16[136,1024]{1,0:T(8,128)(2,1)S(1)}, bf16[136,1024]{1,0:T(8,128)(2,1)S(1)}) custom-call(s32[1]{0:T(128)} %bitcast.1.odd_ref, f32[1792,128]{1,0:T(8,128)} %bitcast.16, f32[16,1792]{1,0:T(8,128)} %along_in.3, f32[16,1792]{1,0:T(8,128)} %across_in.3, f32[16,1792]{1,0:T(8,128)} %viscous_in.3, s32[16,1792]{1,0:T(8,128)} %solid_in.3), custom_call_target="tpu_custom_call" | custom-call | flops 100000000 | bytes 3670016 | tf_op jit(solution)/shard_map/pallas_call | solution.py:361
  2.5 0.0 copy-start
  2.5 3.0 %collective-permute-start = (bf16[136,1024]{1,0:T(8,128)(2,1)S(1)}, bf16[136,1024]{1,0:T(8,128)(2,1)S(1)}, u32[]{:S(2)}, u32[]{:S(2)}) collective-permute-start(bf16[136,1024]{1,0:T(8,128)(2,1)S(1)} %get-tuple-element.19), channel_id=1, source_target_pairs={{0,2},{2,0},{4,6},{6,4},{8,10},{10,8},{12,14},{14,12},{1,3},{3,1},... | collective-permute-start | bytes 835592 | tf_op jit(solution)/shard_map/ppermute | solution.py:384
  5.6 0.0 copy-start.1
  5.6 0.0 copy-start.2
  5.6 0.0 copy-start.3
  5.6 0.0 copy-start.4
  5.6 0.8 %collective-permute-start.1 = (bf16[136,1024]{1,0:T(8,128)(2,1)S(1)}, bf16[136,1024]{1,0:T(8,128)(2,1)S(1)}, u32[]{:S(2)}, u32[]{:S(2)}) collective-permute-start(bf16[136,1024]{1,0:T(8,128)(2,1)S(1)} %get-tuple-element.20), channel_id=1, source_target_pairs={{2,4},{4,2},{6,8},{8,6},{10,12},{12,10},{3,5},{5,3},{7,9},{9,7},{1... | collective-permute-start | bytes 835592 | tf_op jit(solution)/shard_map/ppermute | solution.py:384
  6.4 1.7 %shard_map.79 = (bf16[136,768]{1,0:T(8,128)(2,1)S(1)}, bf16[136,768]{1,0:T(8,128)(2,1)S(1)}) custom-call(s32[1]{0:T(128)} %bitcast.1.odd_ref, f32[1792,128]{1,0:T(8,128)} %bitcast.17, f32[16,1792]{1,0:T(8,128)} %along_in.3, f32[16,1792]{1,0:T(8,128)} %across_in.3, f32[16,1792]{1,0:T(8,128)} %viscous_in.3, s32[16,1792]{1,0:T(8,128)} %solid_in.3), custom_call_target="tpu_custom_call" | custom-call | flops 100000000 | bytes 3670016 | tf_op jit(solution)/shard_map/pallas_call | solution.py:361
  8.1 4.3 %collective-permute-start.2 = (bf16[136,768]{1,0:T(8,128)(2,1)S(1)}, bf16[136,768]{1,0:T(8,128)(2,1)S(1)}, u32[]{:S(2)}, u32[]{:S(2)}) collective-permute-start(bf16[136,768]{1,0:T(8,128)(2,1)S(1)} %get-tuple-element.23), channel_id=1, source_target_pairs={{0,2},{2,0},{4,6},{6,4},{8,10},{10,8},{12,14},{14,12},{1,3},{3,1},... | collective-permute-start | bytes 626696 | tf_op jit(solution)/shard_map/ppermute | solution.py:384
  12.4 0.7 %collective-permute-start.3 = (bf16[136,768]{1,0:T(8,128)(2,1)S(1)}, bf16[136,768]{1,0:T(8,128)(2,1)S(1)}, u32[]{:S(2)}, u32[]{:S(2)}) collective-permute-start(bf16[136,768]{1,0:T(8,128)(2,1)S(1)} %get-tuple-element.24), channel_id=1, source_target_pairs={{2,4},{4,2},{6,8},{8,6},{10,12},{12,10},{3,5},{5,3},{7,9},{9,7},{1... | collective-permute-start | bytes 626696 | tf_op jit(solution)/shard_map/ppermute | solution.py:384
  13.1 0.1 pad_add_fusion.adjoint_ref.flags
  13.2 0.0 copy-done.5
  13.2 0.0 copy-done
  13.2 0.0 copy-done.1
  13.2 0.0 copy-done.2
  13.2 0.0 copy-done.3
  13.2 0.0 copy-done.4
  13.2 2.7 %prepare.1 = (f32[128,1792]{1,0:T(8,128)S(1)}, f32[5,224,128]{2,1,0:T(8,128)S(1)}, f32[224,128]{1,0:T(8,128)S(1)}) custom-call(s32[2]{0:T(128)S(1)} %pad_add_fusion.adjoint_ref.flags, f32[1792,128]{1,0:T(8,128)S(1)} %bitcast.18, f32[16,1792]{1,0:T(8,128)S(1)} %copy-done.1, f32[16,1792]{1,0:T(8,128)S(1)} %copy-done.2, f32[16,1792]{1,0:T(8,128)S(1)} %copy-done.3, ...), custom_call_target="tpu_custom_call" | custom-call | flops 1000000000 | bytes 3670016 | tf_op jit(solution)/shard_map/prepare/pallas_call | solution.py:404
  15.9 7.2 %collective-permute-done.refs_0_ = bf16[136,1024]{1,0:T(8,128)(2,1)S(1)} collective-permute-done((bf16[136,1024]{1,0:T(8,128)(2,1)S(1)}, bf16[136,1024]{1,0:T(8,128)(2,1)S(1)}, u32[]{:S(2)}, u32[]{:S(2)}) %collective-permute-start) | collective-permute-done | bytes 278560 | tf_op jit(solution)/shard_map/ppermute | solution.py:384
  23.1 0.0 collective-permute-done.1.refs_1_
  23.1 6.1 %shard_map.78 = (f32[128,1024]{1,0:T(8,128)S(1)}, bf16[32,8192]{1,0:T(8,128)(2,1)S(1)}, bf16[32,8192]{1,0:T(8,128)(2,1)S(1)}, bf16[2,136,256]{2,1,0:T(8,128)(2,1)S(1)}) custom-call(s32[2]{0:T(128)S(1)} %pad_add_fusion.adjoint_ref.flags, f32[128,1792]{1,0:T(8,128)S(1)} %get-tuple-element.16.own, f32[5,224,128]{2,1,0:T(8,128)S(1)} %get-tuple-element.17.own_weights, ...), custom_call_target="tpu_custom_call" | custom-call | flops 1000000000 | bytes 3670016 | tf_op jit(solution)/shard_map/pallas_call | solution.py:411
  29.2 0.0 collective-permute-done.2.refs_2_
  29.2 0.0 collective-permute-done.3.refs_3_
  29.2 6.3 %shard_map.80 = (f32[128,1024]{1,0:T(8,128)S(1)}, bf16[32,8192]{1,0:T(8,128)(2,1)S(1)}, bf16[32,8192]{1,0:T(8,128)(2,1)S(1)}) custom-call(s32[2]{0:T(128)S(1)} %pad_add_fusion.adjoint_ref.flags, f32[128,1792]{1,0:T(8,128)S(1)} %get-tuple-element.16.own, f32[5,224,128]{2,1,0:T(8,128)S(1)} %get-tuple-element.17.own_weights, ...), custom_call_target="tpu_custom_call" | custom-call | flops 1000000000 | bytes 3670016 | tf_op jit(solution)/shard_map/pallas_call | solution.py:411
  35.6 0.1 collective-permute-start.5
  35.6 0.5 collective-permute-start.4
  36.1 1.4 %collective-permute-done.5.other_b = bf16[32,8192]{1,0:T(8,128)(2,1)S(1)} collective-permute-done((bf16[32,8192]{1,0:T(8,128)(2,1)S(1)}, bf16[32,8192]{1,0:T(8,128)(2,1)S(1)}, u32[]{:S(2)}, u32[]{:S(2)}) %collective-permute-start.5) | collective-permute-done | bytes 524320 | tf_op jit(solution)/shard_map/ppermute | solution.py:444
  37.5 0.7 %collective-permute-done.4.other_a = bf16[32,8192]{1,0:T(8,128)(2,1)S(1)} collective-permute-done((bf16[32,8192]{1,0:T(8,128)(2,1)S(1)}, bf16[32,8192]{1,0:T(8,128)(2,1)S(1)}, u32[]{:S(2)}, u32[]{:S(2)}) %collective-permute-start.4) | collective-permute-done | bytes 524320 | tf_op jit(solution)/shard_map/ppermute | solution.py:443
  38.3 0.9 %meet.1 = f32[32,32]{1,0:T(8,128)S(1)} custom-call(s32[2]{0:T(128)S(1)} %pad_add_fusion.adjoint_ref.flags, bf16[32,8192]{1,0:T(8,128)(2,1)S(1)} %get-tuple-element.26.mine_a, bf16[32,8192]{1,0:T(8,128)(2,1)S(1)} %collective-permute-done.4.other_a, bf16[32,8192]{1,0:T(8,128)(2,1)S(1)} %get-tuple-element.28.mine_b, ...), custom_call_target="tpu_custom_call" | custom-call | tf_op jit(solution)/shard_map/meet/pallas_call | solution.py:445
  39.2 0.2 collective-permute-start.6
  39.4 1.0 %collective-permute-done.6 = f32[32,32]{1,0:T(8,128)S(1)} collective-permute-done((f32[32,32]{1,0:T(8,128)S(1)}, f32[32,32]{1,0:T(8,128)S(1)}, u32[]{:S(2)}, u32[]{:S(2)}) %collective-permute-start.6) | collective-permute-done | bytes 4128 | tf_op jit(solution)/shard_map/ppermute | solution.py:453
  40.4 2.5 %collective-permute-start.7 = (f32[32,32]{1,0:T(8,128)S(1)}, f32[32,32]{1,0:T(8,128)S(1)}, u32[]{:S(2)}, u32[]{:S(2)}) collective-permute-start(f32[32,32]{1,0:T(8,128)S(1)} %add.17), channel_id=1, source_target_pairs={{0,2},{2,0},{4,6},{6,4},{8,10},{10,8},{12,14},{14,12},{1,3},{3,1},... | collective-permute-start | bytes 12296 | tf_op jit(solution)/shard_map/ppermute | solution.py:457
  42.9 1.7 %collective-permute-done.7 = f32[32,32]{1,0:T(8,128)S(1)} collective-permute-done((f32[32,32]{1,0:T(8,128)S(1)}, f32[32,32]{1,0:T(8,128)S(1)}, u32[]{:S(2)}, u32[]{:S(2)}) %collective-permute-start.7) | collective-permute-done | bytes 4128 | tf_op jit(solution)/shard_map/ppermute | solution.py:457
  44.6 2.1 %collective-permute-start.8 = (f32[32,32]{1,0:T(8,128)S(1)}, f32[32,32]{1,0:T(8,128)S(1)}, u32[]{:S(2)}, u32[]{:S(2)}) collective-permute-start(f32[32,32]{1,0:T(8,128)S(1)} %add.18), channel_id=1, source_target_pairs={{0,4},{2,6},{4,0},{6,2},{8,12},{10,14},{12,8},{14,10},{1,5},{3,7},... | collective-permute-start | bytes 12296 | tf_op jit(solution)/shard_map/ppermute | solution.py:457
  46.8 1.7 %collective-permute-done.8 = f32[32,32]{1,0:T(8,128)S(1)} collective-permute-done((f32[32,32]{1,0:T(8,128)S(1)}, f32[32,32]{1,0:T(8,128)S(1)}, u32[]{:S(2)}, u32[]{:S(2)}) %collective-permute-start.8) | collective-permute-done | bytes 4128 | tf_op jit(solution)/shard_map/ppermute | solution.py:457
  48.5 3.0 %collective-permute-start.9 = (f32[32,32]{1,0:T(8,128)S(1)}, f32[32,32]{1,0:T(8,128)S(1)}, u32[]{:S(2)}, u32[]{:S(2)}) collective-permute-start(f32[32,32]{1,0:T(8,128)S(1)} %add.19), channel_id=1, source_target_pairs={{0,8},{2,10},{4,12},{6,14},{8,0},{10,2},{12,4},{14,6},{1,9},{3,11}... | collective-permute-start | bytes 12296 | tf_op jit(solution)/shard_map/ppermute | solution.py:457
  51.5 1.8 %finish.1 = f32[1792,128]{1,0:T(8,128)} custom-call(f32[128,1024]{1,0:T(8,128)S(1)} %get-tuple-element.21.left, f32[128,1024]{1,0:T(8,128)S(1)} %get-tuple-element.25.right), custom_call_target="tpu_custom_call" | custom-call | flops 10000000 | bytes 3670016 | tf_op jit(solution)/shard_map/finish/pallas_call | solution.py:462
  53.3 0.0 collective-permute-done.9
  53.4 0.6 %add_multiply_fusion = f32[32,32]{1,0:T(8,128)} fusion(f32[32,32]{1,0:T(8,128)S(1)} %add.19, f32[32,32]{1,0:T(8,128)S(1)} %collective-permute-done.9), kind=kLoop, calls=%fused_computation.2 | loop fusion | flops 2048 | bytes 12288 | tf_op jit(solution)/shard_map/mul | solution.py:461
  (4 shorter events, 0.0 us)
Async XLA Ops:
  0.6 12.6 %copy-start.5 = (f32[16,1792]{1,0:T(8,128)S(1)}, f32[16,1792]{1,0:T(8,128)}, u32[]{:S(2)}) copy-start(f32[16,1792]{1,0:T(8,128)} %area.1) | copy-start | bytes 344068
  2.5 10.7 %copy-start = (f32[1,8,16,1792]{3,2,1,0:T(8,128)S(1)}, f32[1,8,16,1792]{3,2,1,0:T(8,128)}, u32[]{:S(2)}) copy-start(f32[1,8,16,1792]{3,2,1,0:T(8,128)} %param.6) | copy-start | bytes 2752516
  2.5 20.5 %collective-permute-start = (bf16[136,1024]{1,0:T(8,128)(2,1)S(1)}, bf16[136,1024]{1,0:T(8,128)(2,1)S(1)}, u32[]{:S(2)}, u32[]{:S(2)}) collective-permute-start(bf16[136,1024]{1,0:T(8,128)(2,1)S(1)} %get-tuple-element.19), channel_id=1, source_target_pairs={{0,2},{2,0},{4,6},{6,4},{8,10},{10,8},{12,14},{14,12},{1,3},{3,1},... | collective-permute-start | bytes 835592 | tf_op jit(solution)/shard_map/ppermute | solution.py:384
  5.6 7.6 %copy-start.1 = (f32[16,1792]{1,0:T(8,128)S(1)}, f32[16,1792]{1,0:T(8,128)}, u32[]{:S(2)}) copy-start(f32[16,1792]{1,0:T(8,128)} %along_in.3) | copy-start | bytes 344068
  5.6 7.6 %copy-start.2 = (f32[16,1792]{1,0:T(8,128)S(1)}, f32[16,1792]{1,0:T(8,128)}, u32[]{:S(2)}) copy-start(f32[16,1792]{1,0:T(8,128)} %across_in.3) | copy-start | bytes 344068
  5.6 7.6 %copy-start.3 = (f32[16,1792]{1,0:T(8,128)S(1)}, f32[16,1792]{1,0:T(8,128)}, u32[]{:S(2)}) copy-start(f32[16,1792]{1,0:T(8,128)} %viscous_in.3) | copy-start | bytes 344068
  5.6 7.6 %copy-start.4 = (s32[16,1792]{1,0:T(8,128)S(1)}, s32[16,1792]{1,0:T(8,128)}, u32[]{:S(2)}) copy-start(s32[16,1792]{1,0:T(8,128)} %solid_in.3) | copy-start | bytes 344068
  5.6 17.5 %collective-permute-start.1 = (bf16[136,1024]{1,0:T(8,128)(2,1)S(1)}, bf16[136,1024]{1,0:T(8,128)(2,1)S(1)}, u32[]{:S(2)}, u32[]{:S(2)}) collective-permute-start(bf16[136,1024]{1,0:T(8,128)(2,1)S(1)} %get-tuple-element.20), channel_id=1, source_target_pairs={{2,4},{4,2},{6,8},{8,6},{10,12},{12,10},{3,5},{5,3},{7,9},{9,7},{1... | collective-permute-start | bytes 835592 | tf_op jit(solution)/shard_map/ppermute | solution.py:384
  8.1 21.1 %collective-permute-start.2 = (bf16[136,768]{1,0:T(8,128)(2,1)S(1)}, bf16[136,768]{1,0:T(8,128)(2,1)S(1)}, u32[]{:S(2)}, u32[]{:S(2)}) collective-permute-start(bf16[136,768]{1,0:T(8,128)(2,1)S(1)} %get-tuple-element.23), channel_id=1, source_target_pairs={{0,2},{2,0},{4,6},{6,4},{8,10},{10,8},{12,14},{14,12},{1,3},{3,1},... | collective-permute-start | bytes 626696 | tf_op jit(solution)/shard_map/ppermute | solution.py:384
  12.4 16.8 %collective-permute-start.3 = (bf16[136,768]{1,0:T(8,128)(2,1)S(1)}, bf16[136,768]{1,0:T(8,128)(2,1)S(1)}, u32[]{:S(2)}, u32[]{:S(2)}) collective-permute-start(bf16[136,768]{1,0:T(8,128)(2,1)S(1)} %get-tuple-element.24), channel_id=1, source_target_pairs={{2,4},{4,2},{6,8},{8,6},{10,12},{12,10},{3,5},{5,3},{7,9},{9,7},{1... | collective-permute-start | bytes 626696 | tf_op jit(solution)/shard_map/ppermute | solution.py:384
  35.6 2.0 %collective-permute-start.5 = (bf16[32,8192]{1,0:T(8,128)(2,1)S(1)}, bf16[32,8192]{1,0:T(8,128)(2,1)S(1)}, u32[]{:S(2)}, u32[]{:S(2)}) collective-permute-start(bf16[32,8192]{1,0:T(8,128)(2,1)S(1)} %get-tuple-element.29), channel_id=1, source_target_pairs={{0,1},{1,0},{2,3},{3,2},{4,5},{5,4},{6,7},{7,6},{8,9},{9,8},{10,11... | collective-permute-start | bytes 1572872 | tf_op jit(solution)/shard_map/ppermute | solution.py:444
  35.6 2.6 %collective-permute-start.4 = (bf16[32,8192]{1,0:T(8,128)(2,1)S(1)}, bf16[32,8192]{1,0:T(8,128)(2,1)S(1)}, u32[]{:S(2)}, u32[]{:S(2)}) collective-permute-start(bf16[32,8192]{1,0:T(8,128)(2,1)S(1)} %get-tuple-element.27), channel_id=1, source_target_pairs={{0,1},{1,0},{2,3},{3,2},{4,5},{5,4},{6,7},{7,6},{8,9},{9,8},{10,11... | collective-permute-start | bytes 1572872 | tf_op jit(solution)/shard_map/ppermute | solution.py:443
  39.2 1.2 %collective-permute-start.6 = (f32[32,32]{1,0:T(8,128)S(1)}, f32[32,32]{1,0:T(8,128)S(1)}, u32[]{:S(2)}, u32[]{:S(2)}) collective-permute-start(f32[32,32]{1,0:T(8,128)S(1)} %meet.1), channel_id=1, source_target_pairs={{0,1},{1,0},{2,3},{3,2},{4,5},{5,4},{6,7},{7,6},{8,9},{9,8},{10,11... | collective-permute-start | bytes 12296 | tf_op jit(solution)/shard_map/ppermute | solution.py:453
  40.4 4.2 %collective-permute-start.7 = (f32[32,32]{1,0:T(8,128)S(1)}, f32[32,32]{1,0:T(8,128)S(1)}, u32[]{:S(2)}, u32[]{:S(2)}) collective-permute-start(f32[32,32]{1,0:T(8,128)S(1)} %add.17), channel_id=1, source_target_pairs={{0,2},{2,0},{4,6},{6,4},{8,10},{10,8},{12,14},{14,12},{1,3},{3,1},... | collective-permute-start | bytes 12296 | tf_op jit(solution)/shard_map/ppermute | solution.py:457
  44.6 3.8 %collective-permute-start.8 = (f32[32,32]{1,0:T(8,128)S(1)}, f32[32,32]{1,0:T(8,128)S(1)}, u32[]{:S(2)}, u32[]{:S(2)}) collective-permute-start(f32[32,32]{1,0:T(8,128)S(1)} %add.18), channel_id=1, source_target_pairs={{0,4},{2,6},{4,0},{6,2},{8,12},{10,14},{12,8},{14,10},{1,5},{3,7},... | collective-permute-start | bytes 12296 | tf_op jit(solution)/shard_map/ppermute | solution.py:457
  48.5 4.9 %collective-permute-start.9 = (f32[32,32]{1,0:T(8,128)S(1)}, f32[32,32]{1,0:T(8,128)S(1)}, u32[]{:S(2)}, u32[]{:S(2)}) collective-permute-start(f32[32,32]{1,0:T(8,128)S(1)} %add.19), channel_id=1, source_target_pairs={{0,8},{2,10},{4,12},{6,14},{8,0},{10,2},{12,4},{14,6},{1,9},{3,11}... | collective-permute-start | bytes 12296 | tf_op jit(solution)/shard_map/ppermute | solution.py:457

commit v6 on v5

--- a/solution.py
+++ b/solution.py
@@ -176,7 +176,7 @@
             weights[index, tile * rows : (tile + 1) * rows, :] = values
 
 
-def march_kernel(rows, inputs, first_pair, last_pair, sources, owned, all_pairs, flags, own, own_weights, scale, *refs):
+def march_kernel(rows, inputs, first_pair, last_pair, sources, owned, all_pairs, adjoint_ref, odd_ref, own, own_weights, scale, *refs):
     count = 2 * (1 + max(operand for operand, _ in sources))
     halos, refs = refs[:count], refs[count:]
     both = None
@@ -184,9 +184,9 @@
         both = refs[3]
         refs = (*refs[:3], *refs[4:])
     last, kept, sent, state_a, state_b, coefs, east_w, west_w, north_w, south_w, centre_w = refs
-    adjoint = flags[0]
+    adjoint = adjoint_ref[0]
     is_adjoint = adjoint == 1
-    is_odd = flags[1] == 1
+    is_odd = odd_ref[0] == 1
     tiles = 2 * (last_pair - first_pair)
     tile0 = 2 * first_pair
     span = rows + 2 * HALO
@@ -329,8 +329,8 @@
 
 def local(init_fields, streamwise, crossflow, diffusivity, obstacle, cell_weight):
     adjoint = lax.axis_index("fa").astype(jnp.int32)
-    flag = jnp.stack([adjoint, lax.axis_index("rows").astype(jnp.int32) % 2])
-    odd = flag[1:]
+    flag = adjoint[None]
+    odd = (lax.axis_index("rows").astype(jnp.int32) % 2)[None]
     _, inputs, rows, cols = init_fields.shape
     field = tiled(init_fields[0])
     coef_rows = up8(3 * HALO)
@@ -417,7 +417,7 @@
                 *[shape(NSNAP * inputs, rows * chunk // 2, dtype=BF16)] * 2,
                 *more,
             ),
-            in_specs=[smem] + [vmem] * (3 + len(halos)),
+            in_specs=[smem] * 2 + [vmem] * (3 + len(halos)),
             out_specs=(vmem,) * (3 + len(more)),
             scratch_shapes=[
                 *[pltpu.VMEM(((span + 2) * inputs, chunk), F32)] * 2,
@@ -426,7 +426,7 @@
             ],
             compiler_params=params,
             cost_estimate=cost(10**9),
-        )(flag, own, own_weights, scale, *halos)
+        )(flag, odd, own, own_weights, scale, *halos)
 
     middle = LANES // 2
     last_a, kept_a, sent_a, both = march(

time: 54.2 us -> 52.6 us (0.970)
  Pallas kernels: 21.5 us -> 19.3 us
  waiting for transfers between devices: 13.8 us -> 14.4 us
    pallas_call x2, Pallas kernels: 12.5 us -> 11.4 us  [march(): pl.pallas_call(functools.partial(march_kernel, rows, inputs, first_pair,...]
    ppermute x2, waiting for transfers between devices: 7.16 us -> 7.74 us  [exchange(): lax.ppermute(parts[0], 'rows', inner)]
    pallas_call x1, Pallas kernels: 0.95 us -> 0.4 us  [local(): pl.pallas_call(meet_kernel, out_shape=shape(NSNAP * inputs, NSNAP * input...]
  transfers between devices with their start and end apart: 10 -> 10, of which waited for: 6 -> 6; matrix products, arithmetic and copies ran while one was open for 0% -> 0% of each run, Pallas kernels for 23% -> 21%
where the time goes in v6:
time: 52.6 us; the launch traced here: 52.4 us
  Pallas kernels  19.3 us (37%)
  starting transfers between devices  17.2 us (33%)
  waiting for transfers between devices  14.4 us (27%)
  between operations  0.81 us (2%)
  other arithmetic  0.62 us (1%)
    pallas_call x2, Pallas kernels, march(): pl.pallas_call(functools.partial(march_kernel, rows, inputs, first_pair,...  11.4 us
    ppermute x2, waiting for transfers between devices, exchange(): lax.ppermute(parts[0], 'rows', inner)  7.74 us
    ppermute x3, starting transfers between devices, local(): lax.ppermute(total, 'rows', [(i, i ^ stride) for i in range(size)])  7.63 us
    ppermute x2, starting transfers between devices, exchange(): lax.ppermute(parts[0], 'rows', inner)  7.36 us
    pallas_call x2, Pallas kernels, pack(): pl.pallas_call(functools.partial(pack_kernel, rows, inputs, left), out_sh...  3.57 us
    ppermute x3, waiting for transfers between devices, local(): lax.ppermute(total, 'rows', [(i, i ^ stride) for i in range(size)])  3.43 us
    pallas_call x1, Pallas kernels, local(): prepare(flag, field, streamwise, crossflow, diffusivity, obstacle, cell_w...  2.13 us
    pallas_call x1, Pallas kernels, local(): pl.pallas_call(functools.partial(finish_kernel, rows, inputs, shared), ou...  1.82 us
  transfers between devices with their start and end apart: 10, of which 6 were waited for; matrix products, arithmetic and copies ran while one was open for 0% of the time, Pallas kernels for 21%

profile of v6, /device:TPU:0, one launch (start us, length us, event | category | flops | bytes accessed | tf_op | source)
XLA Modules:
  0.0 52.4 jit_solution(2412421907634766932)
XLA Ops:
  0.6 0.0 copy-start.5
  0.7 1.9 %shard_map.77 = (bf16[136,1024]{1,0:T(8,128)(2,1)S(1)}, bf16[136,1024]{1,0:T(8,128)(2,1)S(1)}) custom-call(s32[1]{0:T(128)} %bitcast.1.odd_ref, f32[1792,128]{1,0:T(8,128)} %bitcast.16, f32[16,1792]{1,0:T(8,128)} %along_in.3, f32[16,1792]{1,0:T(8,128)} %across_in.3, f32[16,1792]{1,0:T(8,128)} %viscous_in.3, s32[16,1792]{1,0:T(8,128)} %solid_in.3), custom_call_target="tpu_custom_call" | custom-call | flops 100000000 | bytes 3670016 | tf_op jit(solution)/shard_map/pallas_call | solution.py:361
  2.5 0.0 copy-start
  2.5 3.0 %collective-permute-start = (bf16[136,1024]{1,0:T(8,128)(2,1)S(1)}, bf16[136,1024]{1,0:T(8,128)(2,1)S(1)}, u32[]{:S(2)}, u32[]{:S(2)}) collective-permute-start(bf16[136,1024]{1,0:T(8,128)(2,1)S(1)} %get-tuple-element.19), channel_id=1, source_target_pairs={{0,2},{2,0},{4,6},{6,4},{8,10},{10,8},{12,14},{14,12},{1,3},{3,1},... | collective-permute-start | bytes 835592 | tf_op jit(solution)/shard_map/ppermute | solution.py:384
  5.6 0.0 copy-start.1
  5.6 0.0 copy-start.2
  5.6 0.0 copy-start.3
  5.6 0.0 copy-start.4
  5.6 0.8 %collective-permute-start.1 = (bf16[136,1024]{1,0:T(8,128)(2,1)S(1)}, bf16[136,1024]{1,0:T(8,128)(2,1)S(1)}, u32[]{:S(2)}, u32[]{:S(2)}) collective-permute-start(bf16[136,1024]{1,0:T(8,128)(2,1)S(1)} %get-tuple-element.20), channel_id=1, source_target_pairs={{2,4},{4,2},{6,8},{8,6},{10,12},{12,10},{3,5},{5,3},{7,9},{9,7},{1... | collective-permute-start | bytes 835592 | tf_op jit(solution)/shard_map/ppermute | solution.py:384
  6.4 1.7 %shard_map.79 = (bf16[136,768]{1,0:T(8,128)(2,1)S(1)}, bf16[136,768]{1,0:T(8,128)(2,1)S(1)}) custom-call(s32[1]{0:T(128)} %bitcast.1.odd_ref, f32[1792,128]{1,0:T(8,128)} %bitcast.17, f32[16,1792]{1,0:T(8,128)} %along_in.3, f32[16,1792]{1,0:T(8,128)} %across_in.3, f32[16,1792]{1,0:T(8,128)} %viscous_in.3, s32[16,1792]{1,0:T(8,128)} %solid_in.3), custom_call_target="tpu_custom_call" | custom-call | flops 100000000 | bytes 3670016 | tf_op jit(solution)/shard_map/pallas_call | solution.py:361
  8.1 4.3 %collective-permute-start.2 = (bf16[136,768]{1,0:T(8,128)(2,1)S(1)}, bf16[136,768]{1,0:T(8,128)(2,1)S(1)}, u32[]{:S(2)}, u32[]{:S(2)}) collective-permute-start(bf16[136,768]{1,0:T(8,128)(2,1)S(1)} %get-tuple-element.23), channel_id=1, source_target_pairs={{0,2},{2,0},{4,6},{6,4},{8,10},{10,8},{12,14},{14,12},{1,3},{3,1},... | collective-permute-start | bytes 626696 | tf_op jit(solution)/shard_map/ppermute | solution.py:384
  12.4 0.7 %collective-permute-start.3 = (bf16[136,768]{1,0:T(8,128)(2,1)S(1)}, bf16[136,768]{1,0:T(8,128)(2,1)S(1)}, u32[]{:S(2)}, u32[]{:S(2)}) collective-permute-start(bf16[136,768]{1,0:T(8,128)(2,1)S(1)} %get-tuple-element.24), channel_id=1, source_target_pairs={{2,4},{4,2},{6,8},{8,6},{10,12},{12,10},{3,5},{5,3},{7,9},{9,7},{1... | collective-permute-start | bytes 626696 | tf_op jit(solution)/shard_map/ppermute | solution.py:384
  13.1 0.0 copy-done.5
  13.1 0.0 copy-done
  13.1 0.0 copy-done.1
  13.1 0.0 copy-done.2
  13.2 0.0 copy-done.3
  13.2 0.0 copy-done.4
  13.2 2.1 %prepare.1 = (f32[128,1792]{1,0:T(8,128)S(1)}, f32[5,224,128]{2,1,0:T(8,128)S(1)}, f32[224,128]{1,0:T(8,128)S(1)}) custom-call(s32[1]{0:T(128)} %bitcast.adjoint_ref, f32[1792,128]{1,0:T(8,128)S(1)} %bitcast.18, f32[16,1792]{1,0:T(8,128)S(1)} %copy-done.1, f32[16,1792]{1,0:T(8,128)S(1)} %copy-done.2, f32[16,1792]{1,0:T(8,128)S(1)} %copy-done.3, ...), custom_call_target="tpu_custom_call" | custom-call | flops 1000000000 | bytes 3670016 | tf_op jit(solution)/shard_map/prepare/pallas_call | solution.py:404
  15.3 7.7 %collective-permute-done.refs_0_ = bf16[136,1024]{1,0:T(8,128)(2,1)S(1)} collective-permute-done((bf16[136,1024]{1,0:T(8,128)(2,1)S(1)}, bf16[136,1024]{1,0:T(8,128)(2,1)S(1)}, u32[]{:S(2)}, u32[]{:S(2)}) %collective-permute-start) | collective-permute-done | bytes 278560 | tf_op jit(solution)/shard_map/ppermute | solution.py:384
  23.1 0.0 collective-permute-done.1.refs_1_
  23.1 5.6 %shard_map.78 = (f32[128,1024]{1,0:T(8,128)S(1)}, bf16[32,8192]{1,0:T(8,128)(2,1)S(1)}, bf16[32,8192]{1,0:T(8,128)(2,1)S(1)}, bf16[2,136,256]{2,1,0:T(8,128)(2,1)S(1)}) custom-call(s32[1]{0:T(128)} %bitcast.adjoint_ref, s32[1]{0:T(128)} %bitcast.1.odd_ref, f32[128,1792]{1,0:T(8,128)S(1)} %get-tuple-element.16.own, ...), custom_call_target="tpu_custom_call" | custom-call | flops 1000000000 | bytes 3670016 | tf_op jit(solution)/shard_map/pallas_call | solution.py:411
  28.7 0.0 collective-permute-done.2.refs_2_
  28.7 0.0 collective-permute-done.3.refs_3_
  28.7 5.8 %shard_map.80 = (f32[128,1024]{1,0:T(8,128)S(1)}, bf16[32,8192]{1,0:T(8,128)(2,1)S(1)}, bf16[32,8192]{1,0:T(8,128)(2,1)S(1)}) custom-call(s32[1]{0:T(128)} %bitcast.adjoint_ref, s32[1]{0:T(128)} %bitcast.1.odd_ref, f32[128,1792]{1,0:T(8,128)S(1)} %get-tuple-element.16.own, f32[5,224,128]{2,1,0:T(8,128)S(1)} %get-tuple-element.17.own_weights, ...), custom_call_target="tpu_custom_call" | custom-call | flops 1000000000 | bytes 3670016 | tf_op jit(solution)/shard_map/pallas_call | solution.py:411
  34.5 0.1 collective-permute-start.5
  34.6 0.5 collective-permute-start.4
  35.1 1.4 %collective-permute-done.5.other_b = bf16[32,8192]{1,0:T(8,128)(2,1)S(1)} collective-permute-done((bf16[32,8192]{1,0:T(8,128)(2,1)S(1)}, bf16[32,8192]{1,0:T(8,128)(2,1)S(1)}, u32[]{:S(2)}, u32[]{:S(2)}) %collective-permute-start.5) | collective-permute-done | bytes 524320 | tf_op jit(solution)/shard_map/ppermute | solution.py:444
  36.5 0.7 %collective-permute-done.4.other_a = bf16[32,8192]{1,0:T(8,128)(2,1)S(1)} collective-permute-done((bf16[32,8192]{1,0:T(8,128)(2,1)S(1)}, bf16[32,8192]{1,0:T(8,128)(2,1)S(1)}, u32[]{:S(2)}, u32[]{:S(2)}) %collective-permute-start.4) | collective-permute-done | bytes 524320 | tf_op jit(solution)/shard_map/ppermute | solution.py:443
  37.2 0.4 meet.1
  37.7 0.1 collective-permute-start.6
  37.8 1.1 %collective-permute-done.6 = f32[32,32]{1,0:T(8,128)S(1)} collective-permute-done((f32[32,32]{1,0:T(8,128)S(1)}, f32[32,32]{1,0:T(8,128)S(1)}, u32[]{:S(2)}, u32[]{:S(2)}) %collective-permute-start.6) | collective-permute-done | bytes 4128 | tf_op jit(solution)/shard_map/ppermute | solution.py:453
  38.9 2.5 %collective-permute-start.7 = (f32[32,32]{1,0:T(8,128)S(1)}, f32[32,32]{1,0:T(8,128)S(1)}, u32[]{:S(2)}, u32[]{:S(2)}) collective-permute-start(f32[32,32]{1,0:T(8,128)S(1)} %add.17), channel_id=1, source_target_pairs={{0,2},{2,0},{4,6},{6,4},{8,10},{10,8},{12,14},{14,12},{1,3},{3,1},... | collective-permute-start | bytes 12296 | tf_op jit(solution)/shard_map/ppermute | solution.py:457
  41.3 1.7 %collective-permute-done.7 = f32[32,32]{1,0:T(8,128)S(1)} collective-permute-done((f32[32,32]{1,0:T(8,128)S(1)}, f32[32,32]{1,0:T(8,128)S(1)}, u32[]{:S(2)}, u32[]{:S(2)}) %collective-permute-start.7) | collective-permute-done | bytes 4128 | tf_op jit(solution)/shard_map/ppermute | solution.py:457
  43.1 2.1 %collective-permute-start.8 = (f32[32,32]{1,0:T(8,128)S(1)}, f32[32,32]{1,0:T(8,128)S(1)}, u32[]{:S(2)}, u32[]{:S(2)}) collective-permute-start(f32[32,32]{1,0:T(8,128)S(1)} %add.18), channel_id=1, source_target_pairs={{0,4},{2,6},{4,0},{6,2},{8,12},{10,14},{12,8},{14,10},{1,5},{3,7},... | collective-permute-start | bytes 12296 | tf_op jit(solution)/shard_map/ppermute | solution.py:457
  45.2 1.7 %collective-permute-done.8 = f32[32,32]{1,0:T(8,128)S(1)} collective-permute-done((f32[32,32]{1,0:T(8,128)S(1)}, f32[32,32]{1,0:T(8,128)S(1)}, u32[]{:S(2)}, u32[]{:S(2)}) %collective-permute-start.8) | collective-permute-done | bytes 4128 | tf_op jit(solution)/shard_map/ppermute | solution.py:457
  46.9 3.0 %collective-permute-start.9 = (f32[32,32]{1,0:T(8,128)S(1)}, f32[32,32]{1,0:T(8,128)S(1)}, u32[]{:S(2)}, u32[]{:S(2)}) collective-permute-start(f32[32,32]{1,0:T(8,128)S(1)} %add.19), channel_id=1, source_target_pairs={{0,8},{2,10},{4,12},{6,14},{8,0},{10,2},{12,4},{14,6},{1,9},{3,11}... | collective-permute-start | bytes 12296 | tf_op jit(solution)/shard_map/ppermute | solution.py:457
  49.9 1.8 %finish.1 = f32[1792,128]{1,0:T(8,128)} custom-call(f32[128,1024]{1,0:T(8,128)S(1)} %get-tuple-element.21.left, f32[128,1024]{1,0:T(8,128)S(1)} %get-tuple-element.25.right), custom_call_target="tpu_custom_call" | custom-call | flops 10000000 | bytes 3670016 | tf_op jit(solution)/shard_map/finish/pallas_call | solution.py:462
  51.7 0.0 collective-permute-done.9
  51.8 0.6 %add_multiply_fusion = f32[32,32]{1,0:T(8,128)} fusion(f32[32,32]{1,0:T(8,128)S(1)} %add.19, f32[32,32]{1,0:T(8,128)S(1)} %collective-permute-done.9), kind=kLoop, calls=%fused_computation.2 | loop fusion | flops 2048 | bytes 12288 | tf_op jit(solution)/shard_map/mul | solution.py:461
  (4 shorter events, 0.0 us)
Async XLA Ops:
  0.6 12.5 %copy-start.5 = (f32[16,1792]{1,0:T(8,128)S(1)}, f32[16,1792]{1,0:T(8,128)}, u32[]{:S(2)}) copy-start(f32[16,1792]{1,0:T(8,128)} %area.1) | copy-start | bytes 344068
  2.5 10.6 %copy-start = (f32[1,8,16,1792]{3,2,1,0:T(8,128)S(1)}, f32[1,8,16,1792]{3,2,1,0:T(8,128)}, u32[]{:S(2)}) copy-start(f32[1,8,16,1792]{3,2,1,0:T(8,128)} %param.6) | copy-start | bytes 2752516
  2.5 20.5 %collective-permute-start = (bf16[136,1024]{1,0:T(8,128)(2,1)S(1)}, bf16[136,1024]{1,0:T(8,128)(2,1)S(1)}, u32[]{:S(2)}, u32[]{:S(2)}) collective-permute-start(bf16[136,1024]{1,0:T(8,128)(2,1)S(1)} %get-tuple-element.19), channel_id=1, source_target_pairs={{0,2},{2,0},{4,6},{6,4},{8,10},{10,8},{12,14},{14,12},{1,3},{3,1},... | collective-permute-start | bytes 835592 | tf_op jit(solution)/shard_map/ppermute | solution.py:384
  5.6 7.6 %copy-start.1 = (f32[16,1792]{1,0:T(8,128)S(1)}, f32[16,1792]{1,0:T(8,128)}, u32[]{:S(2)}) copy-start(f32[16,1792]{1,0:T(8,128)} %along_in.3) | copy-start | bytes 344068
  5.6 7.6 %copy-start.2 = (f32[16,1792]{1,0:T(8,128)S(1)}, f32[16,1792]{1,0:T(8,128)}, u32[]{:S(2)}) copy-start(f32[16,1792]{1,0:T(8,128)} %across_in.3) | copy-start | bytes 344068
  5.6 7.6 %copy-start.3 = (f32[16,1792]{1,0:T(8,128)S(1)}, f32[16,1792]{1,0:T(8,128)}, u32[]{:S(2)}) copy-start(f32[16,1792]{1,0:T(8,128)} %viscous_in.3) | copy-start | bytes 344068
  5.6 7.6 %copy-start.4 = (s32[16,1792]{1,0:T(8,128)S(1)}, s32[16,1792]{1,0:T(8,128)}, u32[]{:S(2)}) copy-start(s32[16,1792]{1,0:T(8,128)} %solid_in.3) | copy-start | bytes 344068
  5.6 17.5 %collective-permute-start.1 = (bf16[136,1024]{1,0:T(8,128)(2,1)S(1)}, bf16[136,1024]{1,0:T(8,128)(2,1)S(1)}, u32[]{:S(2)}, u32[]{:S(2)}) collective-permute-start(bf16[136,1024]{1,0:T(8,128)(2,1)S(1)} %get-tuple-element.20), channel_id=1, source_target_pairs={{2,4},{4,2},{6,8},{8,6},{10,12},{12,10},{3,5},{5,3},{7,9},{9,7},{1... | collective-permute-start | bytes 835592 | tf_op jit(solution)/shard_map/ppermute | solution.py:384
  8.1 20.6 %collective-permute-start.2 = (bf16[136,768]{1,0:T(8,128)(2,1)S(1)}, bf16[136,768]{1,0:T(8,128)(2,1)S(1)}, u32[]{:S(2)}, u32[]{:S(2)}) collective-permute-start(bf16[136,768]{1,0:T(8,128)(2,1)S(1)} %get-tuple-element.23), channel_id=1, source_target_pairs={{0,2},{2,0},{4,6},{6,4},{8,10},{10,8},{12,14},{14,12},{1,3},{3,1},... | collective-permute-start | bytes 626696 | tf_op jit(solution)/shard_map/ppermute | solution.py:384
  12.4 16.3 %collective-permute-start.3 = (bf16[136,768]{1,0:T(8,128)(2,1)S(1)}, bf16[136,768]{1,0:T(8,128)(2,1)S(1)}, u32[]{:S(2)}, u32[]{:S(2)}) collective-permute-start(bf16[136,768]{1,0:T(8,128)(2,1)S(1)} %get-tuple-element.24), channel_id=1, source_target_pairs={{2,4},{4,2},{6,8},{8,6},{10,12},{12,10},{3,5},{5,3},{7,9},{9,7},{1... | collective-permute-start | bytes 626696 | tf_op jit(solution)/shard_map/ppermute | solution.py:384
  34.5 2.0 %collective-permute-start.5 = (bf16[32,8192]{1,0:T(8,128)(2,1)S(1)}, bf16[32,8192]{1,0:T(8,128)(2,1)S(1)}, u32[]{:S(2)}, u32[]{:S(2)}) collective-permute-start(bf16[32,8192]{1,0:T(8,128)(2,1)S(1)} %get-tuple-element.29), channel_id=1, source_target_pairs={{0,1},{1,0},{2,3},{3,2},{4,5},{5,4},{6,7},{7,6},{8,9},{9,8},{10,11... | collective-permute-start | bytes 1572872 | tf_op jit(solution)/shard_map/ppermute | solution.py:444
  34.6 2.6 %collective-permute-start.4 = (bf16[32,8192]{1,0:T(8,128)(2,1)S(1)}, bf16[32,8192]{1,0:T(8,128)(2,1)S(1)}, u32[]{:S(2)}, u32[]{:S(2)}) collective-permute-start(bf16[32,8192]{1,0:T(8,128)(2,1)S(1)} %get-tuple-element.27), channel_id=1, source_target_pairs={{0,1},{1,0},{2,3},{3,2},{4,5},{5,4},{6,7},{7,6},{8,9},{9,8},{10,11... | collective-permute-start | bytes 1572872 | tf_op jit(solution)/shard_map/ppermute | solution.py:443
  37.7 1.2 %collective-permute-start.6 = (f32[32,32]{1,0:T(8,128)S(1)}, f32[32,32]{1,0:T(8,128)S(1)}, u32[]{:S(2)}, u32[]{:S(2)}) collective-permute-start(f32[32,32]{1,0:T(8,128)S(1)} %meet.1), channel_id=1, source_target_pairs={{0,1},{1,0},{2,3},{3,2},{4,5},{5,4},{6,7},{7,6},{8,9},{9,8},{10,11... | collective-permute-start | bytes 12296 | tf_op jit(solution)/shard_map/ppermute | solution.py:453
  38.9 4.2 %collective-permute-start.7 = (f32[32,32]{1,0:T(8,128)S(1)}, f32[32,32]{1,0:T(8,128)S(1)}, u32[]{:S(2)}, u32[]{:S(2)}) collective-permute-start(f32[32,32]{1,0:T(8,128)S(1)} %add.17), channel_id=1, source_target_pairs={{0,2},{2,0},{4,6},{6,4},{8,10},{10,8},{12,14},{14,12},{1,3},{3,1},... | collective-permute-start | bytes 12296 | tf_op jit(solution)/shard_map/ppermute | solution.py:457
  43.1 3.8 %collective-permute-start.8 = (f32[32,32]{1,0:T(8,128)S(1)}, f32[32,32]{1,0:T(8,128)S(1)}, u32[]{:S(2)}, u32[]{:S(2)}) collective-permute-start(f32[32,32]{1,0:T(8,128)S(1)} %add.18), channel_id=1, source_target_pairs={{0,4},{2,6},{4,0},{6,2},{8,12},{10,14},{12,8},{14,10},{1,5},{3,7},... | collective-permute-start | bytes 12296 | tf_op jit(solution)/shard_map/ppermute | solution.py:457
  46.9 4.9 %collective-permute-start.9 = (f32[32,32]{1,0:T(8,128)S(1)}, f32[32,32]{1,0:T(8,128)S(1)}, u32[]{:S(2)}, u32[]{:S(2)}) collective-permute-start(f32[32,32]{1,0:T(8,128)S(1)} %add.19), channel_id=1, source_target_pairs={{0,8},{2,10},{4,12},{6,14},{8,0},{10,2},{12,4},{14,6},{1,9},{3,11}... | collective-permute-start | bytes 12296 | tf_op jit(solution)/shard_map/ppermute | solution.py:457
